TPU v7x, 32 devices: a whole 2x2x4 slice. The times are simulated.
32 devices in a mesh: tm: 8 (over z, core), sec: 4 (over y, x).
Axes of the slice: x: 2, y: 2, z: 4, core: 2. Of those that a mesh axis runs over, the one named last changes fastest.
Arguments:
- green_occ: float32 [8, 4, 512, 512], P('tm', 'sec'), may hold values from -6 to 6
- virtual_green_time: float32 [8, 4, 512, 512], P('tm', 'sec'), may hold values from -6 to 6
- fit_rows: int32 [4, 12], P('sec'), may hold values from 0 to 5, as said below
- fit_cols: int32 [4, 12], P('sec'), may hold values from 0 to 3
- fit_count: int32 [4], P('sec'), may hold values from 6 to 12, as said below
- fit_blocks: float32 [4, 12, 128, 128], P('sec'), may hold values from -0.25 to 0.25
- border_map: int32 [4, 2], P('sec'), may hold values from 0 to 3
- coulomb_metric_root: float32 [4, 512, 512], P('sec'), may hold values from -0.25 to 0.25
- pair_list: int32 [4, 3, 2], P('sec'), may hold values from 0 to 3
- times: float32 [8], replicated, may hold values from 0.05 to 8
- time_weights: float32 [8], replicated, may hold values from 0.2 to 1
- freqs: float32 [8], replicated, may hold values from 0.05 to 8
Outputs:
- screened: float32 [8, 4, 3, 128, 128], P('tm', 'sec')
Inputs may be any that keep to these rules, and one draw needn't show every extreme that they name: `fit_count`: some section lists exactly 12 fit blocks; entries at or past a section's count are unused. Within a section, the listed (fit_rows, fit_cols) positions are all different.
All inputs are finite; a program needn't handle non-finite values.
Results may differ from a plain program's by a relative error of at most 0.0003.
Values sent between devices are 32-bit elements; how exact they have to be, the bound alone decides.
No kernel may reach another device: no remote copies, remote signals or barrier semaphores. Data moves between devices by JAX's collectives and lax.ppermute only.
A program may use at most 128 MiB of HBM per device.

v0:
```python
import jax
import jax.numpy as jnp
from jax import lax
from jax.sharding import PartitionSpec as P

OWN_BLK = 4
BORDER_BLK = 2


LARGEST_FIT = lax.Precision.HIGHEST


def shifted(shard, axis, by):
    devices = lax.axis_size(axis)
    return lax.ppermute(shard, axis, [(i, (i + by) % devices) for i in range(devices)])


def on_device(
    green_occ,
    virtual_green_time,
    fit_rows,
    fit_cols,
    fit_count,
    fit_blocks,
    border_map,
    coulomb_metric_root,
    pair_list,
    times,
    time_weights,
    freqs,
):
    fit_values = fit_blocks[0]
    row_ids = fit_rows[0]
    col_ids = fit_cols[0]
    live_count = fit_count[0]
    block_order = fit_values.shape[-1]
    ext_rows = (OWN_BLK + BORDER_BLK) * block_order
    own_rows = OWN_BLK * block_order

    def one_time(paired):
        product = paired[0] * paired[1]

        def add_left(index, total):
            start_row = row_ids[index] * block_order
            source = lax.dynamic_slice_in_dim(product, col_ids[index] * block_order, block_order, 0)
            update = jnp.dot(fit_values[index], source, precision=LARGEST_FIT)
            current = lax.dynamic_slice_in_dim(total, start_row, block_order, 0)
            return lax.dynamic_update_slice_in_dim(total, current + update, start_row, 0)

        left_factor = lax.fori_loop(
            0, live_count, add_left, jnp.zeros((ext_rows, product.shape[1]), jnp.float32)
        )

        def add_right(index, total):
            start_col = row_ids[index] * block_order
            source = lax.dynamic_slice_in_dim(
                left_factor, col_ids[index] * block_order, block_order, 1
            )
            update = jnp.dot(source, fit_values[index].T, precision=LARGEST_FIT)
            current = lax.dynamic_slice_in_dim(total, start_col, block_order, 1)
            return lax.dynamic_update_slice_in_dim(total, current + update, start_col, 1)

        return lax.fori_loop(0, live_count, add_right, jnp.zeros((ext_rows, ext_rows), jnp.float32))

    extended = lax.map(one_time, (green_occ[:, 0], virtual_green_time[:, 0]))
    time_slots = extended.shape[0]
    own_part = extended[:, :own_rows, :own_rows]
    border = extended[:, own_rows:, own_rows:]
    incoming = shifted(border, "sec", 1)
    spread = (border_map[0][:, None] == jnp.arange(OWN_BLK)[None, :]).astype(jnp.float32)
    incoming = incoming.reshape(time_slots, BORDER_BLK, block_order, BORDER_BLK, block_order)
    border_block_sum = jnp.einsum(
        "ja,tjmkn,kb->tambn", spread, incoming, spread, precision=LARGEST_FIT
    )
    polarization = own_part + border_block_sum.reshape(own_part.shape)
    cosine = time_weights[None, :] * jnp.cos(freqs[:, None] * times[None, :])
    spectral_rows = jnp.einsum(
        "wt,trn->wrn",
        cosine,
        lax.all_to_all(polarization, "tm", split_axis=1, concat_axis=0, tiled=True),
        precision=LARGEST_FIT,
    )
    spectral_polar = lax.all_to_all(spectral_rows, "tm", split_axis=0, concat_axis=1, tiled=True)
    metric = coulomb_metric_root[0]
    left_factor = jnp.einsum("im,fmn->fin", metric, spectral_polar, precision=LARGEST_FIT)
    projected_fit = jnp.einsum("fin,jn->fij", left_factor, metric, precision=LARGEST_FIT)
    projected_fit = projected_fit.reshape(
        projected_fit.shape[0], OWN_BLK, block_order, OWN_BLK, block_order
    )
    pick_rows = (pair_list[0][:, 0][:, None] == jnp.arange(OWN_BLK)[None, :]).astype(jnp.float32)
    pick_cols = (pair_list[0][:, 1][:, None] == jnp.arange(OWN_BLK)[None, :]).astype(jnp.float32)
    screened = jnp.einsum(
        "pa,wambn,pb->wpmn", pick_rows, projected_fit, pick_cols, precision=LARGEST_FIT
    )
    return screened[:, None]


def solution(mesh):
    return jax.shard_map(
        on_device,
        mesh=mesh,
        in_specs=(
            P("tm", "sec", None, None),
            P("tm", "sec", None, None),
            P("sec", None),
            P("sec", None),
            P("sec"),
            P("sec", None, None, None),
            P("sec", None),
            P("sec", None, None),
            P("sec", None, None),
            P(),
            P(),
            P(),
        ),
        out_specs=P("tm", "sec", None, None, None),
        check_vma=False,
    )
```

profile of v0, /device:TPU:0, one launch (start us, length us, event | category | flops | bytes accessed | tf_op | source)
XLA Modules:
  0.0 204.1 jit_solution(11755167323099933766)
XLA Ops:
  0.0 2.8 %multiply_bitcast_fusion = f32[512,512]{1,0:T(8,128)} fusion(f32[1,1,512,512]{3,2,1,0:T(8,128)} %param.16, f32[1,1,512,512]{3,2,1,0:T(8,128)} %param.17), kind=kLoop, calls=%fused_computation.20 | loop fusion | flops 262144 | bytes 3145728 | tf_op jit(solution)/shard_map/while/body/eval_jaxpr/mul | solution.py:41
  3.0 58.0 %while.30 = (s32[]{:T(128)}, f32[768,512]{1,0:T(8,128)S(1)}, s32[]{:T(128)}, s32[12]{0:T(128)S(1)}, f32[12,128,128]{2,1,0:T(8,128)}, /*index=5*/s32[12]{0:T(128)...) while((s32[]{:T(128)}, f32[768,512]{1,0:T(8,128)S(1)}, ...), condition=%wide.region_1.0_spmd, body=%wide.region_0.1_spmd.sunk | while | flops 100728848 | bytes 852255 | solution.py:50
  62.4 54.7 %while.31 = (s32[]{:T(128)}, f32[768,768]{1,0:T(8,128)S(1)}, s32[]{:T(128)}, s32[12]{0:T(128)S(1)}, s32[12]{0:T(128)S(1)}, /*index=5*/f32[768,512]{1,0:T(8,128)}...) while((s32[]{:T(128)}, f32[768,768]{1,0:T(8,128)S(1)}, ...), condition=%wide.region_3.0_spmd, body=%wide.region_2.0_spmd.sunk | while | flops 151093264 | bytes 1245471 | solution.py:63
  65.4 1.5 fusion.50
  69.9 1.5 fusion.50
  74.4 1.5 fusion.50
  83.4 1.5 fusion.50
  87.9 1.5 fusion.50
  92.4 1.5 fusion.50
  96.9 1.5 fusion.50
  101.4 1.5 fusion.50
  105.9 1.5 fusion.50
  110.4 1.5 fusion.50
  117.0 1.6 broadcast_in_dim.5
  118.9 3.0 %collective-permute-start = (f32[1,256,256]{2,0,1:T(1,128)S(1)}, f32[1,256,256]{2,0,1:T(1,128)S(1)}, u32[]{:S(2)}, u32[]{:S(2)}) collective-permute-start(f32[1,256,256]{2,0,1:T(1,128)S(1)} %slice.17), channel_id=1, source_target_pairs={{0,1},{1,2},{2,3},{3,0},{4,5},{5,6},{6,7},{7,4},{8,9},{9,10},{10,1... | collective-permute-start | bytes 786440 | tf_op jit(solution)/shard_map/ppermute | solution.py:15
  121.9 6.6 %collective-permute-done = f32[1,256,256]{2,0,1:T(1,128)S(1)} collective-permute-done((f32[1,256,256]{2,0,1:T(1,128)S(1)}, f32[1,256,256]{2,0,1:T(1,128)S(1)}, u32[]{:S(2)}, u32[]{:S(2)}) %collective-permute-start) | collective-permute-done | bytes 262176 | tf_op jit(solution)/shard_map/ppermute | solution.py:15
  131.9 32.2 %all_to_all.21 = f32[1,512,512]{2,0,1:T(1,128)S(1)} all-to-all(f32[1,512,512]{2,0,1:T(1,128)S(1)} %slice_add_fusion), channel_id=1, replica_groups=mesh['tm'=8,'sec'=4] {'tm'}, dimensions={1} | all-to-all | bytes 2097152 | tf_op jit(solution)/shard_map/all_to_all | solution.py:80
  164.2 1.6 fusion.13
  165.8 1.6 copy.28
  167.4 3.7 %all-to-all-start.1 = ((f32[8,64,512]{2,1,0:T(8,128)}), f32[8,64,512]{2,1,0:T(8,128)S(1)}, u32[]{:S(2)}, u32[]{:S(2)}) async-start(f32[8,64,512]{2,1,0:T(8,128)} %copy.28), calls=%async_computation.1 | async-start | bytes 2097152 | tf_op jit(solution)/shard_map/all_to_all | solution.py:83
  171.2 26.2 %all-to-all-done.1 = f32[8,64,512]{2,1,0:T(8,128)S(1)} async-done(((f32[8,64,512]{2,1,0:T(8,128)}), f32[8,64,512]{2,1,0:T(8,128)S(1)}, u32[]{:S(2)}, u32[]{:S(2)}) %all-to-all-start.1) | async-done | bytes 1048608 | tf_op jit(solution)/shard_map/all_to_all | solution.py:83
  197.4 1.9 fusion.10
  199.3 1.9 fusion.35
  201.2 2.2 %convolution_bitcast_fusion.1 = f32[1,1,3,128,128]{4,2,3,1,0:T(4,128)S(1)} fusion(f32[4,128,4,128]{3,1,2,0:T(8,128)S(1)} %fusion.35, f32[3,4]{0,1:T(4,128)S(1)} %fusion.30, f32[3,4]{1,0:T(4,128)S(1)} %fusion.29), kind=kOutput, calls=%fused_computation.13 | convolution fusion | flops 9437232 | bytes 1245280 | tf_op jit(solution)/shard_map/pa,wambn,pb->wpmn/dot_general | solution.py:92
  (92 shorter events, 55.5 us)
Async XLA Ops:
  0.0 197.4 %copy-start = (f32[1,512,512]{2,1,0:T(8,128)S(1)}, f32[1,512,512]{2,1,0:T(8,128)}, u32[]{:S(2)}) copy-start(f32[1,512,512]{2,1,0:T(8,128)} %param.23) | copy-start | bytes 3145732
  0.0 3.0 %copy-start.7 = (s32[1,12]{1,0:T(1,128)S(1)}, s32[1,12]{1,0:T(1,128)}, u32[]{:S(2)}) copy-start(s32[1,12]{1,0:T(1,128)} %param.18) | copy-start | bytes 148
  0.0 3.0 %copy-start.8 = (s32[1,12]{1,0:T(1,128)S(1)}, s32[1,12]{1,0:T(1,128)}, u32[]{:S(2)}) copy-start(s32[1,12]{1,0:T(1,128)} %param.19) | copy-start | bytes 148
  61.0 1.2 copy-start.1
  117.0 11.5 %copy-start.2 = (s32[1,2]{1,0:T(1,128)S(1)}, s32[1,2]{1,0:T(1,128)}, u32[]{:S(2)}) copy-start(s32[1,2]{1,0:T(1,128)} %param.22) | copy-start | bytes 28
  118.9 9.7 %collective-permute-start = (f32[1,256,256]{2,0,1:T(1,128)S(1)}, f32[1,256,256]{2,0,1:T(1,128)S(1)}, u32[]{:S(2)}, u32[]{:S(2)}) collective-permute-start(f32[1,256,256]{2,0,1:T(1,128)S(1)} %slice.17), channel_id=1, source_target_pairs={{0,1},{1,2},{2,3},{3,0},{4,5},{5,6},{6,7},{7,4},{8,9},{9,10},{10,1... | collective-permute-start | bytes 786440 | tf_op jit(solution)/shard_map/ppermute | solution.py:15
  131.9 32.3 %copy-start.4 = (f32[8]{0:T(128)S(1)}, f32[8]{0:T(128)}, u32[]{:S(2)}) copy-start(f32[8]{0:T(128)} %param.25) | copy-start | bytes 100
  131.9 32.3 %copy-start.5 = (f32[8]{0:T(128)S(1)}, f32[8]{0:T(128)}, u32[]{:S(2)}) copy-start(f32[8]{0:T(128)} %param.27) | copy-start | bytes 100
  131.9 32.3 %copy-start.6 = (f32[8]{0:T(128)S(1)}, f32[8]{0:T(128)}, u32[]{:S(2)}) copy-start(f32[8]{0:T(128)} %param.26) | copy-start | bytes 100
  165.8 5.4 %copy-start.3 = (s32[1,3,2]{1,2,0:T(2,128)S(1)}, s32[1,3,2]{1,2,0:T(2,128)}, u32[]{:S(2)}) copy-start(s32[1,3,2]{1,2,0:T(2,128)} %param.24) | copy-start | bytes 76
  167.4 30.1 %all-to-all-start.1 = ((f32[8,64,512]{2,1,0:T(8,128)}), f32[8,64,512]{2,1,0:T(8,128)S(1)}, u32[]{:S(2)}, u32[]{:S(2)}) async-start(f32[8,64,512]{2,1,0:T(8,128)} %copy.28), calls=%async_computation.1 | async-start | bytes 2097152 | tf_op jit(solution)/shard_map/all_to_all | solution.py:83
where the time goes:
time: 205 us; the launch traced here: 204 us
  loops' own time  48.2 us (24%)
  matrix products  43.7 us (21%)
  local copies, waits for them, and re-layouts  36.1 us (18%)
  waiting for transfers between devices  32.8 us (16%)
  blocking collectives  32.2 us (16%)
  starting transfers between devices  6.77 us (3%)
  other arithmetic  4.04 us (2%)
    all_to_all x1, blocking collectives, on_device(): lax.all_to_all(polarization, 'tm', split_axis=1, concat_axis=0, tiled=True)  32.2 us
    all_to_all x1, waiting for transfers between devices, on_device(): lax.all_to_all(spectral_rows, 'tm', split_axis=0, concat_axis=1, tiled=True)  26.2 us
    another operation x1, loops' own time, one_time(): lax.fori_loop(0, live_count, add_left, jnp.zeros((ext_rows, product.shape...  25.6 us
    another operation x1, loops' own time, one_time(): lax.fori_loop(0, live_count, add_right, jnp.zeros((ext_rows, ext_rows), j...  22.7 us
    dot_general x12, matrix products, add_right(): update = jnp.dot(source, fit_values[index].T, precision=LARGEST_FIT)  17.8 us
    dot_general x12, matrix products, add_left(): update = jnp.dot(fit_values[index], source, precision=LARGEST_FIT)  16.4 us
    dynamic_slice x12, local copies, waits for them, and re-layouts, add_left(): start_row = row_ids[index] * block_order  8.05 us
    dynamic_slice x12, local copies, waits for them, and re-layouts, add_left(): col_ids[index] * block_order  8.03 us
  transfers between devices with their start and end apart: 2, of which 2 were waited for; matrix products, arithmetic and copies ran while one was open for 0% of the time, Pallas kernels for 0%

commit v1 on v0

v1 whole, which is shorter than its diff:
```python
import functools

import jax
import jax.numpy as jnp
from jax import lax
from jax.experimental import pallas as pl
from jax.experimental.pallas import tpu as pltpu
from jax.sharding import PartitionSpec as P

OWN_BLK = 4
BORDER_BLK = 2
CORES = 2

VMEM = pl.BlockSpec(memory_space=pltpu.VMEM)
SMEM = pl.BlockSpec(memory_space=pltpu.SMEM)
NN = (((1,), (0,)), ((), ()))
NT = (((1,), (1,)), ((), ()))


def split(x):
    high = x.astype(jnp.bfloat16)
    return high, (x - high.astype(jnp.float32)).astype(jnp.bfloat16)


def dot3(a, b, dims):
    mm = functools.partial(
        lax.dot_general, dimension_numbers=dims, preferred_element_type=jnp.float32
    )
    return mm(a[0], b[0]) + (mm(a[0], b[1]) + mm(a[1], b[0]))


def place_fit(rows, cols, count, blocks, high_ref, low_ref, first, last):
    order = blocks.shape[-1]
    high_ref[...] = jnp.zeros(high_ref.shape, high_ref.dtype)
    low_ref[...] = jnp.zeros(low_ref.shape, low_ref.dtype)
    for f in range(blocks.shape[0]):
        row = rows[0, f]

        @pl.when((f < count[0]) & (row >= first) & (row < last))
        def _():
            high, low = split(blocks[f])
            at_row = pl.ds(pl.multiple_of((row - first) * order, order), order)
            at_col = pl.ds(pl.multiple_of(cols[0, f] * order, order), order)
            high_ref[at_row, at_col] = high
            low_ref[at_row, at_col] = low


def border_kernel(rows, cols, count, occ, virt, blocks, out, fit_high, fit_low):
    place_fit(rows, cols, count, blocks, fit_high, fit_low, OWN_BLK, OWN_BLK + BORDER_BLK)
    product = split(occ[...] * virt[...])
    fit = (fit_high[...], fit_low[...])
    left = split(dot3(fit, product, NN))
    out[...] = dot3(left, fit, NT)


def own_kernel(
    rows, cols, count, border_map, pairs, occ, virt, blocks, metric,
    out, edge_high, edge_low,
    fit_high, fit_low, proj_high, proj_low, pick_high, pick_low,
):
    order = blocks.shape[-1]
    place_fit(rows, cols, count, blocks, fit_high, fit_low, 0, OWN_BLK)
    metric_parts = split(metric[...])
    for j in range(BORDER_BLK):
        at = pl.ds(pl.multiple_of(border_map[0, j] * order, order), order)
        high, low = split(metric[:, at])
        edge_high[:, j * order : (j + 1) * order] = high
        edge_low[:, j * order : (j + 1) * order] = low
    high, low = split(dot3(metric_parts, (fit_high[...], fit_low[...]), NN))
    proj_high[...] = high
    proj_low[...] = low
    count_pairs = out.shape[0]
    for p in range(count_pairs):
        at = pl.ds(pl.multiple_of(pairs[0, p, 0] * order, order), order)
        pick_high[p * order : (p + 1) * order, :] = proj_high[at, :]
        pick_low[p * order : (p + 1) * order, :] = proj_low[at, :]
    product = split(occ[...] * virt[...])
    left = dot3((pick_high[...], pick_low[...]), product, NN)
    for p in range(count_pairs):
        at = pl.ds(pl.multiple_of(pairs[0, p, 1] * order, order), order)
        out[p] = dot3(
            split(left[p * order : (p + 1) * order, :]), (proj_high[at, :], proj_low[at, :]), NT
        )


def join_kernel(pairs, place, border, own, edge_high, edge_low, *refs):
    pick_high, pick_low, total = refs[-3:]
    outs = refs[:-3]
    count_pairs, order, _ = own.shape
    for p in range(count_pairs):
        at = pl.ds(pl.multiple_of(pairs[0, p, 0] * order, order), order)
        pick_high[p * order : (p + 1) * order, :] = edge_high[at, :]
        pick_low[p * order : (p + 1) * order, :] = edge_low[at, :]
    left = dot3((pick_high[...], pick_low[...]), split(border[...]), NN)
    for p in range(count_pairs):
        at = pl.ds(pl.multiple_of(pairs[0, p, 1] * order, order), order)
        total[p] = own[p] + dot3(
            split(left[p * order : (p + 1) * order, :]), (edge_high[at, :], edge_low[at, :]), NT
        )
    share = outs[0].shape[1]
    for k, out in enumerate(outs):
        at = pl.ds(pl.multiple_of((place[0] ^ k) * share, share), share)
        out[...] = total[:, at, :]


def combine_kernel(place, cosine, *refs):
    chips = len(refs) // 3
    mine, other, outs = refs[:chips], refs[chips : 2 * chips], refs[2 * chips :]
    chip, core = place[0], place[1]
    times = CORES * chips
    shape = outs[0].shape
    for k in range(chips):
        freq = ((chip ^ k) * CORES + core) * times
        total = jnp.zeros(shape, jnp.float32)
        for j in range(chips):
            at = freq + (chip ^ j) * CORES
            total += cosine[at + core] * mine[j][...] + cosine[at + 1 - core] * other[j][...]
        outs[k][...] = total


def gather_kernel(place, *refs):
    out = refs[-1]
    for k, part in enumerate(refs[:-1]):
        share = part.shape[1]
        at = pl.ds(pl.multiple_of((place[0] ^ k) * share, share), share)
        out[0, 0, :, at, :] = part[...]


def on_device(
    green_occ,
    virtual_green_time,
    fit_rows,
    fit_cols,
    fit_count,
    fit_blocks,
    border_map,
    coulomb_metric_root,
    pair_list,
    times,
    time_weights,
    freqs,
):
    points = green_occ.shape[-1]
    order = fit_blocks.shape[-1]
    own_rows = OWN_BLK * order
    edge_rows = BORDER_BLK * order
    pairs = pair_list.shape[1]
    devices = lax.axis_size("tm")
    chips = devices // CORES
    share = order // chips
    f32, bf16 = jnp.float32, jnp.bfloat16
    occ, virt = green_occ[0, 0], virtual_green_time[0, 0]
    blocks, metric = fit_blocks[0], coulomb_metric_root[0]
    index = lax.axis_index("tm")
    place = jnp.stack([index // CORES, index % CORES]).astype(jnp.int32)
    cosine = (time_weights[None, :] * jnp.cos(freqs[:, None] * times[None, :])).reshape(-1)

    border = pl.pallas_call(
        border_kernel,
        out_shape=jax.ShapeDtypeStruct((edge_rows, edge_rows), f32),
        in_specs=[SMEM] * 3 + [VMEM] * 3,
        out_specs=VMEM,
        scratch_shapes=[pltpu.VMEM((edge_rows, points), bf16)] * 2,
        cost_estimate=pl.CostEstimate(flops=10**9, bytes_accessed=3 << 20, transcendentals=0),
        name="border",
    )(fit_rows, fit_cols, fit_count, occ, virt, blocks)
    sections = lax.axis_size("sec")
    border = lax.ppermute(border, "sec", [(i, (i + 1) % sections) for i in range(sections)])

    own, edge_high, edge_low = pl.pallas_call(
        own_kernel,
        out_shape=(
            jax.ShapeDtypeStruct((pairs, order, order), f32),
            jax.ShapeDtypeStruct((own_rows, edge_rows), bf16),
            jax.ShapeDtypeStruct((own_rows, edge_rows), bf16),
        ),
        in_specs=[SMEM] * 5 + [VMEM] * 4,
        out_specs=(VMEM,) * 3,
        scratch_shapes=[pltpu.VMEM((own_rows, points), bf16)] * 4
        + [pltpu.VMEM((pairs * order, points), bf16)] * 2,
        cost_estimate=pl.CostEstimate(flops=2 * 10**9, bytes_accessed=5 << 20, transcendentals=0),
        name="own",
    )(fit_rows, fit_cols, fit_count, border_map, pair_list, occ, virt, blocks, metric)

    part = jax.ShapeDtypeStruct((pairs, share, order), f32)
    parts = pl.pallas_call(
        join_kernel,
        out_shape=(part,) * chips,
        in_specs=[SMEM] * 2 + [VMEM] * 4,
        out_specs=(VMEM,) * chips,
        scratch_shapes=[pltpu.VMEM((pairs * order, edge_rows), bf16)] * 2
        + [pltpu.VMEM((pairs, order, order), f32)],
        name="join",
    )(pair_list, place, border, own, edge_high, edge_low)

    def across(x, k):
        return lax.ppermute(x, "tm", [(i, i ^ (CORES * k)) for i in range(devices)])

    def swap(x):
        return lax.ppermute(x, "tm", [(i, i ^ 1) for i in range(devices)])

    mine = [parts[0]] + [across(parts[k], k) for k in range(1, chips)]
    other = [swap(x) for x in mine]
    parts = pl.pallas_call(
        combine_kernel,
        out_shape=(part,) * chips,
        in_specs=[SMEM] * 2 + [VMEM] * (2 * chips),
        out_specs=(VMEM,) * chips,
        name="combine",
    )(place, cosine, *mine, *other)
    parts = [parts[0]] + [across(parts[k], k) for k in range(1, chips)]
    return pl.pallas_call(
        gather_kernel,
        out_shape=jax.ShapeDtypeStruct((1, 1, pairs, order, order), f32),
        in_specs=[SMEM] + [VMEM] * chips,
        out_specs=VMEM,
        name="gather",
    )(place, *parts)


def solution(mesh):
    return jax.shard_map(
        on_device,
        mesh=mesh,
        in_specs=(
            P("tm", "sec", None, None),
            P("tm", "sec", None, None),
            P("sec", None),
            P("sec", None),
            P("sec"),
            P("sec", None, None, None),
            P("sec", None),
            P("sec", None, None),
            P("sec", None, None),
            P(),
            P(),
            P(),
        ),
        out_specs=P("tm", "sec", None, None, None),
        check_vma=False,
    )
```

time: 205 us -> 43 us (0.21)
  loops' own time: 48.2 us -> 0 us
  matrix products: 43.7 us -> 0 us
  blocking collectives: 32.2 us -> 0 us
  local copies, waits for them, and re-layouts: 36.1 us -> 4.15 us
  waiting for transfers between devices: 32.8 us -> 9.4 us
  Pallas kernels: 0 us -> 15.4 us
  starting transfers between devices: 6.77 us -> 12.3 us
  other arithmetic: 4.04 us -> 0.71 us
    another operation x2 -> x0, loops' own time: 48.2 us -> none  [the longest x1 25.6 us: one_time(): lax.fori_loop(0, live_count, add_left, jnp.zeros((ext_rows, product.shape...]
    dot_general x30 -> x0, matrix products: 43.7 us -> none  [the longest x12 17.8 us: add_right(): update = jnp.dot(source, fit_values[index].T, precision=LARGEST_FIT)]
    all_to_all x1 -> x0, blocking collectives: 32.2 us -> none  [on_device(): lax.all_to_all(polarization, 'tm', split_axis=1, concat_axis=0, tiled=True)]
    dynamic_slice x48 -> x0, local copies, waits for them, and re-layouts: 30.3 us -> none  [the longest x12 8.05 us: add_left(): start_row = row_ids[index] * block_order]
    all_to_all x1 -> x0, waiting for transfers between devices: 26.2 us -> none  [on_device(): lax.all_to_all(spectral_rows, 'tm', split_axis=0, concat_axis=1, tiled=True)]
    pallas_call x0 -> x5, Pallas kernels: none -> 15.4 us  [the longest x1 5.56 us: on_device(): pl.pallas_call(own_kernel, out_shape=(jax.ShapeDtypeStruct((pairs, order,...]
    ppermute x1 -> x11, starting transfers between devices: 3.03 us -> 12.3 us  [the longest x6 8.77 us: across(): return lax.ppermute(x, 'tm', [(i, i ^ CORES * k) for i in range(devices)])]
    all_to_all x1 -> x0, starting transfers between devices: 3.74 us -> none  [on_device(): lax.all_to_all(spectral_rows, 'tm', split_axis=0, concat_axis=1, tiled=True)]
  transfers between devices with their start and end apart: 2 -> 11, of which waited for: 2 -> 4; matrix products, arithmetic and copies ran while one was open for 0% -> 5% of each run, Pallas kernels for 0% -> 13%
where the time goes in v1:
time: 43 us; the launch traced here: 42.7 us
  Pallas kernels  15.4 us (36%)
  starting transfers between devices  12.3 us (29%)
  waiting for transfers between devices  9.4 us (22%)
  local copies, waits for them, and re-layouts  4.15 us (10%)
  between operations  0.74 us (2%)
  other arithmetic  0.71 us (2%)
    ppermute x6, waiting for transfers between devices, across(): return lax.ppermute(x, 'tm', [(i, i ^ CORES * k) for i in range(devices)])  8.98 us
    ppermute x6, starting transfers between devices, across(): return lax.ppermute(x, 'tm', [(i, i ^ CORES * k) for i in range(devices)])  8.77 us
    pallas_call x1, Pallas kernels, on_device(): pl.pallas_call(own_kernel, out_shape=(jax.ShapeDtypeStruct((pairs, order,...  5.56 us
    pallas_call x1, Pallas kernels, on_device(): pl.pallas_call(border_kernel, out_shape=jax.ShapeDtypeStruct((edge_rows,...  3.83 us
    unnamed x31, local copies, waits for them, and re-layouts  3.52 us
    ppermute x1, starting transfers between devices, on_device(): lax.ppermute(border, 'sec', [(i, (i + 1) % sections) for i in range(secti...  3.02 us
    pallas_call x1, Pallas kernels, on_device(): pl.pallas_call(join_kernel, out_shape=(part,) * chips, in_specs=[SMEM] *...  2.68 us
    pallas_call x1, Pallas kernels, on_device(): pl.pallas_call(combine_kernel, out_shape=(part,) * chips, in_specs=[SMEM]...  1.72 us
  transfers between devices with their start and end apart: 11, of which 4 were waited for; matrix products, arithmetic and copies ran while one was open for 5% of the time, Pallas kernels for 13%

profile of v1, /device:TPU:0, one launch (start us, length us, event | category | flops | bytes accessed | tf_op | source)
XLA Modules:
  0.0 42.7 jit_solution(9760506182548730359)
XLA Ops:
  0.7 3.8 %border.1 = f32[256,256]{1,0:T(8,128)} custom-call(s32[1,12]{1,0:T(1,128)} %rows.3, s32[1,12]{1,0:T(1,128)} %cols.3, s32[1]{0:T(128)S(6)} %copy.15.count, f32[512,512]{1,0:T(8,128)} %bitcast.6, f32[512,512]{1,0:T(8,128)} %bitcast.8, f32[12,128,128]{2,1,0:T(8,128)} %bitcast.11), custom_call_target="tpu_custom_call" | custom-call | flops 1000000000 | bytes 3145728 | tf_op jit(solution)/shard_map/border/pallas_call | solution.py:158
  4.5 3.0 %collective-permute-start = (f32[256,256]{1,0:T(8,128)}, f32[256,256]{1,0:T(8,128)S(1)}, u32[]{:S(2)}, u32[]{:S(2)}) collective-permute-start(f32[256,256]{1,0:T(8,128)} %border.1), channel_id=1, source_target_pairs={{0,1},{1,2},{2,3},{3,0},{4,5},{5,6},{6,7},{7,4},{8,9},{9,10},{10,1... | collective-permute-start | bytes 786440 | tf_op jit(solution)/shard_map/ppermute | solution.py:168
  7.5 0.7 %copy-done.11 = s32[1,3,2]{1,2,0:T(2,128)S(1)} copy-done((s32[1,3,2]{1,2,0:T(2,128)S(1)}, s32[1,3,2]{1,2,0:T(2,128)}, u32[]{:S(2)}) %copy-start.11) | copy-done | bytes 48
  8.2 0.7 %copy.14.pairs = s32[1,3,2]{2,1,0:T(4,128)} copy(s32[1,3,2]{1,2,0:T(2,128)S(1)} %copy-done.11) | data formatting | bytes 48 | tf_op args[8]
  8.8 0.6 %pad_add_fusion.place = s32[2]{0:T(128)} fusion(s32[1]{0:T(128)} %bitcast.1, s32[1]{0:T(128)} %bitcast), kind=kLoop, calls=%fused_computation.1 | loop fusion | flops 2 | bytes 16 | tf_op jit(solution)/shard_map/stack | solution.py:155
  9.4 5.6 %own.1 = (f32[3,128,128]{2,1,0:T(8,128)}, bf16[512,256]{1,0:T(8,128)(2,1)}, bf16[512,256]{1,0:T(8,128)(2,1)}) custom-call(s32[1,12]{1,0:T(1,128)} %rows.3, s32[1,12]{1,0:T(1,128)} %cols.3, s32[1]{0:T(128)S(6)} %copy.15.count, s32[1,2]{1,0:T(1,128)} %border_map.1, s32[1,3,2]{2,1,0:T(4,128)} %copy.14.pairs, f32[512,512]{1,0:T(8,128)} %bitcast.7, ...), custom_call_target="tpu_custom_call" | custom-call | flops 2000000000 | bytes 5242880 | tf_op jit(solution)/shard_map/own/pallas_call | solution.py:170
  15.0 0.7 %copy-done = f32[256,256]{1,0:T(8,128)} copy-done((f32[256,256]{1,0:T(8,128)}, f32[256,256]{1,0:T(8,128)S(1)}, u32[]{:S(2)}) %copy-start) | copy-done | bytes 262168
  15.7 2.7 %join.1 = (f32[3,32,128]{2,1,0:T(8,128)}, f32[3,32,128]{2,1,0:T(8,128)}, f32[3,32,128]{2,1,0:T(8,128)}, f32[3,32,128]{2,1,0:T(8,128)}) custom-call(s32[1,3,2]{2,1,0:T(4,128)} %copy.14.pairs, s32[2]{0:T(128)} %pad_add_fusion.place, f32[256,256]{1,0:T(8,128)} %copy-done, f32[3,128,128]{2,1,0:T(8,128)} %get-tuple-element.16.own, ...), custom_call_target="tpu_custom_call" | custom-call | tf_op jit(solution)/shard_map/join/pallas_call | solution.py:186
  18.4 1.7 %collective-permute-start.1 = (f32[3,32,128]{2,1,0:T(8,128)}, f32[3,32,128]{2,1,0:T(8,128)S(1)}, u32[]{:S(2)}, u32[]{:S(2)}) collective-permute-start(f32[3,32,128]{2,1,0:T(8,128)} %get-tuple-element.20), channel_id=1, source_target_pairs={{0,8},{4,12},{8,0},{12,4},{16,24},{20,28},{24,16},{28,20},{1,9},{5... | collective-permute-start | bytes 147464 | tf_op jit(solution)/shard_map/ppermute | solution.py:197
  20.1 2.6 %collective-permute-start.2 = (f32[3,32,128]{2,1,0:T(8,128)}, f32[3,32,128]{2,1,0:T(8,128)S(1)}, u32[]{:S(2)}, u32[]{:S(2)}) collective-permute-start(f32[3,32,128]{2,1,0:T(8,128)} %get-tuple-element.21), channel_id=1, source_target_pairs={{0,16},{4,20},{8,24},{12,28},{16,0},{20,4},{24,8},{28,12},{1,17},{... | collective-permute-start | bytes 147464 | tf_op jit(solution)/shard_map/ppermute | solution.py:197
  22.8 0.5 %collective-permute-start.5 = (f32[3,32,128]{2,1,0:T(8,128)S(1)}, f32[3,32,128]{2,1,0:T(8,128)S(1)}, u32[]{:S(2)}, u32[]{:S(2)}) collective-permute-start(f32[3,32,128]{2,1,0:T(8,128)S(1)} %collective-permute-done.1.refs_1_), channel_id=1, source_target_pairs={{0,4},{4,0},{8,12},{12,8},{16,20},{20,16},{24,28},{28,24},{1,5},{5... | collective-permute-start | bytes 147464 | tf_op jit(solution)/shard_map/ppermute | solution.py:200
  23.3 2.5 %collective-permute-done.2.refs_2_ = f32[3,32,128]{2,1,0:T(8,128)S(1)} collective-permute-done((f32[3,32,128]{2,1,0:T(8,128)}, f32[3,32,128]{2,1,0:T(8,128)S(1)}, u32[]{:S(2)}, u32[]{:S(2)}) %collective-permute-start.2) | collective-permute-done | bytes 49184 | tf_op jit(solution)/shard_map/ppermute | solution.py:197
  25.8 3.0 %collective-permute-done.3.refs_3_ = f32[3,32,128]{2,1,0:T(8,128)S(1)} collective-permute-done((f32[3,32,128]{2,1,0:T(8,128)}, f32[3,32,128]{2,1,0:T(8,128)S(1)}, u32[]{:S(2)}, u32[]{:S(2)}) %collective-permute-start.3) | collective-permute-done | bytes 49184 | tf_op jit(solution)/shard_map/ppermute | solution.py:197
  28.8 0.1 cosine_multiply_fusion
  28.9 0.6 %mul.32.cosine = f32[64]{0:T(128)} reshape(f32[8,8]{1,0:T(8,128)S(1)} %cosine_multiply_fusion) | data formatting | bytes 512 | tf_op jit(solution)/shard_map/mul | solution.py:156
  29.6 0.4 collective-permute-done.7.refs_7_
  30.0 0.1 copy-done.4
  30.2 0.6 %copy-done.7 = f32[3,32,128]{2,1,0:T(8,128)} copy-done((f32[3,32,128]{2,1,0:T(8,128)}, f32[3,32,128]{2,1,0:T(8,128)S(1)}, u32[]{:S(2)}) %copy-start.7) | copy-done | bytes 49176
  30.8 1.7 %combine.1 = (f32[3,32,128]{2,1,0:T(8,128)}, f32[3,32,128]{2,1,0:T(8,128)}, f32[3,32,128]{2,1,0:T(8,128)}, f32[3,32,128]{2,1,0:T(8,128)}) custom-call(s32[2]{0:T(128)} %pad_add_fusion.place, f32[64]{0:T(128)} %mul.32.cosine, f32[3,32,128]{2,1,0:T(8,128)} %get-tuple-element.19.refs_0_, f32[3,32,128]{2,1,0:T(8,128)} %copy-done.1, f32[3,32,128]{2,1,0:T(8,128)} %copy-done.2, ...), custom_call_target="tpu_custom_call" | custom-call | tf_op jit(solution)/shard_map/combine/pallas_call | solution.py:204
  32.6 1.2 %collective-permute-start.9 = (f32[3,32,128]{2,1,0:T(8,128)}, f32[3,32,128]{2,1,0:T(8,128)S(1)}, u32[]{:S(2)}, u32[]{:S(2)}) collective-permute-start(f32[3,32,128]{2,1,0:T(8,128)} %get-tuple-element.25), channel_id=1, source_target_pairs={{0,16},{4,20},{8,24},{12,28},{16,0},{20,4},{24,8},{28,12},{1,17},{... | collective-permute-start | bytes 147464 | tf_op jit(solution)/shard_map/ppermute | solution.py:197
  33.7 3.2 %collective-permute-start.10 = (f32[3,32,128]{2,1,0:T(8,128)}, f32[3,32,128]{2,1,0:T(8,128)S(1)}, u32[]{:S(2)}, u32[]{:S(2)}) collective-permute-start(f32[3,32,128]{2,1,0:T(8,128)} %get-tuple-element.26), channel_id=1, source_target_pairs={{0,24},{4,28},{8,16},{12,20},{16,8},{20,12},{24,0},{28,4},{1,25},{... | collective-permute-start | bytes 147464 | tf_op jit(solution)/shard_map/ppermute | solution.py:197
  36.9 3.5 %collective-permute-done.9.refs_2_ = f32[3,32,128]{2,1,0:T(8,128)S(1)} collective-permute-done((f32[3,32,128]{2,1,0:T(8,128)}, f32[3,32,128]{2,1,0:T(8,128)S(1)}, u32[]{:S(2)}, u32[]{:S(2)}) %collective-permute-start.9) | collective-permute-done | bytes 49184 | tf_op jit(solution)/shard_map/ppermute | solution.py:197
  40.5 0.6 %copy-done.9 = f32[3,32,128]{2,1,0:T(8,128)} copy-done((f32[3,32,128]{2,1,0:T(8,128)}, f32[3,32,128]{2,1,0:T(8,128)S(1)}, u32[]{:S(2)}) %copy-start.9) | copy-done | bytes 49176
  41.1 1.6 %gather.1 = f32[1,1,3,128,128]{4,3,2,1,0:T(8,128)} custom-call(s32[2]{0:T(128)} %pad_add_fusion.place, f32[3,32,128]{2,1,0:T(8,128)} %get-tuple-element.23.refs_0_, f32[3,32,128]{2,1,0:T(8,128)} %copy-done.8, f32[3,32,128]{2,1,0:T(8,128)} %copy-done.9, f32[3,32,128]{2,1,0:T(8,128)} %copy-done.10), custom_call_target="tpu_custom_call" | custom-call | tf_op jit(solution)/shard_map/gather/pallas_call | solution.py:212
  (37 shorter events, 0.2 us)
Async XLA Ops:
  4.5 10.5 %collective-permute-start = (f32[256,256]{1,0:T(8,128)}, f32[256,256]{1,0:T(8,128)S(1)}, u32[]{:S(2)}, u32[]{:S(2)}) collective-permute-start(f32[256,256]{1,0:T(8,128)} %border.1), channel_id=1, source_target_pairs={{0,1},{1,2},{2,3},{3,0},{4,5},{5,6},{6,7},{7,4},{8,9},{9,10},{10,1... | collective-permute-start | bytes 786440 | tf_op jit(solution)/shard_map/ppermute | solution.py:168
  7.5 0.7 %copy-start.11 = (s32[1,3,2]{1,2,0:T(2,128)S(1)}, s32[1,3,2]{1,2,0:T(2,128)}, u32[]{:S(2)}) copy-start(s32[1,3,2]{1,2,0:T(2,128)} %param.20) | copy-start | bytes 76
  15.0 0.7 %copy-start = (f32[256,256]{1,0:T(8,128)}, f32[256,256]{1,0:T(8,128)S(1)}, u32[]{:S(2)}) copy-start(f32[256,256]{1,0:T(8,128)S(1)} %collective-permute-done.border) | copy-start | bytes 786436
  18.4 4.4 %collective-permute-start.1 = (f32[3,32,128]{2,1,0:T(8,128)}, f32[3,32,128]{2,1,0:T(8,128)S(1)}, u32[]{:S(2)}, u32[]{:S(2)}) collective-permute-start(f32[3,32,128]{2,1,0:T(8,128)} %get-tuple-element.20), channel_id=1, source_target_pairs={{0,8},{4,12},{8,0},{12,4},{16,24},{20,28},{24,16},{28,20},{1,9},{5... | collective-permute-start | bytes 147464 | tf_op jit(solution)/shard_map/ppermute | solution.py:197
  20.1 5.7 %collective-permute-start.2 = (f32[3,32,128]{2,1,0:T(8,128)}, f32[3,32,128]{2,1,0:T(8,128)S(1)}, u32[]{:S(2)}, u32[]{:S(2)}) collective-permute-start(f32[3,32,128]{2,1,0:T(8,128)} %get-tuple-element.21), channel_id=1, source_target_pairs={{0,16},{4,20},{8,24},{12,28},{16,0},{20,4},{24,8},{28,12},{1,17},{... | collective-permute-start | bytes 147464 | tf_op jit(solution)/shard_map/ppermute | solution.py:197
  22.7 6.1 %copy-start.12 = (f32[8]{0:T(128)S(1)}, f32[8]{0:T(128)}, u32[]{:S(2)}) copy-start(f32[8]{0:T(128)} %param.21) | copy-start | bytes 100
  22.7 6.1 %copy-start.13 = (f32[8]{0:T(128)S(1)}, f32[8]{0:T(128)}, u32[]{:S(2)}) copy-start(f32[8]{0:T(128)} %param.23) | copy-start | bytes 100
  22.7 6.1 %copy-start.14 = (f32[8]{0:T(128)S(1)}, f32[8]{0:T(128)}, u32[]{:S(2)}) copy-start(f32[8]{0:T(128)} %param.22) | copy-start | bytes 100
  22.7 6.1 %collective-permute-start.3 = (f32[3,32,128]{2,1,0:T(8,128)}, f32[3,32,128]{2,1,0:T(8,128)S(1)}, u32[]{:S(2)}, u32[]{:S(2)}) collective-permute-start(f32[3,32,128]{2,1,0:T(8,128)} %get-tuple-element.22), channel_id=1, source_target_pairs={{0,24},{4,28},{8,16},{12,20},{16,8},{20,12},{24,0},{28,4},{1,25},{... | collective-permute-start | bytes 147464 | tf_op jit(solution)/shard_map/ppermute | solution.py:197
  22.8 6.8 %collective-permute-start.4 = (f32[3,32,128]{2,1,0:T(8,128)}, f32[3,32,128]{2,1,0:T(8,128)S(1)}, u32[]{:S(2)}, u32[]{:S(2)}) collective-permute-start(f32[3,32,128]{2,1,0:T(8,128)} %get-tuple-element.19.refs_0_), channel_id=1, source_target_pairs={{0,4},{4,0},{8,12},{12,8},{16,20},{20,16},{24,28},{28,24},{1,5},{5... | collective-permute-start | bytes 147464 | tf_op jit(solution)/shard_map/ppermute | solution.py:200
  22.8 7.2 %copy-start.1 = (f32[3,32,128]{2,1,0:T(8,128)}, f32[3,32,128]{2,1,0:T(8,128)S(1)}, u32[]{:S(2)}) copy-start(f32[3,32,128]{2,1,0:T(8,128)S(1)} %collective-permute-done.1.refs_1_) | copy-start | bytes 147460
  22.8 6.8 %collective-permute-start.5 = (f32[3,32,128]{2,1,0:T(8,128)S(1)}, f32[3,32,128]{2,1,0:T(8,128)S(1)}, u32[]{:S(2)}, u32[]{:S(2)}) collective-permute-start(f32[3,32,128]{2,1,0:T(8,128)S(1)} %collective-permute-done.1.refs_1_), channel_id=1, source_target_pairs={{0,4},{4,0},{8,12},{12,8},{16,20},{20,16},{24,28},{28,24},{1,5},{5... | collective-permute-start | bytes 147464 | tf_op jit(solution)/shard_map/ppermute | solution.py:200
  25.8 4.2 %copy-start.2 = (f32[3,32,128]{2,1,0:T(8,128)}, f32[3,32,128]{2,1,0:T(8,128)S(1)}, u32[]{:S(2)}) copy-start(f32[3,32,128]{2,1,0:T(8,128)S(1)} %collective-permute-done.2.refs_2_) | copy-start | bytes 147460
  25.8 3.8 %collective-permute-start.6 = (f32[3,32,128]{2,1,0:T(8,128)S(1)}, f32[3,32,128]{2,1,0:T(8,128)S(1)}, u32[]{:S(2)}, u32[]{:S(2)}) collective-permute-start(f32[3,32,128]{2,1,0:T(8,128)S(1)} %collective-permute-done.2.refs_2_), channel_id=1, source_target_pairs={{0,4},{4,0},{8,12},{12,8},{16,20},{20,16},{24,28},{28,24},{1,5},{5... | collective-permute-start | bytes 147464 | tf_op jit(solution)/shard_map/ppermute | solution.py:200
  28.8 1.2 %copy-start.3 = (f32[3,32,128]{2,1,0:T(8,128)}, f32[3,32,128]{2,1,0:T(8,128)S(1)}, u32[]{:S(2)}) copy-start(f32[3,32,128]{2,1,0:T(8,128)S(1)} %collective-permute-done.3.refs_3_) | copy-start | bytes 147460
  28.8 1.2 %collective-permute-start.7 = (f32[3,32,128]{2,1,0:T(8,128)S(1)}, f32[3,32,128]{2,1,0:T(8,128)S(1)}, u32[]{:S(2)}, u32[]{:S(2)}) collective-permute-start(f32[3,32,128]{2,1,0:T(8,128)S(1)} %collective-permute-done.3.refs_3_), channel_id=1, source_target_pairs={{0,4},{4,0},{8,12},{12,8},{16,20},{20,16},{24,28},{28,24},{1,5},{5... | collective-permute-start | bytes 147464 | tf_op jit(solution)/shard_map/ppermute | solution.py:200
  29.6 0.6 %copy-start.4 = (f32[3,32,128]{2,1,0:T(8,128)}, f32[3,32,128]{2,1,0:T(8,128)S(1)}, u32[]{:S(2)}) copy-start(f32[3,32,128]{2,1,0:T(8,128)S(1)} %collective-permute-done.4.refs_4_) | copy-start | bytes 147460
  29.6 0.6 %copy-start.5 = (f32[3,32,128]{2,1,0:T(8,128)}, f32[3,32,128]{2,1,0:T(8,128)S(1)}, u32[]{:S(2)}) copy-start(f32[3,32,128]{2,1,0:T(8,128)S(1)} %collective-permute-done.5.refs_5_) | copy-start | bytes 147460
  29.6 0.6 %copy-start.6 = (f32[3,32,128]{2,1,0:T(8,128)}, f32[3,32,128]{2,1,0:T(8,128)S(1)}, u32[]{:S(2)}) copy-start(f32[3,32,128]{2,1,0:T(8,128)S(1)} %collective-permute-done.6.refs_6_) | copy-start | bytes 147460
  32.6 4.4 %collective-permute-start.8 = (f32[3,32,128]{2,1,0:T(8,128)}, f32[3,32,128]{2,1,0:T(8,128)S(1)}, u32[]{:S(2)}, u32[]{:S(2)}) collective-permute-start(f32[3,32,128]{2,1,0:T(8,128)} %get-tuple-element.24), channel_id=1, source_target_pairs={{0,8},{4,12},{8,0},{12,4},{16,24},{20,28},{24,16},{28,20},{1,9},{5... | collective-permute-start | bytes 147464 | tf_op jit(solution)/shard_map/ppermute | solution.py:197
  32.6 7.9 %collective-permute-start.9 = (f32[3,32,128]{2,1,0:T(8,128)}, f32[3,32,128]{2,1,0:T(8,128)S(1)}, u32[]{:S(2)}, u32[]{:S(2)}) collective-permute-start(f32[3,32,128]{2,1,0:T(8,128)} %get-tuple-element.25), channel_id=1, source_target_pairs={{0,16},{4,20},{8,24},{12,28},{16,0},{20,4},{24,8},{28,12},{1,17},{... | collective-permute-start | bytes 147464 | tf_op jit(solution)/shard_map/ppermute | solution.py:197
  33.7 6.7 %collective-permute-start.10 = (f32[3,32,128]{2,1,0:T(8,128)}, f32[3,32,128]{2,1,0:T(8,128)S(1)}, u32[]{:S(2)}, u32[]{:S(2)}) collective-permute-start(f32[3,32,128]{2,1,0:T(8,128)} %get-tuple-element.26), channel_id=1, source_target_pairs={{0,24},{4,28},{8,16},{12,20},{16,8},{20,12},{24,0},{28,4},{1,25},{... | collective-permute-start | bytes 147464 | tf_op jit(solution)/shard_map/ppermute | solution.py:197
  36.9 3.5 %copy-start.8 = (f32[3,32,128]{2,1,0:T(8,128)}, f32[3,32,128]{2,1,0:T(8,128)S(1)}, u32[]{:S(2)}) copy-start(f32[3,32,128]{2,1,0:T(8,128)S(1)} %collective-permute-done.8.refs_1_) | copy-start | bytes 147460
  40.5 0.6 %copy-start.10 = (f32[3,32,128]{2,1,0:T(8,128)}, f32[3,32,128]{2,1,0:T(8,128)S(1)}, u32[]{:S(2)}) copy-start(f32[3,32,128]{2,1,0:T(8,128)S(1)} %collective-permute-done.10.refs_3_) | copy-start | bytes 147460
  (2 other events, 1.2 us)

commit v2 on v1

v2 whole, which is shorter than its diff:
```python
import functools

import jax
import jax.numpy as jnp
from jax import lax
from jax.experimental import pallas as pl
from jax.experimental.pallas import tpu as pltpu
from jax.sharding import PartitionSpec as P


OWN_BLK = 4
BORDER_BLK = 2
CORES = 2
SUBLANES = 8

VMEM = pl.BlockSpec(memory_space=pltpu.VMEM)
SMEM = pl.BlockSpec(memory_space=pltpu.SMEM)
ANY = pl.BlockSpec(memory_space=pl.ANY)
HBM = pl.BlockSpec(memory_space=pltpu.HBM)
CHUNKS = 2
VMEM_LIMIT = 16 << 20


NN = (((1,), (0,)), ((), ()))
NT = (((1,), (1,)), ((), ()))


def split(x):
    high = x.astype(jnp.bfloat16)
    return high, (x - high.astype(jnp.float32)).astype(jnp.bfloat16)


def dot3(a, b, dims):
    mm = functools.partial(
        lax.dot_general, dimension_numbers=dims, preferred_element_type=jnp.float32
    )
    return mm(a[0], b[0]) + (mm(a[0], b[1]) + mm(a[1], b[0]))


def place_fit(rows, cols, count, blocks, high_ref, low_ref, first, last):
    order = blocks.shape[-1]
    high_ref[...] = jnp.zeros(high_ref.shape, high_ref.dtype)
    low_ref[...] = jnp.zeros(low_ref.shape, low_ref.dtype)
    for f in range(blocks.shape[0]):
        row = rows[0, f]

        @pl.when((f < count[0]) & (row >= first) & (row < last))
        def _():
            high, low = split(blocks[f])
            at_row = pl.ds(pl.multiple_of((row - first) * order, order), order)
            at_col = pl.ds(pl.multiple_of(cols[0, f] * order, order), order)
            high_ref[at_row, at_col] = high
            low_ref[at_row, at_col] = low


def border_kernel(
    count, rows_in, cols_in, occ, virt, blocks, out, high_out, low_out,
    rows, cols, occ_buf, virt_buf, blocks_buf, fit_high, fit_low, sems,
):
    points = occ.shape[-1]
    step = points // CHUNKS
    first = [
        pltpu.make_async_copy(src, dst, sems.at[2 * CHUNKS + i])
        for i, (src, dst) in enumerate(
            ((rows_in, rows), (cols_in, cols), (blocks.at[0], blocks_buf))
        )
    ]
    for fetch in first:
        fetch.start()
    fetches = []
    for c in range(CHUNKS):
        at = slice(c * step, (c + 1) * step)
        fetches.append(
            [
                pltpu.make_async_copy(src.at[0, 0, at], dst.at[at], sems.at[2 * c + i])
                for i, (src, dst) in enumerate(((occ, occ_buf), (virt, virt_buf)))
            ]
        )
        for fetch in fetches[c]:
            fetch.start()
    for fetch in first:
        fetch.wait()
    place_fit(rows, cols, count, blocks_buf, fit_high, fit_low, OWN_BLK, OWN_BLK + BORDER_BLK)
    left = None
    for c in range(CHUNKS):
        at = slice(c * step, (c + 1) * step)
        for fetch in fetches[c]:
            fetch.wait()
        product = split(occ_buf[at] * virt_buf[at])
        high_out[at], low_out[at] = product
        term = dot3((fit_high[:, at], fit_low[:, at]), product, NN)
        left = term if left is None else left + term
    out[...] = dot3(split(left), (fit_high[...], fit_low[...]), NT)


def own_kernel(
    rows, cols, count, border_map, pairs, cosine, product_high, product_low, blocks, metric,
    out, row_high, row_low, col_high, col_low, weight,
    fit_high, fit_low, proj_high, proj_low, pick_high, pick_low, edge,
):
    order = blocks.shape[-1]
    place_fit(rows, cols, count, blocks, fit_high, fit_low, 0, OWN_BLK)
    for j in range(BORDER_BLK):
        at = pl.ds(pl.multiple_of(border_map[0, j] * order, order), order)
        edge[:, j * order : (j + 1) * order] = metric[:, at]
    high, low = split(dot3(split(metric[...]), (fit_high[...], fit_low[...]), NN))
    proj_high[...] = high
    proj_low[...] = low
    count_pairs = out.shape[0]
    for p in range(count_pairs):
        here = slice(p * order, (p + 1) * order)
        at = pl.ds(pl.multiple_of(pairs[0, 0, p] * order, order), order)
        pick_high[here, :] = proj_high[at, :]
        pick_low[here, :] = proj_low[at, :]
        row_high[here, :], row_low[here, :] = split(edge[at, :])
        at = pl.ds(pl.multiple_of(pairs[0, 1, p] * order, order), order)
        col_high[here, :], col_low[here, :] = split(edge[at, :])
    left = dot3(
        (pick_high[...], pick_low[...]), (product_high[...], product_low[...]), NN
    )
    for p in range(count_pairs):
        at = pl.ds(pl.multiple_of(pairs[0, 1, p] * order, order), order)
        out[p] = dot3(
            split(left[p * order : (p + 1) * order, :]), (proj_high[at, :], proj_low[at, :]), NT
        )
    index = lax.axis_index("tm")
    chip, core = index // CORES, index % CORES
    chips = weight.shape[0]
    for k in range(chips):
        freq = (chip ^ k) * CORES + core
        for j in range(chips):
            at = (chip ^ j) * CORES
            weight[k, j, 0] = jnp.full(weight.shape[3:], cosine[freq, at + core])
            weight[k, j, 1] = jnp.full(weight.shape[3:], cosine[freq, at + 1 - core])


def join_kernel(border, own, row_high, row_low, col_high, col_low, *refs):
    total, outs = refs[-1], refs[:-1]
    chip = lax.axis_index("tm") // CORES
    count_pairs, order, _ = own.shape
    left = dot3((row_high[...], row_low[...]), split(border[...]), NN)
    for p in range(count_pairs):
        here = slice(p * order, (p + 1) * order)
        total[p] = own[p] + dot3(split(left[here]), (col_high[here], col_low[here]), NT)
    share = outs[0].shape[1]
    for k, out in enumerate(outs):
        at = pl.ds(pl.multiple_of((chip ^ k) * share, share), share)
        out[...] = total[:, at, :]


def combine_kernel(weight, *refs):
    chips = len(refs) // 3
    mine, other, outs = refs[:chips], refs[chips : 2 * chips], refs[2 * chips :]
    for k in range(chips):
        total = jnp.zeros(outs[k].shape, jnp.float32)
        for j in range(chips):
            total += weight[k, j, 0] * mine[j][...]
            total += weight[k, j, 1] * other[j][...]
        outs[k][...] = total


def gather_kernel(*refs):
    parts, out, sems = refs[:-2], refs[-2], refs[-1]
    chip = lax.axis_index("tm") // CORES
    copies = []
    for k, part in enumerate(parts):
        share = part.shape[1]
        at = pl.ds(pl.multiple_of((chip ^ k) * share, share), share)
        copies.append(pltpu.make_async_copy(part, out.at[0, 0, :, at, :], sems.at[k]))
        copies[k].start()
    for copy in copies:
        copy.wait()


def in_vmem(x):
    return pltpu.with_memory_space_constraint(x, pltpu.VMEM)


def in_hbm(x):
    return pltpu.with_memory_space_constraint(x, pltpu.HBM)


def on_device(
    green_occ,
    virtual_green_time,
    fit_rows,
    fit_cols,
    fit_count,
    fit_blocks,
    border_map,
    coulomb_metric_root,
    pair_list,
    times,
    time_weights,
    freqs,
):
    points = green_occ.shape[-1]
    order = fit_blocks.shape[-1]
    own_rows = OWN_BLK * order
    edge_rows = BORDER_BLK * order
    pairs = pair_list.shape[1]
    devices = lax.axis_size("tm")
    chips = devices // CORES
    share = order // chips
    f32, bf16 = jnp.float32, jnp.bfloat16
    cosine = time_weights[None, :] * jnp.cos(freqs[:, None] * times[None, :])
    pair_rows_cols = jnp.swapaxes(pair_list, 1, 2)
    limit = pltpu.CompilerParams(vmem_limit_bytes=VMEM_LIMIT)

    border, product_high, product_low = pl.pallas_call(
        border_kernel,
        out_shape=(
            pltpu.VMEM((edge_rows, edge_rows), f32),
            pltpu.VMEM((points, points), bf16),
            pltpu.VMEM((points, points), bf16),
        ),
        in_specs=[SMEM] + [HBM] * 5,
        out_specs=(VMEM,) * 3,
        scratch_shapes=[pltpu.SMEM(fit_rows.shape, jnp.int32)] * 2
        + [pltpu.VMEM((points, points), f32)] * 2
        + [pltpu.VMEM(fit_blocks.shape[1:], f32)]
        + [pltpu.VMEM((edge_rows, points), bf16)] * 2
        + [pltpu.SemaphoreType.DMA((2 * CHUNKS + 3,))],
        cost_estimate=pl.CostEstimate(flops=10**9, bytes_accessed=3 << 20, transcendentals=0),
        compiler_params=limit,
        name="border",
    )(
        fit_count, in_hbm(fit_rows), in_hbm(fit_cols),
        in_hbm(green_occ), in_hbm(virtual_green_time), in_hbm(fit_blocks),
    )
    sections = lax.axis_size("sec")
    border = lax.ppermute(border, "sec", [(i, (i + 1) % sections) for i in range(sections)])

    edge = pltpu.VMEM((pairs * order, edge_rows), bf16)
    own, row_high, row_low, col_high, col_low, weight = pl.pallas_call(
        own_kernel,
        out_shape=(pltpu.VMEM((pairs, order, order), f32),)
        + (edge,) * 4
        + (pltpu.VMEM((chips, chips, CORES, SUBLANES, order), f32),),
        in_specs=[SMEM] * 6 + [VMEM] * 4,
        out_specs=(VMEM,) * 6,
        scratch_shapes=[pltpu.VMEM((own_rows, points), bf16)] * 4
        + [pltpu.VMEM((pairs * order, points), bf16)] * 2
        + [pltpu.VMEM((own_rows, edge_rows), f32)],
        cost_estimate=pl.CostEstimate(flops=2 * 10**9, bytes_accessed=5 << 20, transcendentals=0),
        compiler_params=limit,
        name="own",
    )(
        fit_rows, fit_cols, fit_count, border_map, pair_rows_cols, cosine,
        in_vmem(product_high), in_vmem(product_low),
        in_vmem(fit_blocks[0]), in_vmem(coulomb_metric_root[0]),
    )

    part = pltpu.VMEM((pairs, share, order), f32)
    parts = pl.pallas_call(
        join_kernel,
        out_shape=(part,) * chips,
        in_specs=[VMEM] * 6,
        out_specs=(VMEM,) * chips,
        scratch_shapes=[pltpu.VMEM((pairs, order, order), f32)],
        compiler_params=limit,
        name="join",
    )(*map(in_vmem, (border, own, row_high, row_low, col_high, col_low)))

    def across(x, k):
        return lax.ppermute(x, "tm", [(i, i ^ (CORES * k)) for i in range(devices)])

    def swap(x):
        return lax.ppermute(x, "tm", [(i, i ^ 1) for i in range(devices)])

    mine = [parts[0]] + [across(parts[k], k) for k in range(1, chips)]
    other = [swap(x) for x in mine]
    tiles = pltpu.VMEM((pairs * share // SUBLANES, SUBLANES, order), f32)
    parts = pl.pallas_call(
        combine_kernel,
        out_shape=(tiles,) * chips,
        in_specs=[VMEM] * (2 * chips + 1),
        out_specs=(VMEM,) * chips,
        compiler_params=limit,
        name="combine",
    )(*(in_vmem(x.reshape(tiles.shape) if x.ndim == 3 else x) for x in (weight, *mine, *other)))
    parts = [x.reshape(part.shape) for x in parts]
    parts = [parts[0]] + [across(parts[k], k) for k in range(1, chips)]
    return pl.pallas_call(
        gather_kernel,
        out_shape=jax.ShapeDtypeStruct((1, 1, pairs, order, order), f32),
        in_specs=[VMEM] * chips,
        out_specs=ANY,
        scratch_shapes=[pltpu.SemaphoreType.DMA((chips,))],
        compiler_params=limit,
        name="gather",
    )(*map(in_vmem, parts))


def solution(mesh):
    return jax.shard_map(
        on_device,
        mesh=mesh,
        in_specs=(
            P("tm", "sec", None, None),
            P("tm", "sec", None, None),
            P("sec", None),
            P("sec", None),
            P("sec"),
            P("sec", None, None, None),
            P("sec", None),
            P("sec", None, None),
            P("sec", None, None),
            P(),
            P(),
            P(),
        ),
        out_specs=P("tm", "sec", None, None, None),
        check_vma=False,
    )
```

time: 43 us -> 34.8 us (0.81)
  Pallas kernels: 15.4 us -> 7.84 us
  waiting for transfers between devices: 9.4 us -> 13 us
  local copies, waits for them, and re-layouts: 4.15 us -> 0.67 us
  other arithmetic: 0.71 us -> 0.11 us
    pallas_call x4, Pallas kernels: 13.8 us -> 7.13 us  [the longest x1 3.22 us: on_device(): pl.pallas_call(own_kernel, out_shape=(pltpu.VMEM((pairs, order, order), f...]
    ppermute x1, waiting for transfers between devices: 0.01 us -> 3.22 us  [on_device(): lax.ppermute(border, 'sec', [(i, (i + 1) % sections) for i in range(secti...]
    unnamed x31 -> x18, local copies, waits for them, and re-layouts: 3.52 us -> 0.67 us
    pallas_call x1, Pallas kernels: 1.57 us -> 0.7 us  [on_device(): pl.pallas_call(gather_kernel, out_shape=jax.ShapeDtypeStruct((1, 1, pairs...]
    ppermute x4, waiting for transfers between devices: 0.43 us -> 1.22 us  [swap(): return lax.ppermute(x, 'tm', [(i, i ^ 1) for i in range(devices)])]
    mul x1 -> x0, local copies, waits for them, and re-layouts: 0.63 us -> none  [on_device(): time_weights[None, :] * jnp.cos(freqs[:, None] * times[None, :])]
    another operation x1 -> x0, other arithmetic: 0.6 us -> none  [on_device(): place = jnp.stack([index // CORES, index % CORES]).astype(jnp.int32)]
  transfers between devices with their start and end apart: 11 -> 11, of which waited for: 4 -> 7; matrix products, arithmetic and copies ran while one was open for 5% -> 0% of each run, Pallas kernels for 13% -> 9%
where the time goes in v2:
time: 34.8 us; the launch traced here: 34.7 us
  waiting for transfers between devices  13 us (37%)
  starting transfers between devices  12.3 us (35%)
  Pallas kernels  7.84 us (23%)
  between operations  0.82 us (2%)
  local copies, waits for them, and re-layouts  0.67 us (2%)
    ppermute x6, starting transfers between devices, across(): return lax.ppermute(x, 'tm', [(i, i ^ CORES * k) for i in range(devices)])  8.9 us
    ppermute x6, waiting for transfers between devices, across(): return lax.ppermute(x, 'tm', [(i, i ^ CORES * k) for i in range(devices)])  8.55 us
    pallas_call x1, Pallas kernels, on_device(): pl.pallas_call(own_kernel, out_shape=(pltpu.VMEM((pairs, order, order), f...  3.22 us
    ppermute x1, waiting for transfers between devices, on_device(): lax.ppermute(border, 'sec', [(i, (i + 1) % sections) for i in range(secti...  3.22 us
    ppermute x1, starting transfers between devices, on_device(): lax.ppermute(border, 'sec', [(i, (i + 1) % sections) for i in range(secti...  3.02 us
    pallas_call x1, Pallas kernels, on_device(): pl.pallas_call(border_kernel, out_shape=(pltpu.VMEM((edge_rows, edge_rows...  3 us
    ppermute x4, waiting for transfers between devices, swap(): return lax.ppermute(x, 'tm', [(i, i ^ 1) for i in range(devices)])  1.22 us
    pallas_call x1, Pallas kernels, on_device(): pl.pallas_call(join_kernel, out_shape=(part,) * chips, in_specs=[VMEM] *...  0.79 us
  transfers between devices with their start and end apart: 11, of which 7 were waited for; matrix products, arithmetic and copies ran while one was open for 0% of the time, Pallas kernels for 9%

profile of v2, /device:TPU:0, one launch (start us, length us, event | category | flops | bytes accessed | tf_op | source)
XLA Modules:
  0.0 34.7 jit_solution(2679743981275393046)
XLA Ops:
  0.7 3.0 %border.1 = (f32[256,256]{1,0:T(8,128)S(1)}, bf16[512,512]{1,0:T(8,128)(2,1)S(1)}, bf16[512,512]{1,0:T(8,128)(2,1)S(1)}) custom-call(s32[1]{0:T(128)S(6)} %copy.13.count, s32[1,12]{1,0:T(1,128)} %rows.1, s32[1,12]{1,0:T(1,128)} %cols.1, f32[1,1,512,512]{3,2,1,0:T(8,128)} %occ.1, f32[1,1,512,512]{3,2,1,0:T(8,128)} %virt.1, f32[1,12,128,128]{3,2,1,0:T(8,128)} %blocks.1), custom_call_target="tpu_custom_call" | custom-call | flops 1000000000 | bytes 3145728 | tf_op jit(solution)/shard_map/border/pallas_call | solution.py:210
  3.7 0.0 copy-start.7
  3.7 0.0 copy-start.8
  3.7 3.0 %collective-permute-start = (f32[256,256]{1,0:T(8,128)S(1)}, f32[256,256]{1,0:T(8,128)S(1)}, u32[]{:S(2)}, u32[]{:S(2)}) collective-permute-start(f32[256,256]{1,0:T(8,128)S(1)} %get-tuple-element.25), channel_id=1, source_target_pairs={{0,1},{1,2},{2,3},{3,0},{4,5},{5,6},{6,7},{7,4},{8,9},{9,10},{10,1... | collective-permute-start | bytes 786440 | tf_op jit(solution)/shard_map/ppermute | solution.py:232
  6.8 0.1 cosine_multiply_fusion.cosine
  6.9 0.6 %copy-done.2 = s32[1,3,2]{1,2,0:T(2,128)S(1)} copy-done((s32[1,3,2]{1,2,0:T(2,128)S(1)}, s32[1,3,2]{1,2,0:T(2,128)}, u32[]{:S(2)}) %copy-start.2) | copy-done | bytes 48
  7.6 3.2 %own.1 = (f32[3,128,128]{2,1,0:T(8,128)S(1)}, bf16[384,256]{1,0:T(8,128)(2,1)S(1)}, bf16[384,256]{1,0:T(8,128)(2,1)S(1)}, bf16[384,256]{1,0:T(8,128)(2,1)S(1)}, ...) custom-call(s32[1,12]{1,0:T(1,128)S(1)} %copy-done.3, s32[1,12]{1,0:T(1,128)S(1)} %copy-done.4, ...), custom_call_target="tpu_custom_call" | custom-call | flops 2000000000 | bytes 5242880 | tf_op jit(solution)/shard_map/own/pallas_call | solution.py:235
  10.8 3.2 %collective-permute-done.border = f32[256,256]{1,0:T(8,128)S(1)} collective-permute-done((f32[256,256]{1,0:T(8,128)S(1)}, f32[256,256]{1,0:T(8,128)S(1)}, u32[]{:S(2)}, u32[]{:S(2)}) %collective-permute-start) | collective-permute-done | bytes 262176 | tf_op jit(solution)/shard_map/ppermute | solution.py:232
  14.0 0.8 %join.1 = (f32[3,32,128]{2,1,0:T(8,128)S(1)}, f32[3,32,128]{2,1,0:T(8,128)S(1)}, f32[3,32,128]{2,1,0:T(8,128)S(1)}, f32[3,32,128]{2,1,0:T(8,128)S(1)}) custom-call(f32[256,256]{1,0:T(8,128)S(1)} %collective-permute-done.border, f32[3,128,128]{2,1,0:T(8,128)S(1)} %get-tuple-element.26.own, bf16[384,256]{1,0:T(8,128)(2,1)S(1)} %get-tuple-element.27.row_high, ...), custom_call_target="tpu_custom_call" | custom-call | tf_op jit(solution)/shard_map/join/pallas_call | solution.py:255
  14.8 1.8 %collective-permute-start.1 = (f32[3,32,128]{2,1,0:T(8,128)S(1)}, f32[3,32,128]{2,1,0:T(8,128)S(1)}, u32[]{:S(2)}, u32[]{:S(2)}) collective-permute-start(f32[3,32,128]{2,1,0:T(8,128)S(1)} %get-tuple-element.32), channel_id=1, source_target_pairs={{0,8},{4,12},{8,0},{12,4},{16,24},{20,28},{24,16},{28,20},{1,9},{5... | collective-permute-start | bytes 147464 | tf_op jit(solution)/shard_map/ppermute | solution.py:266
  16.7 2.6 %collective-permute-start.2 = (f32[3,32,128]{2,1,0:T(8,128)S(1)}, f32[3,32,128]{2,1,0:T(8,128)S(1)}, u32[]{:S(2)}, u32[]{:S(2)}) collective-permute-start(f32[3,32,128]{2,1,0:T(8,128)S(1)} %get-tuple-element.33), channel_id=1, source_target_pairs={{0,16},{4,20},{8,24},{12,28},{16,0},{20,4},{24,8},{28,12},{1,17},{... | collective-permute-start | bytes 147464 | tf_op jit(solution)/shard_map/ppermute | solution.py:266
  19.3 0.0 collective-permute-start.3
  19.3 0.2 collective-permute-done.1
  19.4 0.3 collective-permute-start.5
  19.8 2.9 %collective-permute-done.2 = f32[3,32,128]{2,1,0:T(8,128)S(1)} collective-permute-done((f32[3,32,128]{2,1,0:T(8,128)S(1)}, f32[3,32,128]{2,1,0:T(8,128)S(1)}, u32[]{:S(2)}, u32[]{:S(2)}) %collective-permute-start.2) | collective-permute-done | bytes 49184 | tf_op jit(solution)/shard_map/ppermute | solution.py:266
  22.7 2.4 %collective-permute-done.3 = f32[3,32,128]{2,1,0:T(8,128)S(1)} collective-permute-done((f32[3,32,128]{2,1,0:T(8,128)S(1)}, f32[3,32,128]{2,1,0:T(8,128)S(1)}, u32[]{:S(2)}, u32[]{:S(2)}) %collective-permute-start.3) | collective-permute-done | bytes 49184 | tf_op jit(solution)/shard_map/ppermute | solution.py:266
  25.2 1.2 %collective-permute-done.7 = f32[3,32,128]{2,1,0:T(8,128)S(1)} collective-permute-done((f32[3,32,128]{2,1,0:T(8,128)S(1)}, f32[3,32,128]{2,1,0:T(8,128)S(1)}, u32[]{:S(2)}, u32[]{:S(2)}) %collective-permute-start.7) | collective-permute-done | bytes 49184 | tf_op jit(solution)/shard_map/ppermute | solution.py:269
  26.4 0.1 combine.1
  26.5 0.1 collective-permute-start.8
  26.6 1.1 %collective-permute-start.9 = (f32[3,32,128]{2,1,0:T(8,128)S(1)}, f32[3,32,128]{2,1,0:T(8,128)S(1)}, u32[]{:S(2)}, u32[]{:S(2)}) collective-permute-start(f32[3,32,128]{2,1,0:T(8,128)S(1)} %bitcast.27), channel_id=1, source_target_pairs={{0,16},{4,20},{8,24},{12,28},{16,0},{20,4},{24,8},{28,12},{1,17},{... | collective-permute-start | bytes 147464 | tf_op jit(solution)/shard_map/ppermute | solution.py:266
  27.7 3.3 %collective-permute-start.10 = (f32[3,32,128]{2,1,0:T(8,128)S(1)}, f32[3,32,128]{2,1,0:T(8,128)S(1)}, u32[]{:S(2)}, u32[]{:S(2)}) collective-permute-start(f32[3,32,128]{2,1,0:T(8,128)S(1)} %bitcast.26), channel_id=1, source_target_pairs={{0,24},{4,28},{8,16},{12,20},{16,8},{20,12},{24,0},{28,4},{1,25},{... | collective-permute-start | bytes 147464 | tf_op jit(solution)/shard_map/ppermute | solution.py:266
  30.9 0.3 collective-permute-done.8.refs_1_
  31.2 2.7 %collective-permute-done.9.refs_2_ = f32[3,32,128]{2,1,0:T(8,128)S(1)} collective-permute-done((f32[3,32,128]{2,1,0:T(8,128)S(1)}, f32[3,32,128]{2,1,0:T(8,128)S(1)}, u32[]{:S(2)}, u32[]{:S(2)}) %collective-permute-start.9) | collective-permute-done | bytes 49184 | tf_op jit(solution)/shard_map/ppermute | solution.py:266
  34.0 0.7 %gather.1 = f32[1,1,3,128,128]{4,3,2,1,0:T(8,128)} custom-call(f32[3,32,128]{2,1,0:T(8,128)S(1)} %bitcast.21, f32[3,32,128]{2,1,0:T(8,128)S(1)} %collective-permute-done.8.refs_1_, f32[3,32,128]{2,1,0:T(8,128)S(1)} %collective-permute-done.9.refs_2_, f32[3,32,128]{2,1,0:T(8,128)S(1)} %collective-permute-done.10.refs_3_), custom_call_target="tpu_custom_call" | custom-call | tf_op jit(solution)/shard_map/gather/pallas_call | solution.py:284
  (22 shorter events, 0.1 us)
Async XLA Ops:
  0.7 6.3 %copy-start = (f32[1,512,512]{2,1,0:T(8,128)S(1)}, f32[1,512,512]{2,1,0:T(8,128)}, u32[]{:S(2)}) copy-start(f32[1,512,512]{2,1,0:T(8,128)} %param.19) | copy-start | bytes 3145732
  0.7 6.3 %copy-start.1 = (f32[1,12,128,128]{3,2,1,0:T(8,128)S(1)}, f32[1,12,128,128]{3,2,1,0:T(8,128)}, u32[]{:S(2)}) copy-start(f32[1,12,128,128]{3,2,1,0:T(8,128)} %blocks.1) | copy-start | bytes 2359300
  0.7 6.3 %copy-start.4 = (s32[1,12]{1,0:T(1,128)S(1)}, s32[1,12]{1,0:T(1,128)}, u32[]{:S(2)}) copy-start(s32[1,12]{1,0:T(1,128)} %cols.1) | copy-start | bytes 148
  0.7 6.3 %copy-start.5 = (s32[1,2]{1,0:T(1,128)S(1)}, s32[1,2]{1,0:T(1,128)}, u32[]{:S(2)}) copy-start(s32[1,2]{1,0:T(1,128)} %border_map.1) | copy-start | bytes 28
  3.7 3.1 %copy-start.6 = (f32[8]{0:T(128)S(1)}, f32[8]{0:T(128)}, u32[]{:S(2)}) copy-start(f32[8]{0:T(128)} %param.21) | copy-start | bytes 100
  3.7 3.0 %copy-start.7 = (f32[8]{0:T(128)S(1)}, f32[8]{0:T(128)}, u32[]{:S(2)}) copy-start(f32[8]{0:T(128)} %param.23) | copy-start | bytes 100
  3.7 3.0 %copy-start.8 = (f32[8]{0:T(128)S(1)}, f32[8]{0:T(128)}, u32[]{:S(2)}) copy-start(f32[8]{0:T(128)} %param.22) | copy-start | bytes 100
  3.7 10.3 %collective-permute-start = (f32[256,256]{1,0:T(8,128)S(1)}, f32[256,256]{1,0:T(8,128)S(1)}, u32[]{:S(2)}, u32[]{:S(2)}) collective-permute-start(f32[256,256]{1,0:T(8,128)S(1)} %get-tuple-element.25), channel_id=1, source_target_pairs={{0,1},{1,2},{2,3},{3,0},{4,5},{5,6},{6,7},{7,4},{8,9},{9,10},{10,1... | collective-permute-start | bytes 786440 | tf_op jit(solution)/shard_map/ppermute | solution.py:232
  6.9 0.7 %copy-start.2 = (s32[1,3,2]{1,2,0:T(2,128)S(1)}, s32[1,3,2]{1,2,0:T(2,128)}, u32[]{:S(2)}) copy-start(s32[1,3,2]{1,2,0:T(2,128)} %param.20) | copy-start | bytes 76
  6.9 0.7 %copy-start.3 = (s32[1,12]{1,0:T(1,128)S(1)}, s32[1,12]{1,0:T(1,128)}, u32[]{:S(2)}) copy-start(s32[1,12]{1,0:T(1,128)} %rows.1) | copy-start | bytes 148
  14.8 4.6 %collective-permute-start.1 = (f32[3,32,128]{2,1,0:T(8,128)S(1)}, f32[3,32,128]{2,1,0:T(8,128)S(1)}, u32[]{:S(2)}, u32[]{:S(2)}) collective-permute-start(f32[3,32,128]{2,1,0:T(8,128)S(1)} %get-tuple-element.32), channel_id=1, source_target_pairs={{0,8},{4,12},{8,0},{12,4},{16,24},{20,28},{24,16},{28,20},{1,9},{5... | collective-permute-start | bytes 147464 | tf_op jit(solution)/shard_map/ppermute | solution.py:266
  16.7 6.0 %collective-permute-start.2 = (f32[3,32,128]{2,1,0:T(8,128)S(1)}, f32[3,32,128]{2,1,0:T(8,128)S(1)}, u32[]{:S(2)}, u32[]{:S(2)}) collective-permute-start(f32[3,32,128]{2,1,0:T(8,128)S(1)} %get-tuple-element.33), channel_id=1, source_target_pairs={{0,16},{4,20},{8,24},{12,28},{16,0},{20,4},{24,8},{28,12},{1,17},{... | collective-permute-start | bytes 147464 | tf_op jit(solution)/shard_map/ppermute | solution.py:266
  19.3 5.9 %collective-permute-start.3 = (f32[3,32,128]{2,1,0:T(8,128)S(1)}, f32[3,32,128]{2,1,0:T(8,128)S(1)}, u32[]{:S(2)}, u32[]{:S(2)}) collective-permute-start(f32[3,32,128]{2,1,0:T(8,128)S(1)} %get-tuple-element.34), channel_id=1, source_target_pairs={{0,24},{4,28},{8,16},{12,20},{16,8},{20,12},{24,0},{28,4},{1,25},{... | collective-permute-start | bytes 147464 | tf_op jit(solution)/shard_map/ppermute | solution.py:266
  19.3 5.9 %collective-permute-start.4 = (f32[3,32,128]{2,1,0:T(8,128)S(1)}, f32[3,32,128]{2,1,0:T(8,128)S(1)}, u32[]{:S(2)}, u32[]{:S(2)}) collective-permute-start(f32[3,32,128]{2,1,0:T(8,128)S(1)} %get-tuple-element.31), channel_id=1, source_target_pairs={{0,4},{4,0},{8,12},{12,8},{16,20},{20,16},{24,28},{28,24},{1,5},{5... | collective-permute-start | bytes 147464 | tf_op jit(solution)/shard_map/ppermute | solution.py:269
  19.4 5.7 %collective-permute-start.5 = (f32[3,32,128]{2,1,0:T(8,128)S(1)}, f32[3,32,128]{2,1,0:T(8,128)S(1)}, u32[]{:S(2)}, u32[]{:S(2)}) collective-permute-start(f32[3,32,128]{2,1,0:T(8,128)S(1)} %collective-permute-done.1), channel_id=1, source_target_pairs={{0,4},{4,0},{8,12},{12,8},{16,20},{20,16},{24,28},{28,24},{1,5},{5... | collective-permute-start | bytes 147464 | tf_op jit(solution)/shard_map/ppermute | solution.py:269
  22.7 2.5 %collective-permute-start.6 = (f32[3,32,128]{2,1,0:T(8,128)S(1)}, f32[3,32,128]{2,1,0:T(8,128)S(1)}, u32[]{:S(2)}, u32[]{:S(2)}) collective-permute-start(f32[3,32,128]{2,1,0:T(8,128)S(1)} %collective-permute-done.2), channel_id=1, source_target_pairs={{0,4},{4,0},{8,12},{12,8},{16,20},{20,16},{24,28},{28,24},{1,5},{5... | collective-permute-start | bytes 147464 | tf_op jit(solution)/shard_map/ppermute | solution.py:269
  25.1 1.2 %collective-permute-start.7 = (f32[3,32,128]{2,1,0:T(8,128)S(1)}, f32[3,32,128]{2,1,0:T(8,128)S(1)}, u32[]{:S(2)}, u32[]{:S(2)}) collective-permute-start(f32[3,32,128]{2,1,0:T(8,128)S(1)} %collective-permute-done.3), channel_id=1, source_target_pairs={{0,4},{4,0},{8,12},{12,8},{16,20},{20,16},{24,28},{28,24},{1,5},{5... | collective-permute-start | bytes 147464 | tf_op jit(solution)/shard_map/ppermute | solution.py:269
  26.5 4.8 %collective-permute-start.8 = (f32[3,32,128]{2,1,0:T(8,128)S(1)}, f32[3,32,128]{2,1,0:T(8,128)S(1)}, u32[]{:S(2)}, u32[]{:S(2)}) collective-permute-start(f32[3,32,128]{2,1,0:T(8,128)S(1)} %bitcast.28), channel_id=1, source_target_pairs={{0,8},{4,12},{8,0},{12,4},{16,24},{20,28},{24,16},{28,20},{1,9},{5... | collective-permute-start | bytes 147464 | tf_op jit(solution)/shard_map/ppermute | solution.py:266
  26.6 7.4 %collective-permute-start.9 = (f32[3,32,128]{2,1,0:T(8,128)S(1)}, f32[3,32,128]{2,1,0:T(8,128)S(1)}, u32[]{:S(2)}, u32[]{:S(2)}) collective-permute-start(f32[3,32,128]{2,1,0:T(8,128)S(1)} %bitcast.27), channel_id=1, source_target_pairs={{0,16},{4,20},{8,24},{12,28},{16,0},{20,4},{24,8},{28,12},{1,17},{... | collective-permute-start | bytes 147464 | tf_op jit(solution)/shard_map/ppermute | solution.py:266
  27.7 6.3 %collective-permute-start.10 = (f32[3,32,128]{2,1,0:T(8,128)S(1)}, f32[3,32,128]{2,1,0:T(8,128)S(1)}, u32[]{:S(2)}, u32[]{:S(2)}) collective-permute-start(f32[3,32,128]{2,1,0:T(8,128)S(1)} %bitcast.26), channel_id=1, source_target_pairs={{0,24},{4,28},{8,16},{12,20},{16,8},{20,12},{24,0},{28,4},{1,25},{... | collective-permute-start | bytes 147464 | tf_op jit(solution)/shard_map/ppermute | solution.py:266

commit v3 on v2

--- a/solution.py
+++ b/solution.py
@@ -21,8 +21,35 @@
 VMEM_LIMIT = 16 << 20
 
 
+ROUTES = ("xor", "ring")
+
+
 NN = (((1,), (0,)), ((), ()))
 NT = (((1,), (1,)), ((), ()))
+
+
+def pick(flag, yes, no):
+    return (yes if flag else no) if isinstance(flag, bool) else jnp.where(flag, yes, no)
+
+
+def ring_place(chip, chips):
+    return pick(chip % 2 == 1, (chip + 1) // 2, (chips - chip // 2) % chips)
+
+
+def ring_chip(place, chips):
+    return pick(place == 0, 0, pick(place <= chips // 2, 2 * place - 1, 2 * (chips - place)))
+
+
+def to_chip(phase, chip, step, chips):
+    if ROUTES[phase] == "xor":
+        return chip ^ step
+    return ring_chip((ring_place(chip, chips) + step) % chips, chips)
+
+
+def from_chip(phase, chip, step, chips):
+    if ROUTES[phase] == "xor":
+        return chip ^ step
+    return ring_chip((ring_place(chip, chips) + chips - step) % chips, chips)
 
 
 def split(x):
@@ -54,8 +81,8 @@
 
 
 def border_kernel(
-    count, rows_in, cols_in, occ, virt, blocks, out, high_out, low_out,
-    rows, cols, occ_buf, virt_buf, blocks_buf, fit_high, fit_low, sems,
+    count, rows_in, cols_in, occ, virt, blocks, out, high_out, low_out, blocks_buf,
+    rows, cols, occ_buf, virt_buf, fit_high, fit_low, sems,
 ):
     points = occ.shape[-1]
     step = points // CHUNKS
@@ -127,9 +154,9 @@
     chip, core = index // CORES, index % CORES
     chips = weight.shape[0]
     for k in range(chips):
-        freq = (chip ^ k) * CORES + core
+        freq = to_chip(1, chip, k, chips) * CORES + core
         for j in range(chips):
-            at = (chip ^ j) * CORES
+            at = from_chip(0, chip, j, chips) * CORES
             weight[k, j, 0] = jnp.full(weight.shape[3:], cosine[freq, at + core])
             weight[k, j, 1] = jnp.full(weight.shape[3:], cosine[freq, at + 1 - core])
 
@@ -144,7 +171,7 @@
         total[p] = own[p] + dot3(split(left[here]), (col_high[here], col_low[here]), NT)
     share = outs[0].shape[1]
     for k, out in enumerate(outs):
-        at = pl.ds(pl.multiple_of((chip ^ k) * share, share), share)
+        at = pl.ds(pl.multiple_of(to_chip(0, chip, k, len(outs)) * share, share), share)
         out[...] = total[:, at, :]
 
 
@@ -165,7 +192,7 @@
     copies = []
     for k, part in enumerate(parts):
         share = part.shape[1]
-        at = pl.ds(pl.multiple_of((chip ^ k) * share, share), share)
+        at = pl.ds(pl.multiple_of(from_chip(1, chip, k, len(parts)) * share, share), share)
         copies.append(pltpu.make_async_copy(part, out.at[0, 0, :, at, :], sems.at[k]))
         copies[k].start()
     for copy in copies:
@@ -207,18 +234,18 @@
     pair_rows_cols = jnp.swapaxes(pair_list, 1, 2)
     limit = pltpu.CompilerParams(vmem_limit_bytes=VMEM_LIMIT)
 
-    border, product_high, product_low = pl.pallas_call(
+    border, product_high, product_low, blocks = pl.pallas_call(
         border_kernel,
         out_shape=(
             pltpu.VMEM((edge_rows, edge_rows), f32),
             pltpu.VMEM((points, points), bf16),
             pltpu.VMEM((points, points), bf16),
+            pltpu.VMEM(fit_blocks.shape[1:], f32),
         ),
         in_specs=[SMEM] + [HBM] * 5,
-        out_specs=(VMEM,) * 3,
+        out_specs=(VMEM,) * 4,
         scratch_shapes=[pltpu.SMEM(fit_rows.shape, jnp.int32)] * 2
         + [pltpu.VMEM((points, points), f32)] * 2
-        + [pltpu.VMEM(fit_blocks.shape[1:], f32)]
         + [pltpu.VMEM((edge_rows, points), bf16)] * 2
         + [pltpu.SemaphoreType.DMA((2 * CHUNKS + 3,))],
         cost_estimate=pl.CostEstimate(flops=10**9, bytes_accessed=3 << 20, transcendentals=0),
@@ -248,7 +275,7 @@
     )(
         fit_rows, fit_cols, fit_count, border_map, pair_rows_cols, cosine,
         in_vmem(product_high), in_vmem(product_low),
-        in_vmem(fit_blocks[0]), in_vmem(coulomb_metric_root[0]),
+        in_vmem(blocks), in_hbm(coulomb_metric_root[0]),
     )
 
     part = pltpu.VMEM((pairs, share, order), f32)
@@ -262,13 +289,16 @@
         name="join",
     )(*map(in_vmem, (border, own, row_high, row_low, col_high, col_low)))
 
-    def across(x, k):
-        return lax.ppermute(x, "tm", [(i, i ^ (CORES * k)) for i in range(devices)])
+    def across(x, k, phase):
+        pairs_of = [
+            (i, to_chip(phase, i // CORES, k, chips) * CORES + i % CORES) for i in range(devices)
+        ]
+        return lax.ppermute(x, "tm", pairs_of)
 
     def swap(x):
         return lax.ppermute(x, "tm", [(i, i ^ 1) for i in range(devices)])
 
-    mine = [parts[0]] + [across(parts[k], k) for k in range(1, chips)]
+    mine = [parts[0]] + [across(parts[k], k, 0) for k in range(1, chips)]
     other = [swap(x) for x in mine]
     tiles = pltpu.VMEM((pairs * share // SUBLANES, SUBLANES, order), f32)
     parts = pl.pallas_call(
@@ -280,7 +310,7 @@
         name="combine",
     )(*(in_vmem(x.reshape(tiles.shape) if x.ndim == 3 else x) for x in (weight, *mine, *other)))
     parts = [x.reshape(part.shape) for x in parts]
-    parts = [parts[0]] + [across(parts[k], k) for k in range(1, chips)]
+    parts = [parts[0]] + [across(parts[k], k, 1) for k in range(1, chips)]
     return pl.pallas_call(
         gather_kernel,
         out_shape=jax.ShapeDtypeStruct((1, 1, pairs, order, order), f32),

time: 34.8 us -> 34.1 us (0.980)
  starting transfers between devices: 12.3 us -> 10.8 us
  Pallas kernels: 7.84 us -> 8.32 us
    ppermute x6, starting transfers between devices: 8.9 us -> 7.42 us  [across(): return lax.ppermute(x, 'tm', pairs_of)]
    ppermute x6, waiting for transfers between devices: 8.55 us -> 9.38 us  [across(): return lax.ppermute(x, 'tm', pairs_of)]
    pallas_call x1, Pallas kernels: 3.22 us -> 3.83 us  [on_device(): pl.pallas_call(own_kernel, out_shape=(pltpu.VMEM((pairs, order, order), f...]
    ppermute x1, waiting for transfers between devices: 3.22 us -> 2.62 us  [on_device(): lax.ppermute(border, 'sec', [(i, (i + 1) % sections) for i in range(secti...]
  transfers between devices with their start and end apart: 11 -> 11, of which waited for: 7 -> 6; matrix products, arithmetic and copies ran while one was open for 0% -> 0% of each run, Pallas kernels for 9% -> 11%
where the time goes in v3:
time: 34.1 us; the launch traced here: 33.9 us
  waiting for transfers between devices  13.2 us (39%)
  starting transfers between devices  10.8 us (32%)
  Pallas kernels  8.32 us (24%)
  between operations  0.78 us (2%)
  local copies, waits for them, and re-layouts  0.68 us (2%)
    ppermute x6, waiting for transfers between devices, across(): return lax.ppermute(x, 'tm', pairs_of)  9.38 us
    ppermute x6, starting transfers between devices, across(): return lax.ppermute(x, 'tm', pairs_of)  7.42 us
    pallas_call x1, Pallas kernels, on_device(): pl.pallas_call(own_kernel, out_shape=(pltpu.VMEM((pairs, order, order), f...  3.83 us
    ppermute x1, starting transfers between devices, on_device(): lax.ppermute(border, 'sec', [(i, (i + 1) % sections) for i in range(secti...  3.03 us
    pallas_call x1, Pallas kernels, on_device(): pl.pallas_call(border_kernel, out_shape=(pltpu.VMEM((edge_rows, edge_rows...  2.88 us
    ppermute x1, waiting for transfers between devices, on_device(): lax.ppermute(border, 'sec', [(i, (i + 1) % sections) for i in range(secti...  2.62 us
    ppermute x4, waiting for transfers between devices, swap(): return lax.ppermute(x, 'tm', [(i, i ^ 1) for i in range(devices)])  1.22 us
    pallas_call x1, Pallas kernels, on_device(): pl.pallas_call(join_kernel, out_shape=(part,) * chips, in_specs=[VMEM] *...  0.79 us
  transfers between devices with their start and end apart: 11, of which 6 were waited for; matrix products, arithmetic and copies ran while one was open for 0% of the time, Pallas kernels for 11%

profile of v3, /device:TPU:0, one launch (start us, length us, event | category | flops | bytes accessed | tf_op | source)
XLA Modules:
  0.0 33.9 jit_solution(10773359124173117912)
XLA Ops:
  0.7 2.9 %border.1 = (f32[256,256]{1,0:T(8,128)S(1)}, bf16[512,512]{1,0:T(8,128)(2,1)S(1)}, bf16[512,512]{1,0:T(8,128)(2,1)S(1)}, f32[12,128,128]{2,1,0:T(8,128)S(1)}) custom-call(s32[1]{0:T(128)S(6)} %copy.13.count, s32[1,12]{1,0:T(1,128)} %rows.1, s32[1,12]{1,0:T(1,128)} %cols.1, f32[1,1,512,512]{3,2,1,0:T(8,128)} %occ.1, f32[1,1,512,512]{3,2,1,0:T(8,128)} %virt.1, ...), custom_call_target="tpu_custom_call" | custom-call | flops 1000000000 | bytes 3145728 | tf_op jit(solution)/shard_map/border/pallas_call | solution.py:237
  3.6 0.0 copy-start.5
  3.6 0.0 copy-start.6
  3.6 3.0 %collective-permute-start = (f32[256,256]{1,0:T(8,128)S(1)}, f32[256,256]{1,0:T(8,128)S(1)}, u32[]{:S(2)}, u32[]{:S(2)}) collective-permute-start(f32[256,256]{1,0:T(8,128)S(1)} %get-tuple-element.27), channel_id=1, source_target_pairs={{0,1},{1,2},{2,3},{3,0},{4,5},{5,6},{6,7},{7,4},{8,9},{9,10},{10,1... | collective-permute-start | bytes 786440 | tf_op jit(solution)/shard_map/ppermute | solution.py:259
  6.6 0.1 cosine_multiply_fusion.cosine
  6.8 0.0 copy-start.1
  6.8 0.6 %copy-done = s32[1,3,2]{1,2,0:T(2,128)S(1)} copy-done((s32[1,3,2]{1,2,0:T(2,128)S(1)}, s32[1,3,2]{1,2,0:T(2,128)}, u32[]{:S(2)}) %copy-start) | copy-done | bytes 48
  7.4 3.8 %own.1 = (f32[3,128,128]{2,1,0:T(8,128)S(1)}, bf16[384,256]{1,0:T(8,128)(2,1)S(1)}, bf16[384,256]{1,0:T(8,128)(2,1)S(1)}, bf16[384,256]{1,0:T(8,128)(2,1)S(1)}, ...) custom-call(s32[1,12]{1,0:T(1,128)S(1)} %copy-done.1, s32[1,12]{1,0:T(1,128)S(1)} %copy-done.2, ...), custom_call_target="tpu_custom_call" | custom-call | flops 2000000000 | bytes 5242880 | tf_op jit(solution)/shard_map/own/pallas_call | solution.py:262
  11.3 2.6 %collective-permute-done.border = f32[256,256]{1,0:T(8,128)S(1)} collective-permute-done((f32[256,256]{1,0:T(8,128)S(1)}, f32[256,256]{1,0:T(8,128)S(1)}, u32[]{:S(2)}, u32[]{:S(2)}) %collective-permute-start) | collective-permute-done | bytes 262176 | tf_op jit(solution)/shard_map/ppermute | solution.py:259
  13.9 0.8 %join.1 = (f32[3,32,128]{2,1,0:T(8,128)S(1)}, f32[3,32,128]{2,1,0:T(8,128)S(1)}, f32[3,32,128]{2,1,0:T(8,128)S(1)}, f32[3,32,128]{2,1,0:T(8,128)S(1)}) custom-call(f32[256,256]{1,0:T(8,128)S(1)} %collective-permute-done.border, f32[3,128,128]{2,1,0:T(8,128)S(1)} %get-tuple-element.28.own, bf16[384,256]{1,0:T(8,128)(2,1)S(1)} %get-tuple-element.29.row_high, ...), custom_call_target="tpu_custom_call" | custom-call | tf_op jit(solution)/shard_map/join/pallas_call | solution.py:282
  14.7 1.8 %collective-permute-start.1 = (f32[3,32,128]{2,1,0:T(8,128)S(1)}, f32[3,32,128]{2,1,0:T(8,128)S(1)}, u32[]{:S(2)}, u32[]{:S(2)}) collective-permute-start(f32[3,32,128]{2,1,0:T(8,128)S(1)} %get-tuple-element.34), channel_id=1, source_target_pairs={{0,8},{4,12},{8,0},{12,4},{16,24},{20,28},{24,16},{28,20},{1,9},{5... | collective-permute-start | bytes 147464 | tf_op jit(solution)/shard_map/ppermute | solution.py:296
  16.5 2.6 %collective-permute-start.2 = (f32[3,32,128]{2,1,0:T(8,128)S(1)}, f32[3,32,128]{2,1,0:T(8,128)S(1)}, u32[]{:S(2)}, u32[]{:S(2)}) collective-permute-start(f32[3,32,128]{2,1,0:T(8,128)S(1)} %get-tuple-element.35), channel_id=1, source_target_pairs={{0,16},{4,20},{8,24},{12,28},{16,0},{20,4},{24,8},{28,12},{1,17},{... | collective-permute-start | bytes 147464 | tf_op jit(solution)/shard_map/ppermute | solution.py:296
  19.1 0.0 collective-permute-start.3
  19.1 0.2 collective-permute-done.1
  19.3 0.4 %collective-permute-start.5 = (f32[3,32,128]{2,1,0:T(8,128)S(1)}, f32[3,32,128]{2,1,0:T(8,128)S(1)}, u32[]{:S(2)}, u32[]{:S(2)}) collective-permute-start(f32[3,32,128]{2,1,0:T(8,128)S(1)} %collective-permute-done.1), channel_id=1, source_target_pairs={{0,4},{4,0},{8,12},{12,8},{16,20},{20,16},{24,28},{28,24},{1,5},{5... | collective-permute-start | bytes 147464 | tf_op jit(solution)/shard_map/ppermute | solution.py:299
  19.7 2.9 %collective-permute-done.2 = f32[3,32,128]{2,1,0:T(8,128)S(1)} collective-permute-done((f32[3,32,128]{2,1,0:T(8,128)S(1)}, f32[3,32,128]{2,1,0:T(8,128)S(1)}, u32[]{:S(2)}, u32[]{:S(2)}) %collective-permute-start.2) | collective-permute-done | bytes 49184 | tf_op jit(solution)/shard_map/ppermute | solution.py:296
  22.6 2.4 %collective-permute-done.3 = f32[3,32,128]{2,1,0:T(8,128)S(1)} collective-permute-done((f32[3,32,128]{2,1,0:T(8,128)S(1)}, f32[3,32,128]{2,1,0:T(8,128)S(1)}, u32[]{:S(2)}, u32[]{:S(2)}) %collective-permute-start.3) | collective-permute-done | bytes 49184 | tf_op jit(solution)/shard_map/ppermute | solution.py:296
  25.0 1.2 %collective-permute-done.7 = f32[3,32,128]{2,1,0:T(8,128)S(1)} collective-permute-done((f32[3,32,128]{2,1,0:T(8,128)S(1)}, f32[3,32,128]{2,1,0:T(8,128)S(1)}, u32[]{:S(2)}, u32[]{:S(2)}) %collective-permute-start.7) | collective-permute-done | bytes 49184 | tf_op jit(solution)/shard_map/ppermute | solution.py:299
  26.2 0.1 combine.1
  26.3 0.1 collective-permute-start.8
  26.4 0.8 %collective-permute-start.9 = (f32[3,32,128]{2,1,0:T(8,128)S(1)}, f32[3,32,128]{2,1,0:T(8,128)S(1)}, u32[]{:S(2)}, u32[]{:S(2)}) collective-permute-start(f32[3,32,128]{2,1,0:T(8,128)S(1)} %bitcast.24), channel_id=1, source_target_pairs={{0,24},{4,28},{8,16},{12,20},{16,8},{20,12},{24,0},{28,4},{1,25},{... | collective-permute-start | bytes 147464 | tf_op jit(solution)/shard_map/ppermute | solution.py:296
  27.2 2.2 %collective-permute-start.10 = (f32[3,32,128]{2,1,0:T(8,128)S(1)}, f32[3,32,128]{2,1,0:T(8,128)S(1)}, u32[]{:S(2)}, u32[]{:S(2)}) collective-permute-start(f32[3,32,128]{2,1,0:T(8,128)S(1)} %bitcast.23), channel_id=1, source_target_pairs={{0,16},{4,20},{8,0},{12,4},{16,24},{20,28},{24,8},{28,12},{1,17},{... | collective-permute-start | bytes 147464 | tf_op jit(solution)/shard_map/ppermute | solution.py:296
  29.3 3.9 %collective-permute-done.8.refs_1_ = f32[3,32,128]{2,1,0:T(8,128)S(1)} collective-permute-done((f32[3,32,128]{2,1,0:T(8,128)S(1)}, f32[3,32,128]{2,1,0:T(8,128)S(1)}, u32[]{:S(2)}, u32[]{:S(2)}) %collective-permute-start.8) | collective-permute-done | bytes 49184 | tf_op jit(solution)/shard_map/ppermute | solution.py:296
  33.2 0.7 %gather.1 = f32[1,1,3,128,128]{4,3,2,1,0:T(8,128)} custom-call(f32[3,32,128]{2,1,0:T(8,128)S(1)} %bitcast.20, f32[3,32,128]{2,1,0:T(8,128)S(1)} %collective-permute-done.8.refs_1_, f32[3,32,128]{2,1,0:T(8,128)S(1)} %collective-permute-done.9.refs_2_, f32[3,32,128]{2,1,0:T(8,128)S(1)} %collective-permute-done.10.refs_3_), custom_call_target="tpu_custom_call" | custom-call | tf_op jit(solution)/shard_map/gather/pallas_call | solution.py:314
  (18 shorter events, 0.0 us)
Async XLA Ops:
  0.7 6.1 %copy-start.2 = (s32[1,12]{1,0:T(1,128)S(1)}, s32[1,12]{1,0:T(1,128)}, u32[]{:S(2)}) copy-start(s32[1,12]{1,0:T(1,128)} %cols.1) | copy-start | bytes 148
  0.7 6.1 %copy-start.3 = (s32[1,2]{1,0:T(1,128)S(1)}, s32[1,2]{1,0:T(1,128)}, u32[]{:S(2)}) copy-start(s32[1,2]{1,0:T(1,128)} %border_map.1) | copy-start | bytes 28
  3.6 3.1 %copy-start.4 = (f32[8]{0:T(128)S(1)}, f32[8]{0:T(128)}, u32[]{:S(2)}) copy-start(f32[8]{0:T(128)} %param.21) | copy-start | bytes 100
  3.6 3.1 %copy-start.5 = (f32[8]{0:T(128)S(1)}, f32[8]{0:T(128)}, u32[]{:S(2)}) copy-start(f32[8]{0:T(128)} %param.23) | copy-start | bytes 100
  3.6 3.0 %copy-start.6 = (f32[8]{0:T(128)S(1)}, f32[8]{0:T(128)}, u32[]{:S(2)}) copy-start(f32[8]{0:T(128)} %param.22) | copy-start | bytes 100
  3.6 10.3 %collective-permute-start = (f32[256,256]{1,0:T(8,128)S(1)}, f32[256,256]{1,0:T(8,128)S(1)}, u32[]{:S(2)}, u32[]{:S(2)}) collective-permute-start(f32[256,256]{1,0:T(8,128)S(1)} %get-tuple-element.27), channel_id=1, source_target_pairs={{0,1},{1,2},{2,3},{3,0},{4,5},{5,6},{6,7},{7,4},{8,9},{9,10},{10,1... | collective-permute-start | bytes 786440 | tf_op jit(solution)/shard_map/ppermute | solution.py:259
  6.7 0.7 %copy-start = (s32[1,3,2]{1,2,0:T(2,128)S(1)}, s32[1,3,2]{1,2,0:T(2,128)}, u32[]{:S(2)}) copy-start(s32[1,3,2]{1,2,0:T(2,128)} %param.20) | copy-start | bytes 76
  6.8 0.7 %copy-start.1 = (s32[1,12]{1,0:T(1,128)S(1)}, s32[1,12]{1,0:T(1,128)}, u32[]{:S(2)}) copy-start(s32[1,12]{1,0:T(1,128)} %rows.1) | copy-start | bytes 148
  14.7 4.6 %collective-permute-start.1 = (f32[3,32,128]{2,1,0:T(8,128)S(1)}, f32[3,32,128]{2,1,0:T(8,128)S(1)}, u32[]{:S(2)}, u32[]{:S(2)}) collective-permute-start(f32[3,32,128]{2,1,0:T(8,128)S(1)} %get-tuple-element.34), channel_id=1, source_target_pairs={{0,8},{4,12},{8,0},{12,4},{16,24},{20,28},{24,16},{28,20},{1,9},{5... | collective-permute-start | bytes 147464 | tf_op jit(solution)/shard_map/ppermute | solution.py:296
  16.5 6.0 %collective-permute-start.2 = (f32[3,32,128]{2,1,0:T(8,128)S(1)}, f32[3,32,128]{2,1,0:T(8,128)S(1)}, u32[]{:S(2)}, u32[]{:S(2)}) collective-permute-start(f32[3,32,128]{2,1,0:T(8,128)S(1)} %get-tuple-element.35), channel_id=1, source_target_pairs={{0,16},{4,20},{8,24},{12,28},{16,0},{20,4},{24,8},{28,12},{1,17},{... | collective-permute-start | bytes 147464 | tf_op jit(solution)/shard_map/ppermute | solution.py:296
  19.1 5.9 %collective-permute-start.3 = (f32[3,32,128]{2,1,0:T(8,128)S(1)}, f32[3,32,128]{2,1,0:T(8,128)S(1)}, u32[]{:S(2)}, u32[]{:S(2)}) collective-permute-start(f32[3,32,128]{2,1,0:T(8,128)S(1)} %get-tuple-element.36), channel_id=1, source_target_pairs={{0,24},{4,28},{8,16},{12,20},{16,8},{20,12},{24,0},{28,4},{1,25},{... | collective-permute-start | bytes 147464 | tf_op jit(solution)/shard_map/ppermute | solution.py:296
  19.1 5.9 %collective-permute-start.4 = (f32[3,32,128]{2,1,0:T(8,128)S(1)}, f32[3,32,128]{2,1,0:T(8,128)S(1)}, u32[]{:S(2)}, u32[]{:S(2)}) collective-permute-start(f32[3,32,128]{2,1,0:T(8,128)S(1)} %get-tuple-element.33), channel_id=1, source_target_pairs={{0,4},{4,0},{8,12},{12,8},{16,20},{20,16},{24,28},{28,24},{1,5},{5... | collective-permute-start | bytes 147464 | tf_op jit(solution)/shard_map/ppermute | solution.py:299
  19.3 5.7 %collective-permute-start.5 = (f32[3,32,128]{2,1,0:T(8,128)S(1)}, f32[3,32,128]{2,1,0:T(8,128)S(1)}, u32[]{:S(2)}, u32[]{:S(2)}) collective-permute-start(f32[3,32,128]{2,1,0:T(8,128)S(1)} %collective-permute-done.1), channel_id=1, source_target_pairs={{0,4},{4,0},{8,12},{12,8},{16,20},{20,16},{24,28},{28,24},{1,5},{5... | collective-permute-start | bytes 147464 | tf_op jit(solution)/shard_map/ppermute | solution.py:299
  22.6 2.5 %collective-permute-start.6 = (f32[3,32,128]{2,1,0:T(8,128)S(1)}, f32[3,32,128]{2,1,0:T(8,128)S(1)}, u32[]{:S(2)}, u32[]{:S(2)}) collective-permute-start(f32[3,32,128]{2,1,0:T(8,128)S(1)} %collective-permute-done.2), channel_id=1, source_target_pairs={{0,4},{4,0},{8,12},{12,8},{16,20},{20,16},{24,28},{28,24},{1,5},{5... | collective-permute-start | bytes 147464 | tf_op jit(solution)/shard_map/ppermute | solution.py:299
  25.0 1.2 %collective-permute-start.7 = (f32[3,32,128]{2,1,0:T(8,128)S(1)}, f32[3,32,128]{2,1,0:T(8,128)S(1)}, u32[]{:S(2)}, u32[]{:S(2)}) collective-permute-start(f32[3,32,128]{2,1,0:T(8,128)S(1)} %collective-permute-done.3), channel_id=1, source_target_pairs={{0,4},{4,0},{8,12},{12,8},{16,20},{20,16},{24,28},{28,24},{1,5},{5... | collective-permute-start | bytes 147464 | tf_op jit(solution)/shard_map/ppermute | solution.py:299
  26.3 6.9 %collective-permute-start.8 = (f32[3,32,128]{2,1,0:T(8,128)S(1)}, f32[3,32,128]{2,1,0:T(8,128)S(1)}, u32[]{:S(2)}, u32[]{:S(2)}) collective-permute-start(f32[3,32,128]{2,1,0:T(8,128)S(1)} %bitcast.25), channel_id=1, source_target_pairs={{0,8},{4,12},{8,24},{12,28},{16,0},{20,4},{24,16},{28,20},{1,9},{5... | collective-permute-start | bytes 147464 | tf_op jit(solution)/shard_map/ppermute | solution.py:296
  26.4 6.8 %collective-permute-start.9 = (f32[3,32,128]{2,1,0:T(8,128)S(1)}, f32[3,32,128]{2,1,0:T(8,128)S(1)}, u32[]{:S(2)}, u32[]{:S(2)}) collective-permute-start(f32[3,32,128]{2,1,0:T(8,128)S(1)} %bitcast.24), channel_id=1, source_target_pairs={{0,24},{4,28},{8,16},{12,20},{16,8},{20,12},{24,0},{28,4},{1,25},{... | collective-permute-start | bytes 147464 | tf_op jit(solution)/shard_map/ppermute | solution.py:296
  27.2 6.1 %collective-permute-start.10 = (f32[3,32,128]{2,1,0:T(8,128)S(1)}, f32[3,32,128]{2,1,0:T(8,128)S(1)}, u32[]{:S(2)}, u32[]{:S(2)}) collective-permute-start(f32[3,32,128]{2,1,0:T(8,128)S(1)} %bitcast.23), channel_id=1, source_target_pairs={{0,16},{4,20},{8,0},{12,4},{16,24},{20,28},{24,8},{28,12},{1,17},{... | collective-permute-start | bytes 147464 | tf_op jit(solution)/shard_map/ppermute | solution.py:296

commit v4 on v3

--- a/solution.py
+++ b/solution.py
@@ -62,6 +62,14 @@
         lax.dot_general, dimension_numbers=dims, preferred_element_type=jnp.float32
     )
     return mm(a[0], b[0]) + (mm(a[0], b[1]) + mm(a[1], b[0]))
+
+
+def dot3_halves(a, b, dims):
+    half = a[0].shape[0] // 2
+    return jnp.concatenate(
+        [dot3((a[0][at], a[1][at]), b, dims) for at in (slice(0, half), slice(half, 2 * half))],
+        axis=0,
+    )
 
 
 def place_fit(rows, cols, count, blocks, high_ref, low_ref, first, last):
@@ -117,7 +125,7 @@
         high_out[at], low_out[at] = product
         term = dot3((fit_high[:, at], fit_low[:, at]), product, NN)
         left = term if left is None else left + term
-    out[...] = dot3(split(left), (fit_high[...], fit_low[...]), NT)
+    out[...] = dot3_halves(split(left), (fit_high[...], fit_low[...]), NT)
 
 
 def own_kernel(
@@ -165,7 +173,7 @@
     total, outs = refs[-1], refs[:-1]
     chip = lax.axis_index("tm") // CORES
     count_pairs, order, _ = own.shape
-    left = dot3((row_high[...], row_low[...]), split(border[...]), NN)
+    left = dot3_halves((row_high[...], row_low[...]), split(border[...]), NN)
     for p in range(count_pairs):
         here = slice(p * order, (p + 1) * order)
         total[p] = own[p] + dot3(split(left[here]), (col_high[here], col_low[here]), NT)

time: 34.1 us -> 33.7 us (0.988)
  Pallas kernels: 8.32 us -> 7.94 us
where the time goes in v4:
time: 33.7 us; the launch traced here: 33.5 us
  waiting for transfers between devices  13.2 us (39%)
  starting transfers between devices  10.8 us (32%)
  Pallas kernels  7.94 us (24%)
  between operations  0.78 us (2%)
  local copies, waits for them, and re-layouts  0.68 us (2%)
    ppermute x6, waiting for transfers between devices, across(): return lax.ppermute(x, 'tm', pairs_of)  9.39 us
    ppermute x6, starting transfers between devices, across(): return lax.ppermute(x, 'tm', pairs_of)  7.42 us
    pallas_call x1, Pallas kernels, on_device(): pl.pallas_call(own_kernel, out_shape=(pltpu.VMEM((pairs, order, order), f...  3.84 us
    ppermute x1, starting transfers between devices, on_device(): lax.ppermute(border, 'sec', [(i, (i + 1) % sections) for i in range(secti...  3.01 us
    pallas_call x1, Pallas kernels, on_device(): pl.pallas_call(border_kernel, out_shape=(pltpu.VMEM((edge_rows, edge_rows...  2.69 us
    ppermute x1, waiting for transfers between devices, on_device(): lax.ppermute(border, 'sec', [(i, (i + 1) % sections) for i in range(secti...  2.61 us
    ppermute x4, waiting for transfers between devices, swap(): return lax.ppermute(x, 'tm', [(i, i ^ 1) for i in range(devices)])  1.22 us
    pallas_call x1, Pallas kernels, on_device(): pl.pallas_call(gather_kernel, out_shape=jax.ShapeDtypeStruct((1, 1, pairs...  0.7 us
  transfers between devices with their start and end apart: 11, of which 6 were waited for; matrix products, arithmetic and copies ran while one was open for 0% of the time, Pallas kernels for 11%

profile of v4, /device:TPU:0, one launch (start us, length us, event | category | flops | bytes accessed | tf_op | source)
XLA Modules:
  0.0 33.5 jit_solution(11772375177990347947)
XLA Ops:
  0.7 2.7 %border.1 = (f32[256,256]{1,0:T(8,128)S(1)}, bf16[512,512]{1,0:T(8,128)(2,1)S(1)}, bf16[512,512]{1,0:T(8,128)(2,1)S(1)}, f32[12,128,128]{2,1,0:T(8,128)S(1)}) custom-call(s32[1]{0:T(128)S(6)} %copy.13.count, s32[1,12]{1,0:T(1,128)} %rows.1, s32[1,12]{1,0:T(1,128)} %cols.1, f32[1,1,512,512]{3,2,1,0:T(8,128)} %occ.1, f32[1,1,512,512]{3,2,1,0:T(8,128)} %virt.1, ...), custom_call_target="tpu_custom_call" | custom-call | flops 1000000000 | bytes 3145728 | tf_op jit(solution)/shard_map/border/pallas_call | solution.py:245
  3.4 0.0 copy-start.4
  3.4 0.0 copy-start.5
  3.4 3.0 %collective-permute-start = (f32[256,256]{1,0:T(8,128)S(1)}, f32[256,256]{1,0:T(8,128)S(1)}, u32[]{:S(2)}, u32[]{:S(2)}) collective-permute-start(f32[256,256]{1,0:T(8,128)S(1)} %get-tuple-element.27), channel_id=1, source_target_pairs={{0,1},{1,2},{2,3},{3,0},{4,5},{5,6},{6,7},{7,4},{8,9},{9,10},{10,1... | collective-permute-start | bytes 786440 | tf_op jit(solution)/shard_map/ppermute | solution.py:267
  6.4 0.1 cosine_multiply_fusion.cosine
  6.5 0.0 copy-start
  6.6 0.6 %copy-done = s32[1,3,2]{1,2,0:T(2,128)S(1)} copy-done((s32[1,3,2]{1,2,0:T(2,128)S(1)}, s32[1,3,2]{1,2,0:T(2,128)}, u32[]{:S(2)}) %copy-start) | copy-done | bytes 48
  7.2 3.8 %own.1 = (f32[3,128,128]{2,1,0:T(8,128)S(1)}, bf16[384,256]{1,0:T(8,128)(2,1)S(1)}, bf16[384,256]{1,0:T(8,128)(2,1)S(1)}, bf16[384,256]{1,0:T(8,128)(2,1)S(1)}, ...) custom-call(s32[1,12]{1,0:T(1,128)S(1)} %copy-done.1, s32[1,12]{1,0:T(1,128)S(1)} %copy-done.2, ...), custom_call_target="tpu_custom_call" | custom-call | flops 2000000000 | bytes 5242880 | tf_op jit(solution)/shard_map/own/pallas_call | solution.py:270
  11.1 2.6 %collective-permute-done.border = f32[256,256]{1,0:T(8,128)S(1)} collective-permute-done((f32[256,256]{1,0:T(8,128)S(1)}, f32[256,256]{1,0:T(8,128)S(1)}, u32[]{:S(2)}, u32[]{:S(2)}) %collective-permute-start) | collective-permute-done | bytes 262176 | tf_op jit(solution)/shard_map/ppermute | solution.py:267
  13.7 0.6 %join.1 = (f32[3,32,128]{2,1,0:T(8,128)S(1)}, f32[3,32,128]{2,1,0:T(8,128)S(1)}, f32[3,32,128]{2,1,0:T(8,128)S(1)}, f32[3,32,128]{2,1,0:T(8,128)S(1)}) custom-call(f32[256,256]{1,0:T(8,128)S(1)} %collective-permute-done.border, f32[3,128,128]{2,1,0:T(8,128)S(1)} %get-tuple-element.28.own, bf16[384,256]{1,0:T(8,128)(2,1)S(1)} %get-tuple-element.29.row_high, ...), custom_call_target="tpu_custom_call" | custom-call | tf_op jit(solution)/shard_map/join/pallas_call | solution.py:290
  14.3 1.8 %collective-permute-start.1 = (f32[3,32,128]{2,1,0:T(8,128)S(1)}, f32[3,32,128]{2,1,0:T(8,128)S(1)}, u32[]{:S(2)}, u32[]{:S(2)}) collective-permute-start(f32[3,32,128]{2,1,0:T(8,128)S(1)} %get-tuple-element.34), channel_id=1, source_target_pairs={{0,8},{4,12},{8,0},{12,4},{16,24},{20,28},{24,16},{28,20},{1,9},{5... | collective-permute-start | bytes 147464 | tf_op jit(solution)/shard_map/ppermute | solution.py:304
  16.1 2.6 %collective-permute-start.2 = (f32[3,32,128]{2,1,0:T(8,128)S(1)}, f32[3,32,128]{2,1,0:T(8,128)S(1)}, u32[]{:S(2)}, u32[]{:S(2)}) collective-permute-start(f32[3,32,128]{2,1,0:T(8,128)S(1)} %get-tuple-element.35), channel_id=1, source_target_pairs={{0,16},{4,20},{8,24},{12,28},{16,0},{20,4},{24,8},{28,12},{1,17},{... | collective-permute-start | bytes 147464 | tf_op jit(solution)/shard_map/ppermute | solution.py:304
  18.7 0.0 collective-permute-start.3
  18.7 0.1 collective-permute-done.1
  18.9 0.4 %collective-permute-start.5 = (f32[3,32,128]{2,1,0:T(8,128)S(1)}, f32[3,32,128]{2,1,0:T(8,128)S(1)}, u32[]{:S(2)}, u32[]{:S(2)}) collective-permute-start(f32[3,32,128]{2,1,0:T(8,128)S(1)} %collective-permute-done.1), channel_id=1, source_target_pairs={{0,4},{4,0},{8,12},{12,8},{16,20},{20,16},{24,28},{28,24},{1,5},{5... | collective-permute-start | bytes 147464 | tf_op jit(solution)/shard_map/ppermute | solution.py:307
  19.3 2.9 %collective-permute-done.2 = f32[3,32,128]{2,1,0:T(8,128)S(1)} collective-permute-done((f32[3,32,128]{2,1,0:T(8,128)S(1)}, f32[3,32,128]{2,1,0:T(8,128)S(1)}, u32[]{:S(2)}, u32[]{:S(2)}) %collective-permute-start.2) | collective-permute-done | bytes 49184 | tf_op jit(solution)/shard_map/ppermute | solution.py:304
  22.2 2.4 %collective-permute-done.3 = f32[3,32,128]{2,1,0:T(8,128)S(1)} collective-permute-done((f32[3,32,128]{2,1,0:T(8,128)S(1)}, f32[3,32,128]{2,1,0:T(8,128)S(1)}, u32[]{:S(2)}, u32[]{:S(2)}) %collective-permute-start.3) | collective-permute-done | bytes 49184 | tf_op jit(solution)/shard_map/ppermute | solution.py:304
  24.6 1.2 %collective-permute-done.7 = f32[3,32,128]{2,1,0:T(8,128)S(1)} collective-permute-done((f32[3,32,128]{2,1,0:T(8,128)S(1)}, f32[3,32,128]{2,1,0:T(8,128)S(1)}, u32[]{:S(2)}, u32[]{:S(2)}) %collective-permute-start.7) | collective-permute-done | bytes 49184 | tf_op jit(solution)/shard_map/ppermute | solution.py:307
  25.8 0.1 combine.1
  26.0 0.1 collective-permute-start.8
  26.0 0.7 %collective-permute-start.9 = (f32[3,32,128]{2,1,0:T(8,128)S(1)}, f32[3,32,128]{2,1,0:T(8,128)S(1)}, u32[]{:S(2)}, u32[]{:S(2)}) collective-permute-start(f32[3,32,128]{2,1,0:T(8,128)S(1)} %bitcast.24), channel_id=1, source_target_pairs={{0,24},{4,28},{8,16},{12,20},{16,8},{20,12},{24,0},{28,4},{1,25},{... | collective-permute-start | bytes 147464 | tf_op jit(solution)/shard_map/ppermute | solution.py:304
  26.8 2.2 %collective-permute-start.10 = (f32[3,32,128]{2,1,0:T(8,128)S(1)}, f32[3,32,128]{2,1,0:T(8,128)S(1)}, u32[]{:S(2)}, u32[]{:S(2)}) collective-permute-start(f32[3,32,128]{2,1,0:T(8,128)S(1)} %bitcast.23), channel_id=1, source_target_pairs={{0,16},{4,20},{8,0},{12,4},{16,24},{20,28},{24,8},{28,12},{1,17},{... | collective-permute-start | bytes 147464 | tf_op jit(solution)/shard_map/ppermute | solution.py:304
  28.9 3.9 %collective-permute-done.8.refs_1_ = f32[3,32,128]{2,1,0:T(8,128)S(1)} collective-permute-done((f32[3,32,128]{2,1,0:T(8,128)S(1)}, f32[3,32,128]{2,1,0:T(8,128)S(1)}, u32[]{:S(2)}, u32[]{:S(2)}) %collective-permute-start.8) | collective-permute-done | bytes 49184 | tf_op jit(solution)/shard_map/ppermute | solution.py:304
  32.8 0.7 %gather.1 = f32[1,1,3,128,128]{4,3,2,1,0:T(8,128)} custom-call(f32[3,32,128]{2,1,0:T(8,128)S(1)} %bitcast.20, f32[3,32,128]{2,1,0:T(8,128)S(1)} %collective-permute-done.8.refs_1_, f32[3,32,128]{2,1,0:T(8,128)S(1)} %collective-permute-done.9.refs_2_, f32[3,32,128]{2,1,0:T(8,128)S(1)} %collective-permute-done.10.refs_3_), custom_call_target="tpu_custom_call" | custom-call | tf_op jit(solution)/shard_map/gather/pallas_call | solution.py:322
  (18 shorter events, 0.0 us)
Async XLA Ops:
  0.7 5.9 %copy-start.2 = (s32[1,12]{1,0:T(1,128)S(1)}, s32[1,12]{1,0:T(1,128)}, u32[]{:S(2)}) copy-start(s32[1,12]{1,0:T(1,128)} %cols.1) | copy-start | bytes 148
  0.7 5.9 %copy-start.3 = (s32[1,2]{1,0:T(1,128)S(1)}, s32[1,2]{1,0:T(1,128)}, u32[]{:S(2)}) copy-start(s32[1,2]{1,0:T(1,128)} %border_map.1) | copy-start | bytes 28
  3.4 3.1 %copy-start.4 = (f32[8]{0:T(128)S(1)}, f32[8]{0:T(128)}, u32[]{:S(2)}) copy-start(f32[8]{0:T(128)} %param.21) | copy-start | bytes 100
  3.4 3.0 %copy-start.5 = (f32[8]{0:T(128)S(1)}, f32[8]{0:T(128)}, u32[]{:S(2)}) copy-start(f32[8]{0:T(128)} %param.23) | copy-start | bytes 100
  3.4 3.0 %copy-start.6 = (f32[8]{0:T(128)S(1)}, f32[8]{0:T(128)}, u32[]{:S(2)}) copy-start(f32[8]{0:T(128)} %param.22) | copy-start | bytes 100
  3.4 10.3 %collective-permute-start = (f32[256,256]{1,0:T(8,128)S(1)}, f32[256,256]{1,0:T(8,128)S(1)}, u32[]{:S(2)}, u32[]{:S(2)}) collective-permute-start(f32[256,256]{1,0:T(8,128)S(1)} %get-tuple-element.27), channel_id=1, source_target_pairs={{0,1},{1,2},{2,3},{3,0},{4,5},{5,6},{6,7},{7,4},{8,9},{9,10},{10,1... | collective-permute-start | bytes 786440 | tf_op jit(solution)/shard_map/ppermute | solution.py:267
  6.5 0.7 %copy-start = (s32[1,3,2]{1,2,0:T(2,128)S(1)}, s32[1,3,2]{1,2,0:T(2,128)}, u32[]{:S(2)}) copy-start(s32[1,3,2]{1,2,0:T(2,128)} %param.20) | copy-start | bytes 76
  6.6 0.7 %copy-start.1 = (s32[1,12]{1,0:T(1,128)S(1)}, s32[1,12]{1,0:T(1,128)}, u32[]{:S(2)}) copy-start(s32[1,12]{1,0:T(1,128)} %rows.1) | copy-start | bytes 148
  14.3 4.6 %collective-permute-start.1 = (f32[3,32,128]{2,1,0:T(8,128)S(1)}, f32[3,32,128]{2,1,0:T(8,128)S(1)}, u32[]{:S(2)}, u32[]{:S(2)}) collective-permute-start(f32[3,32,128]{2,1,0:T(8,128)S(1)} %get-tuple-element.34), channel_id=1, source_target_pairs={{0,8},{4,12},{8,0},{12,4},{16,24},{20,28},{24,16},{28,20},{1,9},{5... | collective-permute-start | bytes 147464 | tf_op jit(solution)/shard_map/ppermute | solution.py:304
  16.1 6.0 %collective-permute-start.2 = (f32[3,32,128]{2,1,0:T(8,128)S(1)}, f32[3,32,128]{2,1,0:T(8,128)S(1)}, u32[]{:S(2)}, u32[]{:S(2)}) collective-permute-start(f32[3,32,128]{2,1,0:T(8,128)S(1)} %get-tuple-element.35), channel_id=1, source_target_pairs={{0,16},{4,20},{8,24},{12,28},{16,0},{20,4},{24,8},{28,12},{1,17},{... | collective-permute-start | bytes 147464 | tf_op jit(solution)/shard_map/ppermute | solution.py:304
  18.7 5.9 %collective-permute-start.3 = (f32[3,32,128]{2,1,0:T(8,128)S(1)}, f32[3,32,128]{2,1,0:T(8,128)S(1)}, u32[]{:S(2)}, u32[]{:S(2)}) collective-permute-start(f32[3,32,128]{2,1,0:T(8,128)S(1)} %get-tuple-element.36), channel_id=1, source_target_pairs={{0,24},{4,28},{8,16},{12,20},{16,8},{20,12},{24,0},{28,4},{1,25},{... | collective-permute-start | bytes 147464 | tf_op jit(solution)/shard_map/ppermute | solution.py:304
  18.7 5.9 %collective-permute-start.4 = (f32[3,32,128]{2,1,0:T(8,128)S(1)}, f32[3,32,128]{2,1,0:T(8,128)S(1)}, u32[]{:S(2)}, u32[]{:S(2)}) collective-permute-start(f32[3,32,128]{2,1,0:T(8,128)S(1)} %get-tuple-element.33), channel_id=1, source_target_pairs={{0,4},{4,0},{8,12},{12,8},{16,20},{20,16},{24,28},{28,24},{1,5},{5... | collective-permute-start | bytes 147464 | tf_op jit(solution)/shard_map/ppermute | solution.py:307
  18.9 5.7 %collective-permute-start.5 = (f32[3,32,128]{2,1,0:T(8,128)S(1)}, f32[3,32,128]{2,1,0:T(8,128)S(1)}, u32[]{:S(2)}, u32[]{:S(2)}) collective-permute-start(f32[3,32,128]{2,1,0:T(8,128)S(1)} %collective-permute-done.1), channel_id=1, source_target_pairs={{0,4},{4,0},{8,12},{12,8},{16,20},{20,16},{24,28},{28,24},{1,5},{5... | collective-permute-start | bytes 147464 | tf_op jit(solution)/shard_map/ppermute | solution.py:307
  22.2 2.5 %collective-permute-start.6 = (f32[3,32,128]{2,1,0:T(8,128)S(1)}, f32[3,32,128]{2,1,0:T(8,128)S(1)}, u32[]{:S(2)}, u32[]{:S(2)}) collective-permute-start(f32[3,32,128]{2,1,0:T(8,128)S(1)} %collective-permute-done.2), channel_id=1, source_target_pairs={{0,4},{4,0},{8,12},{12,8},{16,20},{20,16},{24,28},{28,24},{1,5},{5... | collective-permute-start | bytes 147464 | tf_op jit(solution)/shard_map/ppermute | solution.py:307
  24.6 1.2 %collective-permute-start.7 = (f32[3,32,128]{2,1,0:T(8,128)S(1)}, f32[3,32,128]{2,1,0:T(8,128)S(1)}, u32[]{:S(2)}, u32[]{:S(2)}) collective-permute-start(f32[3,32,128]{2,1,0:T(8,128)S(1)} %collective-permute-done.3), channel_id=1, source_target_pairs={{0,4},{4,0},{8,12},{12,8},{16,20},{20,16},{24,28},{28,24},{1,5},{5... | collective-permute-start | bytes 147464 | tf_op jit(solution)/shard_map/ppermute | solution.py:307
  26.0 6.9 %collective-permute-start.8 = (f32[3,32,128]{2,1,0:T(8,128)S(1)}, f32[3,32,128]{2,1,0:T(8,128)S(1)}, u32[]{:S(2)}, u32[]{:S(2)}) collective-permute-start(f32[3,32,128]{2,1,0:T(8,128)S(1)} %bitcast.25), channel_id=1, source_target_pairs={{0,8},{4,12},{8,24},{12,28},{16,0},{20,4},{24,16},{28,20},{1,9},{5... | collective-permute-start | bytes 147464 | tf_op jit(solution)/shard_map/ppermute | solution.py:304
  26.0 6.8 %collective-permute-start.9 = (f32[3,32,128]{2,1,0:T(8,128)S(1)}, f32[3,32,128]{2,1,0:T(8,128)S(1)}, u32[]{:S(2)}, u32[]{:S(2)}) collective-permute-start(f32[3,32,128]{2,1,0:T(8,128)S(1)} %bitcast.24), channel_id=1, source_target_pairs={{0,24},{4,28},{8,16},{12,20},{16,8},{20,12},{24,0},{28,4},{1,25},{... | collective-permute-start | bytes 147464 | tf_op jit(solution)/shard_map/ppermute | solution.py:304
  26.8 6.1 %collective-permute-start.10 = (f32[3,32,128]{2,1,0:T(8,128)S(1)}, f32[3,32,128]{2,1,0:T(8,128)S(1)}, u32[]{:S(2)}, u32[]{:S(2)}) collective-permute-start(f32[3,32,128]{2,1,0:T(8,128)S(1)} %bitcast.23), channel_id=1, source_target_pairs={{0,16},{4,20},{8,0},{12,4},{16,24},{20,28},{24,8},{28,12},{1,17},{... | collective-permute-start | bytes 147464 | tf_op jit(solution)/shard_map/ppermute | solution.py:304

commit v5 on v4

--- a/solution.py
+++ b/solution.py
@@ -19,37 +19,9 @@
 HBM = pl.BlockSpec(memory_space=pltpu.HBM)
 CHUNKS = 2
 VMEM_LIMIT = 16 << 20
-
-
-ROUTES = ("xor", "ring")
-
-
+PARTNERS = 2
 NN = (((1,), (0,)), ((), ()))
 NT = (((1,), (1,)), ((), ()))
-
-
-def pick(flag, yes, no):
-    return (yes if flag else no) if isinstance(flag, bool) else jnp.where(flag, yes, no)
-
-
-def ring_place(chip, chips):
-    return pick(chip % 2 == 1, (chip + 1) // 2, (chips - chip // 2) % chips)
-
-
-def ring_chip(place, chips):
-    return pick(place == 0, 0, pick(place <= chips // 2, 2 * place - 1, 2 * (chips - place)))
-
-
-def to_chip(phase, chip, step, chips):
-    if ROUTES[phase] == "xor":
-        return chip ^ step
-    return ring_chip((ring_place(chip, chips) + step) % chips, chips)
-
-
-def from_chip(phase, chip, step, chips):
-    if ROUTES[phase] == "xor":
-        return chip ^ step
-    return ring_chip((ring_place(chip, chips) + chips - step) % chips, chips)
 
 
 def split(x):
@@ -160,11 +132,11 @@
         )
     index = lax.axis_index("tm")
     chip, core = index // CORES, index % CORES
-    chips = weight.shape[0]
-    for k in range(chips):
-        freq = to_chip(1, chip, k, chips) * CORES + core
+    chips = weight.shape[1]
+    for k in range(PARTNERS):
+        freq = (chip ^ k) * CORES + core
         for j in range(chips):
-            at = from_chip(0, chip, j, chips) * CORES
+            at = (chip ^ j) * CORES
             weight[k, j, 0] = jnp.full(weight.shape[3:], cosine[freq, at + core])
             weight[k, j, 1] = jnp.full(weight.shape[3:], cosine[freq, at + 1 - core])
 
@@ -179,14 +151,14 @@
         total[p] = own[p] + dot3(split(left[here]), (col_high[here], col_low[here]), NT)
     share = outs[0].shape[1]
     for k, out in enumerate(outs):
-        at = pl.ds(pl.multiple_of(to_chip(0, chip, k, len(outs)) * share, share), share)
+        at = pl.ds(pl.multiple_of(((chip ^ k) % PARTNERS) * share, share), share)
         out[...] = total[:, at, :]
 
 
 def combine_kernel(weight, *refs):
-    chips = len(refs) // 3
+    chips = weight.shape[1]
     mine, other, outs = refs[:chips], refs[chips : 2 * chips], refs[2 * chips :]
-    for k in range(chips):
+    for k in range(PARTNERS):
         total = jnp.zeros(outs[k].shape, jnp.float32)
         for j in range(chips):
             total += weight[k, j, 0] * mine[j][...]
@@ -200,7 +172,7 @@
     copies = []
     for k, part in enumerate(parts):
         share = part.shape[1]
-        at = pl.ds(pl.multiple_of(from_chip(1, chip, k, len(parts)) * share, share), share)
+        at = pl.ds(pl.multiple_of(((chip ^ k) % PARTNERS) * share, share), share)
         copies.append(pltpu.make_async_copy(part, out.at[0, 0, :, at, :], sems.at[k]))
         copies[k].start()
     for copy in copies:
@@ -236,7 +208,7 @@
     pairs = pair_list.shape[1]
     devices = lax.axis_size("tm")
     chips = devices // CORES
-    share = order // chips
+    share = order // PARTNERS
     f32, bf16 = jnp.float32, jnp.bfloat16
     cosine = time_weights[None, :] * jnp.cos(freqs[:, None] * times[None, :])
     pair_rows_cols = jnp.swapaxes(pair_list, 1, 2)
@@ -271,7 +243,7 @@
         own_kernel,
         out_shape=(pltpu.VMEM((pairs, order, order), f32),)
         + (edge,) * 4
-        + (pltpu.VMEM((chips, chips, CORES, SUBLANES, order), f32),),
+        + (pltpu.VMEM((PARTNERS, chips, CORES, SUBLANES, order), f32),),
         in_specs=[SMEM] * 6 + [VMEM] * 4,
         out_specs=(VMEM,) * 6,
         scratch_shapes=[pltpu.VMEM((own_rows, points), bf16)] * 4
@@ -289,42 +261,42 @@
     part = pltpu.VMEM((pairs, share, order), f32)
     parts = pl.pallas_call(
         join_kernel,
-        out_shape=(part,) * chips,
+        out_shape=(part,) * PARTNERS,
         in_specs=[VMEM] * 6,
-        out_specs=(VMEM,) * chips,
+        out_specs=(VMEM,) * PARTNERS,
         scratch_shapes=[pltpu.VMEM((pairs, order, order), f32)],
         compiler_params=limit,
         name="join",
     )(*map(in_vmem, (border, own, row_high, row_low, col_high, col_low)))
 
-    def across(x, k, phase):
+    def across(x, k):
         pairs_of = [
-            (i, to_chip(phase, i // CORES, k, chips) * CORES + i % CORES) for i in range(devices)
+            (i, i ^ (CORES * k)) for i in range(devices)
         ]
         return lax.ppermute(x, "tm", pairs_of)
 
     def swap(x):
         return lax.ppermute(x, "tm", [(i, i ^ 1) for i in range(devices)])
 
-    mine = [parts[0]] + [across(parts[k], k, 0) for k in range(1, chips)]
+    mine = [parts[0]] + [across(parts[k % PARTNERS], k) for k in range(1, chips)]
     other = [swap(x) for x in mine]
     tiles = pltpu.VMEM((pairs * share // SUBLANES, SUBLANES, order), f32)
     parts = pl.pallas_call(
         combine_kernel,
-        out_shape=(tiles,) * chips,
+        out_shape=(tiles,) * PARTNERS,
         in_specs=[VMEM] * (2 * chips + 1),
-        out_specs=(VMEM,) * chips,
+        out_specs=(VMEM,) * PARTNERS,
         compiler_params=limit,
         name="combine",
     )(*(in_vmem(x.reshape(tiles.shape) if x.ndim == 3 else x) for x in (weight, *mine, *other)))
     parts = [x.reshape(part.shape) for x in parts]
-    parts = [parts[0]] + [across(parts[k], k, 1) for k in range(1, chips)]
+    parts = [parts[0]] + [across(parts[k], k) for k in range(1, PARTNERS)]
     return pl.pallas_call(
         gather_kernel,
         out_shape=jax.ShapeDtypeStruct((1, 1, pairs, order, order), f32),
-        in_specs=[VMEM] * chips,
+        in_specs=[VMEM] * PARTNERS,
         out_specs=ANY,
-        scratch_shapes=[pltpu.SemaphoreType.DMA((chips,))],
+        scratch_shapes=[pltpu.SemaphoreType.DMA((PARTNERS,))],
         compiler_params=limit,
         name="gather",
     )(*map(in_vmem, parts))

time: 33.7 us -> 32.8 us (0.973)
  starting transfers between devices: 10.8 us -> 8.09 us
  waiting for transfers between devices: 13.2 us -> 15 us
    ppermute x6 -> x4, starting transfers between devices: 7.42 us -> 5.07 us  [across(): return lax.ppermute(x, 'tm', pairs_of)]
    ppermute x6 -> x4, waiting for transfers between devices: 9.39 us -> 11.1 us  [across(): return lax.ppermute(x, 'tm', pairs_of)]
    ppermute x4, starting transfers between devices: 0.37 us -> 0.01 us  [swap(): return lax.ppermute(x, 'tm', [(i, i ^ 1) for i in range(devices)])]
  transfers between devices with their start and end apart: 11 -> 9, of which waited for: 6 -> 7; matrix products, arithmetic and copies ran while one was open for 0% -> 0% of each run, Pallas kernels for 11% -> 12%
where the time goes in v5:
time: 32.8 us; the launch traced here: 32.6 us
  waiting for transfers between devices  15 us (46%)
  starting transfers between devices  8.09 us (25%)
  Pallas kernels  7.9 us (24%)
  between operations  0.76 us (2%)
  local copies, waits for them, and re-layouts  0.68 us (2%)
    ppermute x4, waiting for transfers between devices, across(): return lax.ppermute(x, 'tm', pairs_of)  11.1 us
    ppermute x4, starting transfers between devices, across(): return lax.ppermute(x, 'tm', pairs_of)  5.07 us
    pallas_call x1, Pallas kernels, on_device(): pl.pallas_call(own_kernel, out_shape=(pltpu.VMEM((pairs, order, order), f...  3.81 us
    ppermute x1, starting transfers between devices, on_device(): lax.ppermute(border, 'sec', [(i, (i + 1) % sections) for i in range(secti...  3.01 us
    pallas_call x1, Pallas kernels, on_device(): pl.pallas_call(border_kernel, out_shape=(pltpu.VMEM((edge_rows, edge_rows...  2.69 us
    ppermute x1, waiting for transfers between devices, on_device(): lax.ppermute(border, 'sec', [(i, (i + 1) % sections) for i in range(secti...  2.64 us
    ppermute x4, waiting for transfers between devices, swap(): return lax.ppermute(x, 'tm', [(i, i ^ 1) for i in range(devices)])  1.29 us
    pallas_call x1, Pallas kernels, on_device(): pl.pallas_call(gather_kernel, out_shape=jax.ShapeDtypeStruct((1, 1, pairs...  0.69 us
  transfers between devices with their start and end apart: 9, of which 7 were waited for; matrix products, arithmetic and copies ran while one was open for 0% of the time, Pallas kernels for 12%

profile of v5, /device:TPU:0, one launch (start us, length us, event | category | flops | bytes accessed | tf_op | source)
XLA Modules:
  0.0 32.6 jit_solution(18412564642837964434)
XLA Ops:
  0.7 2.7 %border.1 = (f32[256,256]{1,0:T(8,128)S(1)}, bf16[512,512]{1,0:T(8,128)(2,1)S(1)}, bf16[512,512]{1,0:T(8,128)(2,1)S(1)}, f32[12,128,128]{2,1,0:T(8,128)S(1)}) custom-call(s32[1]{0:T(128)S(6)} %copy.13.count, s32[1,12]{1,0:T(1,128)} %rows.1, s32[1,12]{1,0:T(1,128)} %cols.1, f32[1,1,512,512]{3,2,1,0:T(8,128)} %occ.1, f32[1,1,512,512]{3,2,1,0:T(8,128)} %virt.1, ...), custom_call_target="tpu_custom_call" | custom-call | flops 1000000000 | bytes 3145728 | tf_op jit(solution)/shard_map/border/pallas_call | solution.py:217
  3.4 0.0 copy-start.4
  3.4 0.0 copy-start.5
  3.4 0.0 copy-start.6
  3.4 3.0 %collective-permute-start = (f32[256,256]{1,0:T(8,128)S(1)}, f32[256,256]{1,0:T(8,128)S(1)}, u32[]{:S(2)}, u32[]{:S(2)}) collective-permute-start(f32[256,256]{1,0:T(8,128)S(1)} %get-tuple-element.23), channel_id=1, source_target_pairs={{0,1},{1,2},{2,3},{3,0},{4,5},{5,6},{6,7},{7,4},{8,9},{9,10},{10,1... | collective-permute-start | bytes 786440 | tf_op jit(solution)/shard_map/ppermute | solution.py:239
  6.4 0.1 cosine_multiply_fusion.cosine
  6.5 0.0 copy-start
  6.6 0.0 copy-start.1
  6.6 0.6 %copy-done = s32[1,3,2]{1,2,0:T(2,128)S(1)} copy-done((s32[1,3,2]{1,2,0:T(2,128)S(1)}, s32[1,3,2]{1,2,0:T(2,128)}, u32[]{:S(2)}) %copy-start) | copy-done | bytes 48
  7.2 3.8 %own.1 = (f32[3,128,128]{2,1,0:T(8,128)S(1)}, bf16[384,256]{1,0:T(8,128)(2,1)S(1)}, bf16[384,256]{1,0:T(8,128)(2,1)S(1)}, bf16[384,256]{1,0:T(8,128)(2,1)S(1)}, ...) custom-call(s32[1,12]{1,0:T(1,128)S(1)} %copy-done.1, s32[1,12]{1,0:T(1,128)S(1)} %copy-done.2, ...), custom_call_target="tpu_custom_call" | custom-call | flops 2000000000 | bytes 5242880 | tf_op jit(solution)/shard_map/own/pallas_call | solution.py:242
  11.0 2.6 %collective-permute-done.border = f32[256,256]{1,0:T(8,128)S(1)} collective-permute-done((f32[256,256]{1,0:T(8,128)S(1)}, f32[256,256]{1,0:T(8,128)S(1)}, u32[]{:S(2)}, u32[]{:S(2)}) %collective-permute-start) | collective-permute-done | bytes 262176 | tf_op jit(solution)/shard_map/ppermute | solution.py:239
  13.7 0.6 %join.1 = (f32[3,64,128]{2,1,0:T(8,128)S(1)}, f32[3,64,128]{2,1,0:T(8,128)S(1)}) custom-call(f32[256,256]{1,0:T(8,128)S(1)} %collective-permute-done.border, f32[3,128,128]{2,1,0:T(8,128)S(1)} %get-tuple-element.24.own, bf16[384,256]{1,0:T(8,128)(2,1)S(1)} %get-tuple-element.25.row_high, bf16[384,256]{1,0:T(8,128)(2,1)S(1)} %get-tuple-element.26.row_low, ...), custom_call_target="tpu_custom_call" | custom-call | tf_op jit(solution)/shard_map/join/pallas_call | solution.py:262
  14.3 3.9 %collective-permute-start.3 = (f32[3,64,128]{2,1,0:T(8,128)S(1)}, f32[3,64,128]{2,1,0:T(8,128)S(1)}, u32[]{:S(2)}, u32[]{:S(2)}) collective-permute-start(f32[3,64,128]{2,1,0:T(8,128)S(1)} %get-tuple-element.30), channel_id=1, source_target_pairs={{0,24},{4,28},{8,16},{12,20},{16,8},{20,12},{24,0},{28,4},{1,25},{... | collective-permute-start | bytes 294920 | tf_op jit(solution)/shard_map/ppermute | solution.py:276
  18.1 0.0 collective-permute-start.1
  18.1 0.6 %collective-permute-start.2 = (f32[3,64,128]{2,1,0:T(8,128)S(1)}, f32[3,64,128]{2,1,0:T(8,128)S(1)}, u32[]{:S(2)}, u32[]{:S(2)}) collective-permute-start(f32[3,64,128]{2,1,0:T(8,128)S(1)} %get-tuple-element.29), channel_id=1, source_target_pairs={{0,16},{4,20},{8,24},{12,28},{16,0},{20,4},{24,8},{28,12},{1,17},{... | collective-permute-start | bytes 294920 | tf_op jit(solution)/shard_map/ppermute | solution.py:276
  18.8 2.6 %collective-permute-done.3 = f32[3,64,128]{2,1,0:T(8,128)S(1)} collective-permute-done((f32[3,64,128]{2,1,0:T(8,128)S(1)}, f32[3,64,128]{2,1,0:T(8,128)S(1)}, u32[]{:S(2)}, u32[]{:S(2)}) %collective-permute-start.3) | collective-permute-done | bytes 98336 | tf_op jit(solution)/shard_map/ppermute | solution.py:276
  21.4 3.0 %collective-permute-done.1 = f32[3,64,128]{2,1,0:T(8,128)S(1)} collective-permute-done((f32[3,64,128]{2,1,0:T(8,128)S(1)}, f32[3,64,128]{2,1,0:T(8,128)S(1)}, u32[]{:S(2)}, u32[]{:S(2)}) %collective-permute-start.1) | collective-permute-done | bytes 98336 | tf_op jit(solution)/shard_map/ppermute | solution.py:276
  24.4 1.2 %collective-permute-done.2 = f32[3,64,128]{2,1,0:T(8,128)S(1)} collective-permute-done((f32[3,64,128]{2,1,0:T(8,128)S(1)}, f32[3,64,128]{2,1,0:T(8,128)S(1)}, u32[]{:S(2)}, u32[]{:S(2)}) %collective-permute-start.2) | collective-permute-done | bytes 98336 | tf_op jit(solution)/shard_map/ppermute | solution.py:276
  25.6 0.1 collective-permute-done.5
  25.7 1.2 %collective-permute-done.6 = f32[3,64,128]{2,1,0:T(8,128)S(1)} collective-permute-done((f32[3,64,128]{2,1,0:T(8,128)S(1)}, f32[3,64,128]{2,1,0:T(8,128)S(1)}, u32[]{:S(2)}, u32[]{:S(2)}) %collective-permute-start.6) | collective-permute-done | bytes 98336 | tf_op jit(solution)/shard_map/ppermute | solution.py:279
  26.9 0.1 combine.1
  27.0 0.6 %collective-permute-start.8 = (f32[3,64,128]{2,1,0:T(8,128)S(1)}, f32[3,64,128]{2,1,0:T(8,128)S(1)}, u32[]{:S(2)}, u32[]{:S(2)}) collective-permute-start(f32[3,64,128]{2,1,0:T(8,128)S(1)} %bitcast.21), channel_id=1, source_target_pairs={{0,8},{4,12},{8,0},{12,4},{16,24},{20,28},{24,16},{28,20},{1,9},{5... | collective-permute-start | bytes 294920 | tf_op jit(solution)/shard_map/ppermute | solution.py:276
  27.6 4.3 %collective-permute-done.8.refs_1_ = f32[3,64,128]{2,1,0:T(8,128)S(1)} collective-permute-done((f32[3,64,128]{2,1,0:T(8,128)S(1)}, f32[3,64,128]{2,1,0:T(8,128)S(1)}, u32[]{:S(2)}, u32[]{:S(2)}) %collective-permute-start.8) | collective-permute-done | bytes 98336 | tf_op jit(solution)/shard_map/ppermute | solution.py:276
  31.9 0.7 %gather.1 = f32[1,1,3,128,128]{4,3,2,1,0:T(8,128)} custom-call(f32[3,64,128]{2,1,0:T(8,128)S(1)} %bitcast.12, f32[3,64,128]{2,1,0:T(8,128)S(1)} %collective-permute-done.8.refs_1_), custom_call_target="tpu_custom_call" | custom-call | tf_op jit(solution)/shard_map/gather/pallas_call | solution.py:294
  (14 shorter events, 0.0 us)
Async XLA Ops:
  0.7 5.9 %copy-start.2 = (s32[1,12]{1,0:T(1,128)S(1)}, s32[1,12]{1,0:T(1,128)}, u32[]{:S(2)}) copy-start(s32[1,12]{1,0:T(1,128)} %cols.1) | copy-start | bytes 148
  0.7 5.9 %copy-start.3 = (s32[1,2]{1,0:T(1,128)S(1)}, s32[1,2]{1,0:T(1,128)}, u32[]{:S(2)}) copy-start(s32[1,2]{1,0:T(1,128)} %border_map.1) | copy-start | bytes 28
  3.4 3.1 %copy-start.4 = (f32[8]{0:T(128)S(1)}, f32[8]{0:T(128)}, u32[]{:S(2)}) copy-start(f32[8]{0:T(128)} %param.21) | copy-start | bytes 100
  3.4 3.0 %copy-start.5 = (f32[8]{0:T(128)S(1)}, f32[8]{0:T(128)}, u32[]{:S(2)}) copy-start(f32[8]{0:T(128)} %param.23) | copy-start | bytes 100
  3.4 3.0 %copy-start.6 = (f32[8]{0:T(128)S(1)}, f32[8]{0:T(128)}, u32[]{:S(2)}) copy-start(f32[8]{0:T(128)} %param.22) | copy-start | bytes 100
  3.4 10.3 %collective-permute-start = (f32[256,256]{1,0:T(8,128)S(1)}, f32[256,256]{1,0:T(8,128)S(1)}, u32[]{:S(2)}, u32[]{:S(2)}) collective-permute-start(f32[256,256]{1,0:T(8,128)S(1)} %get-tuple-element.23), channel_id=1, source_target_pairs={{0,1},{1,2},{2,3},{3,0},{4,5},{5,6},{6,7},{7,4},{8,9},{9,10},{10,1... | collective-permute-start | bytes 786440 | tf_op jit(solution)/shard_map/ppermute | solution.py:239
  6.5 0.7 %copy-start = (s32[1,3,2]{1,2,0:T(2,128)S(1)}, s32[1,3,2]{1,2,0:T(2,128)}, u32[]{:S(2)}) copy-start(s32[1,3,2]{1,2,0:T(2,128)} %param.20) | copy-start | bytes 76
  6.6 0.7 %copy-start.1 = (s32[1,12]{1,0:T(1,128)S(1)}, s32[1,12]{1,0:T(1,128)}, u32[]{:S(2)}) copy-start(s32[1,12]{1,0:T(1,128)} %rows.1) | copy-start | bytes 148
  14.3 7.1 %collective-permute-start.3 = (f32[3,64,128]{2,1,0:T(8,128)S(1)}, f32[3,64,128]{2,1,0:T(8,128)S(1)}, u32[]{:S(2)}, u32[]{:S(2)}) collective-permute-start(f32[3,64,128]{2,1,0:T(8,128)S(1)} %get-tuple-element.30), channel_id=1, source_target_pairs={{0,24},{4,28},{8,16},{12,20},{16,8},{20,12},{24,0},{28,4},{1,25},{... | collective-permute-start | bytes 294920 | tf_op jit(solution)/shard_map/ppermute | solution.py:276
  18.1 6.2 %collective-permute-start.1 = (f32[3,64,128]{2,1,0:T(8,128)S(1)}, f32[3,64,128]{2,1,0:T(8,128)S(1)}, u32[]{:S(2)}, u32[]{:S(2)}) collective-permute-start(f32[3,64,128]{2,1,0:T(8,128)S(1)} %get-tuple-element.30), channel_id=1, source_target_pairs={{0,8},{4,12},{8,0},{12,4},{16,24},{20,28},{24,16},{28,20},{1,9},{5... | collective-permute-start | bytes 294920 | tf_op jit(solution)/shard_map/ppermute | solution.py:276
  18.1 7.4 %collective-permute-start.2 = (f32[3,64,128]{2,1,0:T(8,128)S(1)}, f32[3,64,128]{2,1,0:T(8,128)S(1)}, u32[]{:S(2)}, u32[]{:S(2)}) collective-permute-start(f32[3,64,128]{2,1,0:T(8,128)S(1)} %get-tuple-element.29), channel_id=1, source_target_pairs={{0,16},{4,20},{8,24},{12,28},{16,0},{20,4},{24,8},{28,12},{1,17},{... | collective-permute-start | bytes 294920 | tf_op jit(solution)/shard_map/ppermute | solution.py:276
  18.8 6.8 %collective-permute-start.4 = (f32[3,64,128]{2,1,0:T(8,128)S(1)}, f32[3,64,128]{2,1,0:T(8,128)S(1)}, u32[]{:S(2)}, u32[]{:S(2)}) collective-permute-start(f32[3,64,128]{2,1,0:T(8,128)S(1)} %get-tuple-element.29), channel_id=1, source_target_pairs={{0,4},{4,0},{8,12},{12,8},{16,20},{20,16},{24,28},{28,24},{1,5},{5... | collective-permute-start | bytes 294920 | tf_op jit(solution)/shard_map/ppermute | solution.py:279
  21.4 4.2 %collective-permute-start.7 = (f32[3,64,128]{2,1,0:T(8,128)S(1)}, f32[3,64,128]{2,1,0:T(8,128)S(1)}, u32[]{:S(2)}, u32[]{:S(2)}) collective-permute-start(f32[3,64,128]{2,1,0:T(8,128)S(1)} %collective-permute-done.3), channel_id=1, source_target_pairs={{0,4},{4,0},{8,12},{12,8},{16,20},{20,16},{24,28},{28,24},{1,5},{5... | collective-permute-start | bytes 294920 | tf_op jit(solution)/shard_map/ppermute | solution.py:279
  24.4 1.3 %collective-permute-start.5 = (f32[3,64,128]{2,1,0:T(8,128)S(1)}, f32[3,64,128]{2,1,0:T(8,128)S(1)}, u32[]{:S(2)}, u32[]{:S(2)}) collective-permute-start(f32[3,64,128]{2,1,0:T(8,128)S(1)} %collective-permute-done.1), channel_id=1, source_target_pairs={{0,4},{4,0},{8,12},{12,8},{16,20},{20,16},{24,28},{28,24},{1,5},{5... | collective-permute-start | bytes 294920 | tf_op jit(solution)/shard_map/ppermute | solution.py:279
  25.6 1.3 %collective-permute-start.6 = (f32[3,64,128]{2,1,0:T(8,128)S(1)}, f32[3,64,128]{2,1,0:T(8,128)S(1)}, u32[]{:S(2)}, u32[]{:S(2)}) collective-permute-start(f32[3,64,128]{2,1,0:T(8,128)S(1)} %collective-permute-done.2), channel_id=1, source_target_pairs={{0,4},{4,0},{8,12},{12,8},{16,20},{20,16},{24,28},{28,24},{1,5},{5... | collective-permute-start | bytes 294920 | tf_op jit(solution)/shard_map/ppermute | solution.py:279
  27.0 4.9 %collective-permute-start.8 = (f32[3,64,128]{2,1,0:T(8,128)S(1)}, f32[3,64,128]{2,1,0:T(8,128)S(1)}, u32[]{:S(2)}, u32[]{:S(2)}) collective-permute-start(f32[3,64,128]{2,1,0:T(8,128)S(1)} %bitcast.21), channel_id=1, source_target_pairs={{0,8},{4,12},{8,0},{12,4},{16,24},{20,28},{24,16},{28,20},{1,9},{5... | collective-permute-start | bytes 294920 | tf_op jit(solution)/shard_map/ppermute | solution.py:276

commit v6 on v5

--- a/solution.py
+++ b/solution.py
@@ -97,7 +97,10 @@
         high_out[at], low_out[at] = product
         term = dot3((fit_high[:, at], fit_low[:, at]), product, NN)
         left = term if left is None else left + term
-    out[...] = dot3_halves(split(left), (fit_high[...], fit_low[...]), NT)
+    left = split(left)
+    half = out.shape[1] // 2
+    for at in (slice(0, half), slice(half, 2 * half)):
+        out[:, at] = dot3(left, (fit_high[at, :], fit_low[at, :]), NT)
 
 
 def own_kernel(
@@ -173,8 +176,9 @@
     for k, part in enumerate(parts):
         share = part.shape[1]
         at = pl.ds(pl.multiple_of(((chip ^ k) % PARTNERS) * share, share), share)
-        copies.append(pltpu.make_async_copy(part, out.at[0, 0, :, at, :], sems.at[k]))
-        copies[k].start()
+        for p in range(part.shape[0]):
+            copies.append(pltpu.make_async_copy(part.at[p], out.at[0, 0, p, at, :], sems.at[k, p]))
+            copies[-1].start()
     for copy in copies:
         copy.wait()
 
@@ -296,7 +300,7 @@
         out_shape=jax.ShapeDtypeStruct((1, 1, pairs, order, order), f32),
         in_specs=[VMEM] * PARTNERS,
         out_specs=ANY,
-        scratch_shapes=[pltpu.SemaphoreType.DMA((PARTNERS,))],
+        scratch_shapes=[pltpu.SemaphoreType.DMA((PARTNERS, pairs))],
         compiler_params=limit,
         name="gather",
     )(*map(in_vmem, parts))

time: 32.8 us -> 32.9 us (level)
  no operation moved by 1% of the time
where the time goes in v6:
time: 32.9 us; the launch traced here: 32.6 us
  waiting for transfers between devices  15.1 us (46%)
  starting transfers between devices  8.09 us (25%)
  Pallas kernels  7.94 us (24%)
  between operations  0.76 us (2%)
  local copies, waits for them, and re-layouts  0.68 us (2%)
    ppermute x4, waiting for transfers between devices, across(): return lax.ppermute(x, 'tm', pairs_of)  11.1 us
    ppermute x4, starting transfers between devices, across(): return lax.ppermute(x, 'tm', pairs_of)  5.07 us
    pallas_call x1, Pallas kernels, on_device(): pl.pallas_call(own_kernel, out_shape=(pltpu.VMEM((pairs, order, order), f...  3.8 us
    ppermute x1, starting transfers between devices, on_device(): lax.ppermute(border, 'sec', [(i, (i + 1) % sections) for i in range(secti...  3.01 us
    pallas_call x1, Pallas kernels, on_device(): pl.pallas_call(border_kernel, out_shape=(pltpu.VMEM((edge_rows, edge_rows...  2.72 us
    ppermute x1, waiting for transfers between devices, on_device(): lax.ppermute(border, 'sec', [(i, (i + 1) % sections) for i in range(secti...  2.65 us
    ppermute x4, waiting for transfers between devices, swap(): return lax.ppermute(x, 'tm', [(i, i ^ 1) for i in range(devices)])  1.29 us
    pallas_call x1, Pallas kernels, on_device(): pl.pallas_call(gather_kernel, out_shape=jax.ShapeDtypeStruct((1, 1, pairs...  0.72 us
  transfers between devices with their start and end apart: 9, of which 7 were waited for; matrix products, arithmetic and copies ran while one was open for 0% of the time, Pallas kernels for 12%

profile of v6, /device:TPU:0, one launch (start us, length us, event | category | flops | bytes accessed | tf_op | source)
XLA Modules:
  0.0 32.6 jit_solution(2783681887397639521)
XLA Ops:
  0.7 2.7 %border.1 = (f32[256,256]{1,0:T(8,128)S(1)}, bf16[512,512]{1,0:T(8,128)(2,1)S(1)}, bf16[512,512]{1,0:T(8,128)(2,1)S(1)}, f32[12,128,128]{2,1,0:T(8,128)S(1)}) custom-call(s32[1]{0:T(128)S(6)} %copy.13.count, s32[1,12]{1,0:T(1,128)} %rows.1, s32[1,12]{1,0:T(1,128)} %cols.1, f32[1,1,512,512]{3,2,1,0:T(8,128)} %occ.1, f32[1,1,512,512]{3,2,1,0:T(8,128)} %virt.1, ...), custom_call_target="tpu_custom_call" | custom-call | flops 1000000000 | bytes 3145728 | tf_op jit(solution)/shard_map/border/pallas_call | solution.py:221
  3.4 0.0 copy-start.4
  3.4 0.0 copy-start.5
  3.4 0.0 copy-start.6
  3.4 3.0 %collective-permute-start = (f32[256,256]{1,0:T(8,128)S(1)}, f32[256,256]{1,0:T(8,128)S(1)}, u32[]{:S(2)}, u32[]{:S(2)}) collective-permute-start(f32[256,256]{1,0:T(8,128)S(1)} %get-tuple-element.23), channel_id=1, source_target_pairs={{0,1},{1,2},{2,3},{3,0},{4,5},{5,6},{6,7},{7,4},{8,9},{9,10},{10,1... | collective-permute-start | bytes 786440 | tf_op jit(solution)/shard_map/ppermute | solution.py:243
  6.5 0.1 cosine_multiply_fusion.cosine
  6.6 0.0 copy-start
  6.6 0.0 copy-start.1
  6.6 0.6 %copy-done = s32[1,3,2]{1,2,0:T(2,128)S(1)} copy-done((s32[1,3,2]{1,2,0:T(2,128)S(1)}, s32[1,3,2]{1,2,0:T(2,128)}, u32[]{:S(2)}) %copy-start) | copy-done | bytes 48
  7.3 3.8 %own.1 = (f32[3,128,128]{2,1,0:T(8,128)S(1)}, bf16[384,256]{1,0:T(8,128)(2,1)S(1)}, bf16[384,256]{1,0:T(8,128)(2,1)S(1)}, bf16[384,256]{1,0:T(8,128)(2,1)S(1)}, ...) custom-call(s32[1,12]{1,0:T(1,128)S(1)} %copy-done.1, s32[1,12]{1,0:T(1,128)S(1)} %copy-done.2, ...), custom_call_target="tpu_custom_call" | custom-call | flops 2000000000 | bytes 5242880 | tf_op jit(solution)/shard_map/own/pallas_call | solution.py:246
  11.1 2.6 %collective-permute-done.border = f32[256,256]{1,0:T(8,128)S(1)} collective-permute-done((f32[256,256]{1,0:T(8,128)S(1)}, f32[256,256]{1,0:T(8,128)S(1)}, u32[]{:S(2)}, u32[]{:S(2)}) %collective-permute-start) | collective-permute-done | bytes 262176 | tf_op jit(solution)/shard_map/ppermute | solution.py:243
  13.7 0.6 %join.1 = (f32[3,64,128]{2,1,0:T(8,128)S(1)}, f32[3,64,128]{2,1,0:T(8,128)S(1)}) custom-call(f32[256,256]{1,0:T(8,128)S(1)} %collective-permute-done.border, f32[3,128,128]{2,1,0:T(8,128)S(1)} %get-tuple-element.24.own, bf16[384,256]{1,0:T(8,128)(2,1)S(1)} %get-tuple-element.25.row_high, bf16[384,256]{1,0:T(8,128)(2,1)S(1)} %get-tuple-element.26.row_low, ...), custom_call_target="tpu_custom_call" | custom-call | tf_op jit(solution)/shard_map/join/pallas_call | solution.py:266
  14.3 3.9 %collective-permute-start.3 = (f32[3,64,128]{2,1,0:T(8,128)S(1)}, f32[3,64,128]{2,1,0:T(8,128)S(1)}, u32[]{:S(2)}, u32[]{:S(2)}) collective-permute-start(f32[3,64,128]{2,1,0:T(8,128)S(1)} %get-tuple-element.30), channel_id=1, source_target_pairs={{0,24},{4,28},{8,16},{12,20},{16,8},{20,12},{24,0},{28,4},{1,25},{... | collective-permute-start | bytes 294920 | tf_op jit(solution)/shard_map/ppermute | solution.py:280
  18.2 0.0 collective-permute-start.1
  18.2 0.6 %collective-permute-start.2 = (f32[3,64,128]{2,1,0:T(8,128)S(1)}, f32[3,64,128]{2,1,0:T(8,128)S(1)}, u32[]{:S(2)}, u32[]{:S(2)}) collective-permute-start(f32[3,64,128]{2,1,0:T(8,128)S(1)} %get-tuple-element.29), channel_id=1, source_target_pairs={{0,16},{4,20},{8,24},{12,28},{16,0},{20,4},{24,8},{28,12},{1,17},{... | collective-permute-start | bytes 294920 | tf_op jit(solution)/shard_map/ppermute | solution.py:280
  18.8 2.6 %collective-permute-done.3 = f32[3,64,128]{2,1,0:T(8,128)S(1)} collective-permute-done((f32[3,64,128]{2,1,0:T(8,128)S(1)}, f32[3,64,128]{2,1,0:T(8,128)S(1)}, u32[]{:S(2)}, u32[]{:S(2)}) %collective-permute-start.3) | collective-permute-done | bytes 98336 | tf_op jit(solution)/shard_map/ppermute | solution.py:280
  21.4 3.0 %collective-permute-done.1 = f32[3,64,128]{2,1,0:T(8,128)S(1)} collective-permute-done((f32[3,64,128]{2,1,0:T(8,128)S(1)}, f32[3,64,128]{2,1,0:T(8,128)S(1)}, u32[]{:S(2)}, u32[]{:S(2)}) %collective-permute-start.1) | collective-permute-done | bytes 98336 | tf_op jit(solution)/shard_map/ppermute | solution.py:280
  24.4 1.2 %collective-permute-done.2 = f32[3,64,128]{2,1,0:T(8,128)S(1)} collective-permute-done((f32[3,64,128]{2,1,0:T(8,128)S(1)}, f32[3,64,128]{2,1,0:T(8,128)S(1)}, u32[]{:S(2)}, u32[]{:S(2)}) %collective-permute-start.2) | collective-permute-done | bytes 98336 | tf_op jit(solution)/shard_map/ppermute | solution.py:280
  25.6 0.1 collective-permute-done.5
  25.7 1.2 %collective-permute-done.6 = f32[3,64,128]{2,1,0:T(8,128)S(1)} collective-permute-done((f32[3,64,128]{2,1,0:T(8,128)S(1)}, f32[3,64,128]{2,1,0:T(8,128)S(1)}, u32[]{:S(2)}, u32[]{:S(2)}) %collective-permute-start.6) | collective-permute-done | bytes 98336 | tf_op jit(solution)/shard_map/ppermute | solution.py:283
  26.9 0.1 combine.1
  27.0 0.6 %collective-permute-start.8 = (f32[3,64,128]{2,1,0:T(8,128)S(1)}, f32[3,64,128]{2,1,0:T(8,128)S(1)}, u32[]{:S(2)}, u32[]{:S(2)}) collective-permute-start(f32[3,64,128]{2,1,0:T(8,128)S(1)} %bitcast.21), channel_id=1, source_target_pairs={{0,8},{4,12},{8,0},{12,4},{16,24},{20,28},{24,16},{28,20},{1,9},{5... | collective-permute-start | bytes 294920 | tf_op jit(solution)/shard_map/ppermute | solution.py:280
  27.6 4.3 %collective-permute-done.8.refs_1_ = f32[3,64,128]{2,1,0:T(8,128)S(1)} collective-permute-done((f32[3,64,128]{2,1,0:T(8,128)S(1)}, f32[3,64,128]{2,1,0:T(8,128)S(1)}, u32[]{:S(2)}, u32[]{:S(2)}) %collective-permute-start.8) | collective-permute-done | bytes 98336 | tf_op jit(solution)/shard_map/ppermute | solution.py:280
  31.9 0.7 %gather.1 = f32[1,1,3,128,128]{4,3,2,1,0:T(8,128)} custom-call(f32[3,64,128]{2,1,0:T(8,128)S(1)} %bitcast.12, f32[3,64,128]{2,1,0:T(8,128)S(1)} %collective-permute-done.8.refs_1_), custom_call_target="tpu_custom_call" | custom-call | tf_op jit(solution)/shard_map/gather/pallas_call | solution.py:298
  (14 shorter events, 0.0 us)
Async XLA Ops:
  0.7 5.9 %copy-start.2 = (s32[1,12]{1,0:T(1,128)S(1)}, s32[1,12]{1,0:T(1,128)}, u32[]{:S(2)}) copy-start(s32[1,12]{1,0:T(1,128)} %cols.1) | copy-start | bytes 148
  0.7 5.9 %copy-start.3 = (s32[1,2]{1,0:T(1,128)S(1)}, s32[1,2]{1,0:T(1,128)}, u32[]{:S(2)}) copy-start(s32[1,2]{1,0:T(1,128)} %border_map.1) | copy-start | bytes 28
  3.4 3.1 %copy-start.4 = (f32[8]{0:T(128)S(1)}, f32[8]{0:T(128)}, u32[]{:S(2)}) copy-start(f32[8]{0:T(128)} %param.21) | copy-start | bytes 100
  3.4 3.0 %copy-start.5 = (f32[8]{0:T(128)S(1)}, f32[8]{0:T(128)}, u32[]{:S(2)}) copy-start(f32[8]{0:T(128)} %param.23) | copy-start | bytes 100
  3.4 3.0 %copy-start.6 = (f32[8]{0:T(128)S(1)}, f32[8]{0:T(128)}, u32[]{:S(2)}) copy-start(f32[8]{0:T(128)} %param.22) | copy-start | bytes 100
  3.4 10.3 %collective-permute-start = (f32[256,256]{1,0:T(8,128)S(1)}, f32[256,256]{1,0:T(8,128)S(1)}, u32[]{:S(2)}, u32[]{:S(2)}) collective-permute-start(f32[256,256]{1,0:T(8,128)S(1)} %get-tuple-element.23), channel_id=1, source_target_pairs={{0,1},{1,2},{2,3},{3,0},{4,5},{5,6},{6,7},{7,4},{8,9},{9,10},{10,1... | collective-permute-start | bytes 786440 | tf_op jit(solution)/shard_map/ppermute | solution.py:243
  6.6 0.7 %copy-start = (s32[1,3,2]{1,2,0:T(2,128)S(1)}, s32[1,3,2]{1,2,0:T(2,128)}, u32[]{:S(2)}) copy-start(s32[1,3,2]{1,2,0:T(2,128)} %param.20) | copy-start | bytes 76
  6.6 0.7 %copy-start.1 = (s32[1,12]{1,0:T(1,128)S(1)}, s32[1,12]{1,0:T(1,128)}, u32[]{:S(2)}) copy-start(s32[1,12]{1,0:T(1,128)} %rows.1) | copy-start | bytes 148
  14.3 7.1 %collective-permute-start.3 = (f32[3,64,128]{2,1,0:T(8,128)S(1)}, f32[3,64,128]{2,1,0:T(8,128)S(1)}, u32[]{:S(2)}, u32[]{:S(2)}) collective-permute-start(f32[3,64,128]{2,1,0:T(8,128)S(1)} %get-tuple-element.30), channel_id=1, source_target_pairs={{0,24},{4,28},{8,16},{12,20},{16,8},{20,12},{24,0},{28,4},{1,25},{... | collective-permute-start | bytes 294920 | tf_op jit(solution)/shard_map/ppermute | solution.py:280
  18.2 6.2 %collective-permute-start.1 = (f32[3,64,128]{2,1,0:T(8,128)S(1)}, f32[3,64,128]{2,1,0:T(8,128)S(1)}, u32[]{:S(2)}, u32[]{:S(2)}) collective-permute-start(f32[3,64,128]{2,1,0:T(8,128)S(1)} %get-tuple-element.30), channel_id=1, source_target_pairs={{0,8},{4,12},{8,0},{12,4},{16,24},{20,28},{24,16},{28,20},{1,9},{5... | collective-permute-start | bytes 294920 | tf_op jit(solution)/shard_map/ppermute | solution.py:280
  18.2 7.4 %collective-permute-start.2 = (f32[3,64,128]{2,1,0:T(8,128)S(1)}, f32[3,64,128]{2,1,0:T(8,128)S(1)}, u32[]{:S(2)}, u32[]{:S(2)}) collective-permute-start(f32[3,64,128]{2,1,0:T(8,128)S(1)} %get-tuple-element.29), channel_id=1, source_target_pairs={{0,16},{4,20},{8,24},{12,28},{16,0},{20,4},{24,8},{28,12},{1,17},{... | collective-permute-start | bytes 294920 | tf_op jit(solution)/shard_map/ppermute | solution.py:280
  18.8 6.8 %collective-permute-start.4 = (f32[3,64,128]{2,1,0:T(8,128)S(1)}, f32[3,64,128]{2,1,0:T(8,128)S(1)}, u32[]{:S(2)}, u32[]{:S(2)}) collective-permute-start(f32[3,64,128]{2,1,0:T(8,128)S(1)} %get-tuple-element.29), channel_id=1, source_target_pairs={{0,4},{4,0},{8,12},{12,8},{16,20},{20,16},{24,28},{28,24},{1,5},{5... | collective-permute-start | bytes 294920 | tf_op jit(solution)/shard_map/ppermute | solution.py:283
  21.4 4.2 %collective-permute-start.7 = (f32[3,64,128]{2,1,0:T(8,128)S(1)}, f32[3,64,128]{2,1,0:T(8,128)S(1)}, u32[]{:S(2)}, u32[]{:S(2)}) collective-permute-start(f32[3,64,128]{2,1,0:T(8,128)S(1)} %collective-permute-done.3), channel_id=1, source_target_pairs={{0,4},{4,0},{8,12},{12,8},{16,20},{20,16},{24,28},{28,24},{1,5},{5... | collective-permute-start | bytes 294920 | tf_op jit(solution)/shard_map/ppermute | solution.py:283
  24.4 1.3 %collective-permute-start.5 = (f32[3,64,128]{2,1,0:T(8,128)S(1)}, f32[3,64,128]{2,1,0:T(8,128)S(1)}, u32[]{:S(2)}, u32[]{:S(2)}) collective-permute-start(f32[3,64,128]{2,1,0:T(8,128)S(1)} %collective-permute-done.1), channel_id=1, source_target_pairs={{0,4},{4,0},{8,12},{12,8},{16,20},{20,16},{24,28},{28,24},{1,5},{5... | collective-permute-start | bytes 294920 | tf_op jit(solution)/shard_map/ppermute | solution.py:283
  25.6 1.3 %collective-permute-start.6 = (f32[3,64,128]{2,1,0:T(8,128)S(1)}, f32[3,64,128]{2,1,0:T(8,128)S(1)}, u32[]{:S(2)}, u32[]{:S(2)}) collective-permute-start(f32[3,64,128]{2,1,0:T(8,128)S(1)} %collective-permute-done.2), channel_id=1, source_target_pairs={{0,4},{4,0},{8,12},{12,8},{16,20},{20,16},{24,28},{28,24},{1,5},{5... | collective-permute-start | bytes 294920 | tf_op jit(solution)/shard_map/ppermute | solution.py:283
  27.0 4.9 %collective-permute-start.8 = (f32[3,64,128]{2,1,0:T(8,128)S(1)}, f32[3,64,128]{2,1,0:T(8,128)S(1)}, u32[]{:S(2)}, u32[]{:S(2)}) collective-permute-start(f32[3,64,128]{2,1,0:T(8,128)S(1)} %bitcast.21), channel_id=1, source_target_pairs={{0,8},{4,12},{8,0},{12,4},{16,24},{20,28},{24,16},{28,20},{1,9},{5... | collective-permute-start | bytes 294920 | tf_op jit(solution)/shard_map/ppermute | solution.py:280

commit v7 on v5

--- a/solution.py
+++ b/solution.py
@@ -132,13 +132,12 @@
         )
     index = lax.axis_index("tm")
     chip, core = index // CORES, index % CORES
-    chips = weight.shape[1]
     for k in range(PARTNERS):
-        freq = (chip ^ k) * CORES + core
-        for j in range(chips):
-            at = (chip ^ j) * CORES
-            weight[k, j, 0] = jnp.full(weight.shape[3:], cosine[freq, at + core])
-            weight[k, j, 1] = jnp.full(weight.shape[3:], cosine[freq, at + 1 - core])
+        for d in range(CORES):
+            freq = (chip ^ k) * CORES + (core ^ d)
+            for j in range(weight.shape[2]):
+                value = cosine[freq, (chip ^ j) * CORES + core]
+                weight[k, d, j] = jnp.full(weight.shape[3:], value)
 
 
 def join_kernel(border, own, row_high, row_low, col_high, col_low, *refs):
@@ -156,27 +155,22 @@
 
 
 def combine_kernel(weight, *refs):
-    chips = weight.shape[1]
-    mine, other, outs = refs[:chips], refs[chips : 2 * chips], refs[2 * chips :]
+    chips = weight.shape[2]
+    mine, outs = refs[:chips], refs[chips:]
+    for q, out in enumerate(outs):
+        total = jnp.zeros(out.shape, jnp.float32)
+        for j in range(chips):
+            total += weight[q // CORES, q % CORES, j] * mine[j][...]
+        out[...] = total
+
+
+def gather_kernel(*refs):
+    parts, out = refs[:-1], refs[-1]
+    chip = lax.axis_index("tm") // CORES
+    share = parts[0].shape[1]
     for k in range(PARTNERS):
-        total = jnp.zeros(outs[k].shape, jnp.float32)
-        for j in range(chips):
-            total += weight[k, j, 0] * mine[j][...]
-            total += weight[k, j, 1] * other[j][...]
-        outs[k][...] = total
-
-
-def gather_kernel(*refs):
-    parts, out, sems = refs[:-2], refs[-2], refs[-1]
-    chip = lax.axis_index("tm") // CORES
-    copies = []
-    for k, part in enumerate(parts):
-        share = part.shape[1]
         at = pl.ds(pl.multiple_of(((chip ^ k) % PARTNERS) * share, share), share)
-        copies.append(pltpu.make_async_copy(part, out.at[0, 0, :, at, :], sems.at[k]))
-        copies[k].start()
-    for copy in copies:
-        copy.wait()
+        out[0, 0, :, at, :] = parts[k * CORES][...] + parts[k * CORES + 1][...]
 
 
 def in_vmem(x):
@@ -243,7 +237,7 @@
         own_kernel,
         out_shape=(pltpu.VMEM((pairs, order, order), f32),)
         + (edge,) * 4
-        + (pltpu.VMEM((PARTNERS, chips, CORES, SUBLANES, order), f32),),
+        + (pltpu.VMEM((PARTNERS, CORES, chips, SUBLANES, order), f32),),
         in_specs=[SMEM] * 6 + [VMEM] * 4,
         out_specs=(VMEM,) * 6,
         scratch_shapes=[pltpu.VMEM((own_rows, points), bf16)] * 4
@@ -275,31 +269,31 @@
         ]
         return lax.ppermute(x, "tm", pairs_of)
 
-    def swap(x):
-        return lax.ppermute(x, "tm", [(i, i ^ 1) for i in range(devices)])
+    def onward(x, k, d):
+        return lax.ppermute(x, "tm", [(i, i ^ (CORES * k + d)) for i in range(devices)])
 
     mine = [parts[0]] + [across(parts[k % PARTNERS], k) for k in range(1, chips)]
-    other = [swap(x) for x in mine]
     tiles = pltpu.VMEM((pairs * share // SUBLANES, SUBLANES, order), f32)
-    parts = pl.pallas_call(
+    sums = pl.pallas_call(
         combine_kernel,
-        out_shape=(tiles,) * PARTNERS,
-        in_specs=[VMEM] * (2 * chips + 1),
-        out_specs=(VMEM,) * PARTNERS,
+        out_shape=(tiles,) * (PARTNERS * CORES),
+        in_specs=[VMEM] * (chips + 1),
+        out_specs=(VMEM,) * (PARTNERS * CORES),
         compiler_params=limit,
         name="combine",
-    )(*(in_vmem(x.reshape(tiles.shape) if x.ndim == 3 else x) for x in (weight, *mine, *other)))
-    parts = [x.reshape(part.shape) for x in parts]
-    parts = [parts[0]] + [across(parts[k], k) for k in range(1, PARTNERS)]
+    )(in_vmem(weight), *(in_vmem(x.reshape(tiles.shape)) for x in mine))
+    sums = [x.reshape(part.shape) for x in sums]
+    sums = [sums[0]] + [
+        onward(sums[q], q // CORES, q % CORES) for q in range(1, PARTNERS * CORES)
+    ]
     return pl.pallas_call(
         gather_kernel,
         out_shape=jax.ShapeDtypeStruct((1, 1, pairs, order, order), f32),
-        in_specs=[VMEM] * PARTNERS,
-        out_specs=ANY,
-        scratch_shapes=[pltpu.SemaphoreType.DMA((PARTNERS,))],
+        in_specs=[VMEM] * (PARTNERS * CORES),
+        out_specs=VMEM,
         compiler_params=limit,
         name="gather",
-    )(*map(in_vmem, parts))
+    )(*map(in_vmem, sums))
 
 
 def solution(mesh):

time: 32.8 us -> 32.7 us (level)
  waiting for transfers between devices: 15 us -> 13.7 us
  starting transfers between devices: 8.09 us -> 9.35 us
    ppermute x4 -> x3, waiting for transfers between devices: 11.1 us -> 6.1 us  [across(): return lax.ppermute(x, 'tm', pairs_of)]
    ppermute x4 -> x3, waiting for transfers between devices: 1.29 us -> 4.91 us  [onward(): lax.ppermute(x, 'tm', [(i, i ^ CORES * k + d) for i in range(devices)])]
    ppermute x4 -> x3, starting transfers between devices: 0.01 us -> 1.92 us  [onward(): lax.ppermute(x, 'tm', [(i, i ^ CORES * k + d) for i in range(devices)])]
    ppermute x4 -> x3, starting transfers between devices: 5.07 us -> 4.42 us  [across(): return lax.ppermute(x, 'tm', pairs_of)]
  transfers between devices with their start and end apart: 9 -> 7, of which waited for: 7 -> 6; matrix products, arithmetic and copies ran while one was open for 0% -> 0% of each run, Pallas kernels for 12% -> 12%
where the time goes in v7:
time: 32.7 us; the launch traced here: 32.5 us
  waiting for transfers between devices  13.7 us (42%)
  starting transfers between devices  9.35 us (29%)
  Pallas kernels  7.91 us (24%)
  between operations  0.77 us (2%)
  local copies, waits for them, and re-layouts  0.68 us (2%)
    ppermute x3, waiting for transfers between devices, across(): return lax.ppermute(x, 'tm', pairs_of)  6.1 us
    ppermute x3, waiting for transfers between devices, onward(): lax.ppermute(x, 'tm', [(i, i ^ CORES * k + d) for i in range(devices)])  4.91 us
    ppermute x3, starting transfers between devices, across(): return lax.ppermute(x, 'tm', pairs_of)  4.42 us
    pallas_call x1, Pallas kernels, on_device(): pl.pallas_call(own_kernel, out_shape=(pltpu.VMEM((pairs, order, order), f...  3.81 us
    ppermute x1, starting transfers between devices, on_device(): lax.ppermute(border, 'sec', [(i, (i + 1) % sections) for i in range(secti...  3.01 us
    pallas_call x1, Pallas kernels, on_device(): pl.pallas_call(border_kernel, out_shape=(pltpu.VMEM((edge_rows, edge_rows...  2.69 us
    ppermute x1, waiting for transfers between devices, on_device(): lax.ppermute(border, 'sec', [(i, (i + 1) % sections) for i in range(secti...  2.64 us
    ppermute x3, starting transfers between devices, onward(): lax.ppermute(x, 'tm', [(i, i ^ CORES * k + d) for i in range(devices)])  1.92 us
  transfers between devices with their start and end apart: 7, of which 6 were waited for; matrix products, arithmetic and copies ran while one was open for 0% of the time, Pallas kernels for 12%

profile of v7, /device:TPU:0, one launch (start us, length us, event | category | flops | bytes accessed | tf_op | source)
XLA Modules:
  0.0 32.5 jit_solution(16833847156608466462)
XLA Ops:
  0.7 2.7 %border.1 = (f32[256,256]{1,0:T(8,128)S(1)}, bf16[512,512]{1,0:T(8,128)(2,1)S(1)}, bf16[512,512]{1,0:T(8,128)(2,1)S(1)}, f32[12,128,128]{2,1,0:T(8,128)S(1)}) custom-call(s32[1]{0:T(128)S(6)} %copy.13.count, s32[1,12]{1,0:T(1,128)} %rows.1, s32[1,12]{1,0:T(1,128)} %cols.1, f32[1,1,512,512]{3,2,1,0:T(8,128)} %occ.1, f32[1,1,512,512]{3,2,1,0:T(8,128)} %virt.1, ...), custom_call_target="tpu_custom_call" | custom-call | flops 1000000000 | bytes 3145728 | tf_op jit(solution)/shard_map/border/pallas_call | solution.py:211
  3.4 0.0 copy-start.4
  3.4 0.0 copy-start.5
  3.4 0.0 copy-start.6
  3.4 3.0 %collective-permute-start = (f32[256,256]{1,0:T(8,128)S(1)}, f32[256,256]{1,0:T(8,128)S(1)}, u32[]{:S(2)}, u32[]{:S(2)}) collective-permute-start(f32[256,256]{1,0:T(8,128)S(1)} %get-tuple-element.25), channel_id=1, source_target_pairs={{0,1},{1,2},{2,3},{3,0},{4,5},{5,6},{6,7},{7,4},{8,9},{9,10},{10,1... | collective-permute-start | bytes 786440 | tf_op jit(solution)/shard_map/ppermute | solution.py:233
  6.4 0.1 cosine_multiply_fusion.cosine
  6.5 0.0 copy-start
  6.6 0.6 %copy-done = s32[1,3,2]{1,2,0:T(2,128)S(1)} copy-done((s32[1,3,2]{1,2,0:T(2,128)S(1)}, s32[1,3,2]{1,2,0:T(2,128)}, u32[]{:S(2)}) %copy-start) | copy-done | bytes 48
  7.2 3.8 %own.1 = (f32[3,128,128]{2,1,0:T(8,128)S(1)}, bf16[384,256]{1,0:T(8,128)(2,1)S(1)}, bf16[384,256]{1,0:T(8,128)(2,1)S(1)}, bf16[384,256]{1,0:T(8,128)(2,1)S(1)}, ...) custom-call(s32[1,12]{1,0:T(1,128)S(1)} %copy-done.1, s32[1,12]{1,0:T(1,128)S(1)} %copy-done.2, ...), custom_call_target="tpu_custom_call" | custom-call | flops 2000000000 | bytes 5242880 | tf_op jit(solution)/shard_map/own/pallas_call | solution.py:236
  11.0 2.6 %collective-permute-done.border = f32[256,256]{1,0:T(8,128)S(1)} collective-permute-done((f32[256,256]{1,0:T(8,128)S(1)}, f32[256,256]{1,0:T(8,128)S(1)}, u32[]{:S(2)}, u32[]{:S(2)}) %collective-permute-start) | collective-permute-done | bytes 262176 | tf_op jit(solution)/shard_map/ppermute | solution.py:233
  13.7 0.6 %join.1 = (f32[3,64,128]{2,1,0:T(8,128)S(1)}, f32[3,64,128]{2,1,0:T(8,128)S(1)}) custom-call(f32[256,256]{1,0:T(8,128)S(1)} %collective-permute-done.border, f32[3,128,128]{2,1,0:T(8,128)S(1)} %get-tuple-element.26.own, bf16[384,256]{1,0:T(8,128)(2,1)S(1)} %get-tuple-element.27.row_high, bf16[384,256]{1,0:T(8,128)(2,1)S(1)} %get-tuple-element.28.row_low, ...), custom_call_target="tpu_custom_call" | custom-call | tf_op jit(solution)/shard_map/join/pallas_call | solution.py:256
  14.3 2.8 %collective-permute-start.2 = (f32[3,64,128]{2,1,0:T(8,128)S(1)}, f32[3,64,128]{2,1,0:T(8,128)S(1)}, u32[]{:S(2)}, u32[]{:S(2)}) collective-permute-start(f32[3,64,128]{2,1,0:T(8,128)S(1)} %get-tuple-element.31), channel_id=1, source_target_pairs={{0,16},{4,20},{8,24},{12,28},{16,0},{20,4},{24,8},{28,12},{1,17},{... | collective-permute-start | bytes 294920 | tf_op jit(solution)/shard_map/ppermute | solution.py:270
  17.1 1.3 %collective-permute-start.3 = (f32[3,64,128]{2,1,0:T(8,128)S(1)}, f32[3,64,128]{2,1,0:T(8,128)S(1)}, u32[]{:S(2)}, u32[]{:S(2)}) collective-permute-start(f32[3,64,128]{2,1,0:T(8,128)S(1)} %get-tuple-element.32), channel_id=1, source_target_pairs={{0,24},{4,28},{8,16},{12,20},{16,8},{20,12},{24,0},{28,4},{1,25},{... | collective-permute-start | bytes 294920 | tf_op jit(solution)/shard_map/ppermute | solution.py:270
  18.5 0.2 collective-permute-start.1
  18.7 5.2 %collective-permute-done.2 = f32[3,64,128]{2,1,0:T(8,128)S(1)} collective-permute-done((f32[3,64,128]{2,1,0:T(8,128)S(1)}, f32[3,64,128]{2,1,0:T(8,128)S(1)}, u32[]{:S(2)}, u32[]{:S(2)}) %collective-permute-start.2) | collective-permute-done | bytes 98336 | tf_op jit(solution)/shard_map/ppermute | solution.py:270
  23.9 0.4 %collective-permute-done.3 = f32[3,64,128]{2,1,0:T(8,128)S(1)} collective-permute-done((f32[3,64,128]{2,1,0:T(8,128)S(1)}, f32[3,64,128]{2,1,0:T(8,128)S(1)}, u32[]{:S(2)}, u32[]{:S(2)}) %collective-permute-start.3) | collective-permute-done | bytes 98336 | tf_op jit(solution)/shard_map/ppermute | solution.py:270
  24.3 0.5 %collective-permute-done.1 = f32[3,64,128]{2,1,0:T(8,128)S(1)} collective-permute-done((f32[3,64,128]{2,1,0:T(8,128)S(1)}, f32[3,64,128]{2,1,0:T(8,128)S(1)}, u32[]{:S(2)}, u32[]{:S(2)}) %collective-permute-start.1) | collective-permute-done | bytes 98336 | tf_op jit(solution)/shard_map/ppermute | solution.py:270
  24.8 0.1 combine.1
  24.9 0.1 collective-permute-start.4
  25.0 1.4 %collective-permute-start.5 = (f32[3,64,128]{2,1,0:T(8,128)S(1)}, f32[3,64,128]{2,1,0:T(8,128)S(1)}, u32[]{:S(2)}, u32[]{:S(2)}) collective-permute-start(f32[3,64,128]{2,1,0:T(8,128)S(1)} %bitcast.16), channel_id=1, source_target_pairs={{0,8},{4,12},{8,0},{12,4},{16,24},{20,28},{24,16},{28,20},{1,9},{5... | collective-permute-start | bytes 294920 | tf_op jit(solution)/shard_map/ppermute | solution.py:273
  26.4 0.5 %collective-permute-start.6 = (f32[3,64,128]{2,1,0:T(8,128)S(1)}, f32[3,64,128]{2,1,0:T(8,128)S(1)}, u32[]{:S(2)}, u32[]{:S(2)}) collective-permute-start(f32[3,64,128]{2,1,0:T(8,128)S(1)} %bitcast.15), channel_id=1, source_target_pairs={{0,12},{4,8},{8,4},{12,0},{16,28},{20,24},{24,20},{28,16},{1,13},{... | collective-permute-start | bytes 294920 | tf_op jit(solution)/shard_map/ppermute | solution.py:273
  26.9 3.9 %collective-permute-done.5.refs_2_ = f32[3,64,128]{2,1,0:T(8,128)S(1)} collective-permute-done((f32[3,64,128]{2,1,0:T(8,128)S(1)}, f32[3,64,128]{2,1,0:T(8,128)S(1)}, u32[]{:S(2)}, u32[]{:S(2)}) %collective-permute-start.5) | collective-permute-done | bytes 98336 | tf_op jit(solution)/shard_map/ppermute | solution.py:273
  30.7 1.0 %collective-permute-done.6.refs_3_ = f32[3,64,128]{2,1,0:T(8,128)S(1)} collective-permute-done((f32[3,64,128]{2,1,0:T(8,128)S(1)}, f32[3,64,128]{2,1,0:T(8,128)S(1)}, u32[]{:S(2)}, u32[]{:S(2)}) %collective-permute-start.6) | collective-permute-done | bytes 98336 | tf_op jit(solution)/shard_map/ppermute | solution.py:273
  31.8 0.7 %gather.1 = f32[1,1,3,128,128]{4,3,2,1,0:T(8,128)} custom-call(f32[3,64,128]{2,1,0:T(8,128)S(1)} %bitcast.11, f32[3,64,128]{2,1,0:T(8,128)S(1)} %collective-permute-done.4.refs_1_, f32[3,64,128]{2,1,0:T(8,128)S(1)} %collective-permute-done.5.refs_2_, f32[3,64,128]{2,1,0:T(8,128)S(1)} %collective-permute-done.6.refs_3_), custom_call_target="tpu_custom_call" | custom-call | tf_op jit(solution)/shard_map/gather/pallas_call | solution.py:289
  (10 shorter events, 0.0 us)
Async XLA Ops:
  0.7 5.9 %copy-start.2 = (s32[1,12]{1,0:T(1,128)S(1)}, s32[1,12]{1,0:T(1,128)}, u32[]{:S(2)}) copy-start(s32[1,12]{1,0:T(1,128)} %cols.1) | copy-start | bytes 148
  0.7 5.9 %copy-start.3 = (s32[1,2]{1,0:T(1,128)S(1)}, s32[1,2]{1,0:T(1,128)}, u32[]{:S(2)}) copy-start(s32[1,2]{1,0:T(1,128)} %border_map.1) | copy-start | bytes 28
  3.4 3.1 %copy-start.4 = (f32[8]{0:T(128)S(1)}, f32[8]{0:T(128)}, u32[]{:S(2)}) copy-start(f32[8]{0:T(128)} %param.21) | copy-start | bytes 100
  3.4 3.0 %copy-start.5 = (f32[8]{0:T(128)S(1)}, f32[8]{0:T(128)}, u32[]{:S(2)}) copy-start(f32[8]{0:T(128)} %param.23) | copy-start | bytes 100
  3.4 3.0 %copy-start.6 = (f32[8]{0:T(128)S(1)}, f32[8]{0:T(128)}, u32[]{:S(2)}) copy-start(f32[8]{0:T(128)} %param.22) | copy-start | bytes 100
  3.4 10.3 %collective-permute-start = (f32[256,256]{1,0:T(8,128)S(1)}, f32[256,256]{1,0:T(8,128)S(1)}, u32[]{:S(2)}, u32[]{:S(2)}) collective-permute-start(f32[256,256]{1,0:T(8,128)S(1)} %get-tuple-element.25), channel_id=1, source_target_pairs={{0,1},{1,2},{2,3},{3,0},{4,5},{5,6},{6,7},{7,4},{8,9},{9,10},{10,1... | collective-permute-start | bytes 786440 | tf_op jit(solution)/shard_map/ppermute | solution.py:233
  6.5 0.7 %copy-start = (s32[1,3,2]{1,2,0:T(2,128)S(1)}, s32[1,3,2]{1,2,0:T(2,128)}, u32[]{:S(2)}) copy-start(s32[1,3,2]{1,2,0:T(2,128)} %param.20) | copy-start | bytes 76
  6.6 0.7 %copy-start.1 = (s32[1,12]{1,0:T(1,128)S(1)}, s32[1,12]{1,0:T(1,128)}, u32[]{:S(2)}) copy-start(s32[1,12]{1,0:T(1,128)} %rows.1) | copy-start | bytes 148
  14.3 9.6 %collective-permute-start.2 = (f32[3,64,128]{2,1,0:T(8,128)S(1)}, f32[3,64,128]{2,1,0:T(8,128)S(1)}, u32[]{:S(2)}, u32[]{:S(2)}) collective-permute-start(f32[3,64,128]{2,1,0:T(8,128)S(1)} %get-tuple-element.31), channel_id=1, source_target_pairs={{0,16},{4,20},{8,24},{12,28},{16,0},{20,4},{24,8},{28,12},{1,17},{... | collective-permute-start | bytes 294920 | tf_op jit(solution)/shard_map/ppermute | solution.py:270
  17.1 7.1 %collective-permute-start.3 = (f32[3,64,128]{2,1,0:T(8,128)S(1)}, f32[3,64,128]{2,1,0:T(8,128)S(1)}, u32[]{:S(2)}, u32[]{:S(2)}) collective-permute-start(f32[3,64,128]{2,1,0:T(8,128)S(1)} %get-tuple-element.32), channel_id=1, source_target_pairs={{0,24},{4,28},{8,16},{12,20},{16,8},{20,12},{24,0},{28,4},{1,25},{... | collective-permute-start | bytes 294920 | tf_op jit(solution)/shard_map/ppermute | solution.py:270
  18.5 6.3 %collective-permute-start.1 = (f32[3,64,128]{2,1,0:T(8,128)S(1)}, f32[3,64,128]{2,1,0:T(8,128)S(1)}, u32[]{:S(2)}, u32[]{:S(2)}) collective-permute-start(f32[3,64,128]{2,1,0:T(8,128)S(1)} %get-tuple-element.32), channel_id=1, source_target_pairs={{0,8},{4,12},{8,0},{12,4},{16,24},{20,28},{24,16},{28,20},{1,9},{5... | collective-permute-start | bytes 294920 | tf_op jit(solution)/shard_map/ppermute | solution.py:270
  24.9 1.9 %collective-permute-start.4 = (f32[3,64,128]{2,1,0:T(8,128)S(1)}, f32[3,64,128]{2,1,0:T(8,128)S(1)}, u32[]{:S(2)}, u32[]{:S(2)}) collective-permute-start(f32[3,64,128]{2,1,0:T(8,128)S(1)} %bitcast.17), channel_id=1, source_target_pairs={{0,4},{4,0},{8,12},{12,8},{16,20},{20,16},{24,28},{28,24},{1,5},{5... | collective-permute-start | bytes 294920 | tf_op jit(solution)/shard_map/ppermute | solution.py:273
  25.0 5.7 %collective-permute-start.5 = (f32[3,64,128]{2,1,0:T(8,128)S(1)}, f32[3,64,128]{2,1,0:T(8,128)S(1)}, u32[]{:S(2)}, u32[]{:S(2)}) collective-permute-start(f32[3,64,128]{2,1,0:T(8,128)S(1)} %bitcast.16), channel_id=1, source_target_pairs={{0,8},{4,12},{8,0},{12,4},{16,24},{20,28},{24,16},{28,20},{1,9},{5... | collective-permute-start | bytes 294920 | tf_op jit(solution)/shard_map/ppermute | solution.py:273
  26.4 5.4 %collective-permute-start.6 = (f32[3,64,128]{2,1,0:T(8,128)S(1)}, f32[3,64,128]{2,1,0:T(8,128)S(1)}, u32[]{:S(2)}, u32[]{:S(2)}) collective-permute-start(f32[3,64,128]{2,1,0:T(8,128)S(1)} %bitcast.15), channel_id=1, source_target_pairs={{0,12},{4,8},{8,4},{12,0},{16,28},{20,24},{24,20},{28,16},{1,13},{... | collective-permute-start | bytes 294920 | tf_op jit(solution)/shard_map/ppermute | solution.py:273
